TPU v7x, 32 devices: a whole 2x2x4 slice. The times are simulated.
32 devices in a mesh: tile: 4 (over y, x), slab: 8 (over z, core).
Axes of the slice: x: 2, y: 2, z: 4, core: 2. Of those that a mesh axis runs over, the one named last changes fastest.
Arguments:
- raw_stack: bfloat16 [32, 120, 2048], P('slab', None, 'tile'), may hold values from -48 to 48
- shear_offsets: int32 [32], P('slab'), may hold values from 0 to 8
- intersection_widths: int32 [3], replicated, may hold values from 32 to 128
Outputs:
- difference: bfloat16 [128, 32, 2048], P('slab', None, 'tile')
- level_one: bfloat16 [64, 16, 1024], P('slab', None, 'tile')
- level_two: bfloat16 [32, 8, 512], P('slab', None, 'tile')
All inputs are finite; a program needn't handle non-finite values.
Results may differ from a plain program's by a relative error of at most 0.003.
Values may be sent and summed in bfloat16 or wider, within the bound.
No kernel may reach another device: no remote copies, remote signals or barrier semaphores. Data moves between devices by JAX's collectives and lax.ppermute only.
A program may use at most 64 MiB of HBM per device.

v0:
```python
import math

import jax
import jax.numpy as jnp
from jax import lax
from jax.sharding import PartitionSpec as P

SLAB_ROWS = 16
STRIP = 6
RADIUS = 4


def padded_2(block, sides, width):
    for axis, dim in sides:
        count = lax.axis_size(axis)
        forward = [(i, i + 1) for i in range(count - 1)]
        backward = [(target, source) for source, target in forward]
        low = lax.ppermute(
            lax.slice_in_dim(block, block.shape[dim] - width, None, axis=dim), axis, forward
        )
        high = lax.ppermute(lax.slice_in_dim(block, 0, width, axis=dim), axis, backward)
        block = jnp.concatenate([low, block, high], axis=dim)
    return block


def shifted(block, axis, distance):
    devices = range(lax.axis_size(axis))
    route = [(i - distance, i) for i in devices if i - distance in devices]
    return lax.ppermute(block, axis, route)


def gauss_taps(sigma_value, reach_cells):
    entries = [
        math.exp(-(offset * offset) / (2.0 * sigma_value * sigma_value))
        for offset in range(-reach_cells, reach_cells + 1)
    ]
    weight_sum = sum(entries)
    return [entry_value / weight_sum for entry_value in entries]


def binomial_taps():
    return [1.0 / 16.0, 4.0 / 16.0, 6.0 / 16.0, 4.0 / 16.0, 1.0 / 16.0]


def smooth(source, weights, direction, begin_at, length_out, stride):
    result = weights[0] * lax.slice_in_dim(
        source, begin_at, begin_at + (length_out - 1) * stride + 1, stride, direction
    )
    for offset in range(1, len(weights)):
        lowest = begin_at + offset
        window = lax.slice_in_dim(
            source, lowest, lowest + (length_out - 1) * stride + 1, stride, direction
        )
        result = result + weights[offset] * window
    return result


def pad_scans(source, width_cells):
    return jnp.pad(source, ((0, 0), (width_cells, width_cells), (0, 0)))


def deskew(planes_block, shifts, shear_top, total_rows, margin):
    padded = jnp.pad(planes_block, ((0, 0), (shear_top + margin, shear_top + margin), (0, 0)))

    def place_plane(plane, shift_value):
        return lax.dynamic_slice_in_dim(plane, shear_top - shift_value, total_rows + 2 * margin, 0)

    return jax.vmap(place_plane, out_axes=1)(padded, shifts)


def band_table(weights, source_pos, target_pos):
    reach_cells = len(weights) // 2
    offsets = source_pos[:, None] - target_pos[None, :] + reach_cells
    table = jnp.zeros(offsets.shape, jnp.float32)
    for index_tap in range(len(weights)):
        table = table + weights[index_tap] * (offsets == index_tap).astype(jnp.float32)
    return table


def along_columns(pieces, tables):
    total = None
    for piece_field, table in zip(pieces, tables):
        term = jnp.einsum("rsc,co->rso", piece_field, table, precision=lax.Precision.HIGHEST)
        total = term if total is None else total + term
    return total


def body(raw_stack, shear_offsets, intersection_widths):
    slab_count = lax.axis_size("slab")
    tile_count = lax.axis_size("tile")
    tile_index = lax.axis_index("tile")
    planes, camera, columns = raw_stack.shape
    total_rows = SLAB_ROWS * slab_count
    shear_top = total_rows - camera
    row_depth = RADIUS
    deskewed = deskew(raw_stack, shear_offsets, shear_top, total_rows, 0)
    outgoing = deskewed.reshape(slab_count, SLAB_ROWS, planes, columns)
    volume = lax.all_to_all(outgoing, "slab", split_axis=0, concat_axis=2, tiled=True)[0]
    volume = padded_2(volume, (("slab", 0),), row_depth)
    right_width = intersection_widths[jnp.minimum(tile_index, tile_count - 2)]
    left_width = intersection_widths[jnp.maximum(tile_index - 1, 0)]
    toward_right = lax.dynamic_slice_in_dim(volume, columns - right_width - STRIP, STRIP, 2)
    toward_left = lax.dynamic_slice_in_dim(volume, left_width, STRIP, 2)
    from_left = shifted(toward_right, "tile", 1)
    from_right = shifted(toward_left, "tile", -1)
    pieces = (
        volume.astype(jnp.float32),
        from_left.astype(jnp.float32),
        from_right.astype(jnp.float32),
    )
    own_pos = jnp.arange(columns, dtype=jnp.int32)
    left_pos = jnp.arange(STRIP, dtype=jnp.int32) - STRIP
    right_pos = jnp.arange(STRIP, dtype=jnp.int32) + columns
    sources = (own_pos, left_pos, right_pos)
    scan_count = volume.shape[1]

    def gaussian(sigma_value):
        weights = gauss_taps(sigma_value, RADIUS)
        colled = along_columns(pieces, [band_table(weights, place, own_pos) for place in sources])
        along_rows = smooth(colled, weights, 0, row_depth - RADIUS, SLAB_ROWS, 1)
        return smooth(pad_scans(along_rows, RADIUS), weights, 1, 0, scan_count, 1)

    difference = (gaussian(1.0) - gaussian(1.6)).astype(jnp.bfloat16)
    binomial = binomial_taps()
    main_pos = 2 * jnp.arange(columns // 2, dtype=jnp.int32)
    edge_pos = jnp.array([-4, -2, columns, columns + 2], dtype=jnp.int32)
    target_pos = jnp.concatenate([main_pos, edge_pos])
    colled = along_columns(pieces, [band_table(binomial, place, target_pos) for place in sources])
    row_keep = jnp.ones((SLAB_ROWS // 2,), dtype=bool)
    coarse_count = SLAB_ROWS // 2
    rows_blur = smooth(colled, binomial, 0, row_depth - 2, coarse_count, 2)
    scans_blur = smooth(pad_scans(rows_blur, 2), binomial, 1, 0, scan_count // 2, 2)
    edge_keep = ((edge_pos >= 0) | (tile_index > 0)) & (
        (edge_pos < columns) | (tile_index < tile_count - 1)
    )
    main_ext = jnp.where(row_keep[:, None, None], scans_blur[:, :, 0 : columns // 2], 0.0).astype(
        jnp.bfloat16
    )
    edge_mask = row_keep[:, None, None] & edge_keep[None, None, :]
    edge_ext = jnp.where(edge_mask, scans_blur[:, :, columns // 2 :], 0.0).astype(jnp.bfloat16)
    main_index = jnp.arange(columns // 2, dtype=jnp.int32) + 2
    edge_index = jnp.array([0, 1, columns // 2 + 2, columns // 2 + 3], dtype=jnp.int32)
    coarse_target = 2 * jnp.arange(columns // 4, dtype=jnp.int32) + 2
    coarse_cols = along_columns(
        (main_ext.astype(jnp.float32), edge_ext.astype(jnp.float32)),
        [
            band_table(binomial, main_index, coarse_target),
            band_table(binomial, edge_index, coarse_target),
        ],
    )
    coarse_cols = padded_2(coarse_cols, (("slab", 0),), 2)
    rows_two = smooth(coarse_cols, binomial, 0, 0, SLAB_ROWS // 4, 2)
    level_two = smooth(pad_scans(rows_two, 2), binomial, 1, 0, scan_count // 4, 2).astype(
        jnp.bfloat16
    )
    return (difference, main_ext, level_two)


def solution(mesh):
    placed = (P("slab", None, "tile"), P("slab"), P())
    return jax.shard_map(
        body,
        mesh=mesh,
        in_specs=placed,
        out_specs=(P("slab", None, "tile"), P("slab", None, "tile"), P("slab", None, "tile")),
        check_vma=False,
    )
```

profile of v0, /device:TPU:1, one launch (start us, length us, event | category | flops | bytes accessed | tf_op | source)
XLA Modules:
  0.0 147.0 jit_solution(10012603302796135666)
XLA Ops:
  2.8 3.7 %gather_fusion = bf16[4,128,512]{2,0,1:T(4,128)(2,1)} fusion(bf16[4,136,512]{2,0,1:T(4,128)(2,1)S(1)} %pad.20, s32[4]{0:T(128)S(1)} %fusion.504), kind=kCustom, calls=%fused_computation | custom fusion | bytes 1048624 | tf_op jit(solution)/shard_map/vmap()/gather | solution.py:66
  6.5 6.5 %all-to-all-start = ((bf16[8,16,4,512]{3,2,1,0:T(4,128)(2,1)}), bf16[8,16,4,512]{3,2,1,0:T(4,128)(2,1)S(1)}, u32[]{:S(2)}, u32[]{:S(2)}) async-start(bf16[8,16,4,512]{3,2,1,0:T(4,128)(2,1)} %bitcast.3), calls=%async_computation | async-start | bytes 1048576 | tf_op jit(solution)/shard_map/all_to_all | solution.py:98
  13.1 14.4 %all-to-all-done = bf16[8,16,4,512]{3,2,1,0:T(4,128)(2,1)S(1)} async-done(((bf16[8,16,4,512]{3,2,1,0:T(4,128)(2,1)}), bf16[8,16,4,512]{3,2,1,0:T(4,128)(2,1)S(1)}, u32[]{:S(2)}, u32[]{:S(2)}) %all-to-all-start) | async-done | bytes 524320 | tf_op jit(solution)/shard_map/all_to_all | solution.py:98
  36.5 3.8 %collective-permute-done.1 = bf16[4,32,512]{2,1,0:T(8,128)(2,1)S(1)} collective-permute-done((bf16[4,32,512]{2,1,0:T(8,128)(2,1)S(1)}, bf16[4,32,512]{2,1,0:T(8,128)(2,1)S(1)}, u32[]{:S(2)}, u32[]{:S(2)}) %collective-permute-start.1) | collective-permute-done | bytes 131104 | tf_op jit(solution)/shard_map/ppermute | solution.py:21
  40.3 2.7 %fusion.50 = f32[24,32,512]{2,1,0:T(8,128)} fusion(bf16[24,32,512]{2,1,0:T(8,128)(2,1)S(1)} %constant_dynamic-update-slice_fusion), kind=kOutput, calls=%fused_computation.92 | convolution fusion | flops 2423259136 | bytes 2359296 | tf_op jit(solution)/shard_map/rsc,co->rso/dot_general | solution.py:83
  43.0 2.7 %fusion.52 = f32[24,32,512]{2,1,0:T(8,128)} fusion(bf16[24,32,512]{2,1,0:T(8,128)(2,1)S(1)} %constant_dynamic-update-slice_fusion), kind=kOutput, calls=%fused_computation.94 | convolution fusion | flops 2423259136 | bytes 2359296 | tf_op jit(solution)/shard_map/rsc,co->rso/dot_general | solution.py:83
  45.9 3.1 %collective-permute-start.2 = (bf16[24,32,6]{2,1,0:T(8,128)(2,1)S(1)}, bf16[24,32,6]{2,1,0:T(8,128)(2,1)S(1)}, u32[]{:S(2)}, u32[]{:S(2)}) collective-permute-start(bf16[24,32,6]{2,1,0:T(8,128)(2,1)S(1)} %get-tuple-element.7), channel_id=1, source_target_pairs={{0,8},{8,16},{16,24},{1,9},{9,17},{17,25},{2,10},{10,18},{18,26},{... | collective-permute-start | bytes 27656 | tf_op jit(solution)/shard_map/ppermute | solution.py:29
  52.3 3.8 %copy.37 = f32[24,32,260]{1,0,2:T(8,128)} copy(f32[24,32,260]{2,1,0:T(8,128)S(1)} %fusion.115) | data formatting | bytes 1597440 | tf_op jit(solution)/shard_map/rsc,co->rso/dot_general | solution.py:83
  58.2 3.7 %copy.40 = f32[24,32,260]{1,0,2:T(8,128)} copy(f32[24,32,260]{2,1,0:T(8,128)S(1)} %fusion.343) | data formatting | bytes 1597440 | tf_op jit(solution)/shard_map/rsc,co->rso/dot_general | solution.py:83
  62.6 3.8 %copy.38 = f32[24,32,260]{1,0,2:T(8,128)} copy(f32[24,32,260]{2,1,0:T(8,128)S(1)} %fusion.345) | data formatting | bytes 1597440 | tf_op jit(solution)/shard_map/rsc,co->rso/dot_general | solution.py:83
  66.4 4.2 %add_add_fusion = f32[24,32,260]{1,0,2:T(8,128)S(1)} fusion(f32[24,32,260]{1,0,2:T(8,128)} %copy.40, f32[24,32,260]{1,0,2:T(8,128)} %copy.37, f32[24,32,260]{1,0,2:T(8,128)} %copy.38), kind=kLoop, calls=%fused_computation.1 | loop fusion | flops 399360 | bytes 3194880 | tf_op jit(solution)/shard_map/add | solution.py:84
  70.6 4.1 %slice.231 = f32[8,32,260]{1,0,2:T(8,128)} slice(f32[24,32,260]{1,0,2:T(8,128)S(1)} %add_add_fusion), slice={[6:21:2], [0:32:1], [0:260:1]} | slice | bytes 532480 | tf_op jit(solution)/shard_map/slice | solution.py:51
  74.7 4.1 %slice.230 = f32[8,32,260]{1,0,2:T(8,128)} slice(f32[24,32,260]{1,0,2:T(8,128)S(1)} %add_add_fusion), slice={[5:20:2], [0:32:1], [0:260:1]} | slice | bytes 532480 | tf_op jit(solution)/shard_map/slice | solution.py:51
  78.7 4.0 %slice.229 = f32[8,32,260]{1,0,2:T(8,128)} slice(f32[24,32,260]{1,0,2:T(8,128)S(1)} %add_add_fusion), slice={[4:19:2], [0:32:1], [0:260:1]} | slice | bytes 532480 | tf_op jit(solution)/shard_map/slice | solution.py:51
  82.8 4.0 %slice.228 = f32[8,32,260]{1,0,2:T(8,128)} slice(f32[24,32,260]{1,0,2:T(8,128)S(1)} %add_add_fusion), slice={[3:18:2], [0:32:1], [0:260:1]} | slice | bytes 532480 | tf_op jit(solution)/shard_map/slice | solution.py:51
  86.8 4.1 %slice.227 = f32[8,32,260]{1,0,2:T(8,128)} slice(f32[24,32,260]{1,0,2:T(8,128)S(1)} %add_add_fusion), slice={[2:17:2], [0:32:1], [0:260:1]} | slice | bytes 532480 | tf_op jit(solution)/shard_map/slice | solution.py:46
  90.9 2.8 %multiply_add_fusion.1 = f32[8,32,260]{1,0,2:T(8,128)S(1)} fusion(f32[8,32,260]{1,0,2:T(8,128)} %slice.231, f32[8,32,260]{1,0,2:T(8,128)} %slice.230, f32[8,32,260]{1,0,2:T(8,128)} %slice.229, f32[8,32,260]{1,0,2:T(8,128)} %slice.228, f32[8,32,260]{1,0,2:T(8,128)} %slice.227), kind=kLoop, calls=%fused_computation.22 | loop fusion | flops 599040 | bytes 1597440 | tf_op jit(solution)/shard_map/add | solution.py:54
  94.0 6.1 %slice.236 = f32[8,16,260]{1,0,2:T(8,128)S(1)} slice(f32[8,36,260]{1,0,2:T(8,128)S(1)} %pad.23), slice={[0:8:1], [4:35:2], [0:260:1]} | slice | bytes 266240 | tf_op jit(solution)/shard_map/slice | solution.py:51
  100.1 6.1 %slice.235 = f32[8,16,260]{1,0,2:T(8,128)S(1)} slice(f32[8,36,260]{1,0,2:T(8,128)S(1)} %pad.23), slice={[0:8:1], [3:34:2], [0:260:1]} | slice | bytes 266240 | tf_op jit(solution)/shard_map/slice | solution.py:51
  106.2 6.6 %slice.234 = f32[8,16,260]{1,0,2:T(8,128)} slice(f32[8,36,260]{1,0,2:T(8,128)S(1)} %pad.23), slice={[0:8:1], [2:33:2], [0:260:1]} | slice | bytes 266240 | tf_op jit(solution)/shard_map/slice | solution.py:51
  112.7 6.6 %slice.233 = f32[8,16,260]{1,0,2:T(8,128)} slice(f32[8,36,260]{1,0,2:T(8,128)S(1)} %pad.23), slice={[0:8:1], [1:32:2], [0:260:1]} | slice | bytes 266240 | tf_op jit(solution)/shard_map/slice | solution.py:51
  119.3 6.4 %slice.232 = f32[8,16,260]{1,0,2:T(8,128)} slice(f32[8,36,260]{1,0,2:T(8,128)S(1)} %pad.23), slice={[0:8:1], [0:31:2], [0:260:1]} | slice | bytes 266240 | tf_op jit(solution)/shard_map/slice | solution.py:46
  130.9 5.2 %collective-permute-start.4 = (f32[2,16,128]{2,1,0:T(8,128)S(1)}, f32[2,16,128]{2,1,0:T(8,128)S(1)}, u32[]{:S(2)}, u32[]{:S(2)}) collective-permute-start(f32[2,16,128]{2,1,0:T(8,128)S(1)} %get-tuple-element.10), channel_id=1, source_target_pairs={{0,1},{1,2},{2,3},{3,4},{4,5},{5,6},{6,7},{8,9},{9,10},{10,11},{11... | collective-permute-start | bytes 49160 | tf_op jit(solution)/shard_map/ppermute | solution.py:18
  143.3 3.0 %fusion.10 = bf16[16,32,512]{2,1,0:T(8,128)(2,1)} fusion(f32[16,32,512]{2,1,0:T(8,128)S(1)} %get-tuple-element.15, f32[16,32,512]{2,1,0:T(8,128)S(1)} %get-tuple-element.14), kind=kLoop, calls=%fused_computation.33 | loop fusion | flops 9437184 | bytes 2621440 | tf_op jit(solution)/shard_map/convert_element_type | solution.py:123
  (76 shorter events, 27.4 us)
Async XLA Ops:
  6.5 6.6 %copy-start.8 = (pred[4]{0:T(512)(128)(4,1)S(1)}, pred[4]{0:T(512)(128)(4,1)}, u32[]{:S(2)}) copy-start(pred[4]{0:T(512)(128)(4,1)} %constant.255) | copy-start | bytes 16
  6.5 6.6 %copy-start.9 = (pred[4]{0:T(512)(128)(4,1)S(1)}, pred[4]{0:T(512)(128)(4,1)}, u32[]{:S(2)}) copy-start(pred[4]{0:T(512)(128)(4,1)} %constant.254) | copy-start | bytes 16
  6.5 23.2 %copy-start.5 = (s32[3]{0:T(128)S(1)}, s32[3]{0:T(128)}, u32[]{:S(2)}) copy-start(s32[3]{0:T(128)} %param.7) | copy-start | bytes 40
  6.5 27.0 %copy-start.7 = (s32[4]{0:T(128)S(1)}, s32[4]{0:T(128)}, u32[]{:S(2)}) copy-start(s32[4]{0:T(128)} %constant.238.clone) | copy-start | bytes 52
  6.5 21.0 %all-to-all-start = ((bf16[8,16,4,512]{3,2,1,0:T(4,128)(2,1)}), bf16[8,16,4,512]{3,2,1,0:T(4,128)(2,1)S(1)}, u32[]{:S(2)}, u32[]{:S(2)}) async-start(bf16[8,16,4,512]{3,2,1,0:T(4,128)(2,1)} %bitcast.3), calls=%async_computation | async-start | bytes 1048576 | tf_op jit(solution)/shard_map/all_to_all | solution.py:98
  27.7 8.7 %collective-permute-start = (bf16[4,32,512]{2,1,0:T(8,128)(2,1)S(1)}, bf16[4,32,512]{2,1,0:T(8,128)(2,1)S(1)}, u32[]{:S(2)}, u32[]{:S(2)}) collective-permute-start(bf16[4,32,512]{2,1,0:T(8,128)(2,1)S(1)} %slice.190), channel_id=1, source_target_pairs={{0,1},{1,2},{2,3},{3,4},{4,5},{5,6},{6,7},{8,9},{9,10},{10,11},{11... | collective-permute-start | bytes 393224 | tf_op jit(solution)/shard_map/ppermute | solution.py:18
  34.0 6.3 %collective-permute-start.1 = (bf16[4,32,512]{2,1,0:T(8,128)(2,1)S(1)}, bf16[4,32,512]{2,1,0:T(8,128)(2,1)S(1)}, u32[]{:S(2)}, u32[]{:S(2)}) collective-permute-start(bf16[4,32,512]{2,1,0:T(8,128)(2,1)S(1)} %slice.192), channel_id=1, source_target_pairs={{1,0},{2,1},{3,2},{4,3},{5,4},{6,5},{7,6},{9,8},{10,9},{11,10},{12... | collective-permute-start | bytes 393224 | tf_op jit(solution)/shard_map/ppermute | solution.py:21
  45.9 16.0 %collective-permute-start.2 = (bf16[24,32,6]{2,1,0:T(8,128)(2,1)S(1)}, bf16[24,32,6]{2,1,0:T(8,128)(2,1)S(1)}, u32[]{:S(2)}, u32[]{:S(2)}) collective-permute-start(bf16[24,32,6]{2,1,0:T(8,128)(2,1)S(1)} %get-tuple-element.7), channel_id=1, source_target_pairs={{0,8},{8,16},{16,24},{1,9},{9,17},{17,25},{2,10},{10,18},{18,26},{... | collective-permute-start | bytes 27656 | tf_op jit(solution)/shard_map/ppermute | solution.py:29
  49.0 8.5 %collective-permute-start.3 = (bf16[24,32,6]{2,1,0:T(8,128)(2,1)S(1)}, bf16[24,32,6]{2,1,0:T(8,128)(2,1)S(1)}, u32[]{:S(2)}, u32[]{:S(2)}) collective-permute-start(bf16[24,32,6]{2,1,0:T(8,128)(2,1)S(1)} %get-tuple-element.6), channel_id=1, source_target_pairs={{8,0},{16,8},{24,16},{9,1},{17,9},{25,17},{10,2},{18,10},{26,18},{... | collective-permute-start | bytes 27656 | tf_op jit(solution)/shard_map/ppermute | solution.py:29
  61.9 0.7 copy-start
  127.9 0.8 copy-start.6
  127.9 8.2 %copy-start.1 = (bf16[24,32,6]{2,1,0:T(8,128)(2,1)S(1)}, bf16[24,32,6]{2,1,0:T(8,128)(2,1)}, u32[]{:S(2)}) copy-start(bf16[24,32,6]{2,1,0:T(8,128)(2,1)} %copy-done) | copy-start | bytes 27652
  128.3 8.7 %copy-start.4 = (bf16[8,16,256]{2,1,0:T(8,128)(2,1)}, bf16[8,16,256]{2,1,0:T(8,128)(2,1)S(1)}, u32[]{:S(2)}) copy-start(bf16[8,16,256]{2,1,0:T(8,128)(2,1)S(1)} %copy.43) | copy-start | bytes 196612
  129.0 17.3 %collective-permute-start.5 = (f32[2,16,128]{2,1,0:T(8,128)S(1)}, f32[2,16,128]{2,1,0:T(8,128)S(1)}, u32[]{:S(2)}, u32[]{:S(2)}) collective-permute-start(f32[2,16,128]{2,1,0:T(8,128)S(1)} %get-tuple-element.11), channel_id=1, source_target_pairs={{1,0},{2,1},{3,2},{4,3},{5,4},{6,5},{7,6},{9,8},{10,9},{11,10},{12... | collective-permute-start | bytes 49160 | tf_op jit(solution)/shard_map/ppermute | solution.py:21
  130.9 15.4 %collective-permute-start.4 = (f32[2,16,128]{2,1,0:T(8,128)S(1)}, f32[2,16,128]{2,1,0:T(8,128)S(1)}, u32[]{:S(2)}, u32[]{:S(2)}) collective-permute-start(f32[2,16,128]{2,1,0:T(8,128)S(1)} %get-tuple-element.10), channel_id=1, source_target_pairs={{0,1},{1,2},{2,3},{3,4},{4,5},{5,6},{6,7},{8,9},{9,10},{10,11},{11... | collective-permute-start | bytes 49160 | tf_op jit(solution)/shard_map/ppermute | solution.py:18
  137.0 1.4 copy-start.3
  138.4 1.4 copy-start.2
where the time goes:
time: 148 us; the launch traced here: 147 us
  local copies, waits for them, and re-layouts  71.6 us (48%)
  starting transfers between devices  22.6 us (15%)
  waiting for transfers between devices  19.7 us (13%)
  other arithmetic  16.2 us (11%)
  matrix products  12.6 us (9%)
  between operations  4.31 us (3%)
    slice x12, local copies, waits for them, and re-layouts, smooth(): lax.slice_in_dim(source, lowest, lowest + (length_out - 1) * stride + 1,...  41.5 us
    all_to_all x1, waiting for transfers between devices, body(): lax.all_to_all(outgoing, 'slab', split_axis=0, concat_axis=2, tiled=True)[0]  14.4 us
    dot_general x11, matrix products, along_columns(): jnp.einsum('rsc,co->rso', piece_field, table, precision=lax.Precision.HIG...  12.6 us
    dot_general x3, local copies, waits for them, and re-layouts, along_columns(): jnp.einsum('rsc,co->rso', piece_field, table, precision=lax.Precision.HIG...  11.3 us
    slice x3, local copies, waits for them, and re-layouts, smooth(): lax.slice_in_dim(source, begin_at, begin_at + (length_out - 1) * stride +...  10.4 us
    add x4, other arithmetic, smooth(): result = result + weights[offset] * window  7.57 us
    ppermute x2, starting transfers between devices, padded_2(): lax.ppermute(lax.slice_in_dim(block, block.shape[dim] - width, None, axis...  7.1 us
    all_to_all x1, starting transfers between devices, body(): lax.all_to_all(outgoing, 'slab', split_axis=0, concat_axis=2, tiled=True)[0]  6.52 us
  transfers between devices with their start and end apart: 7, of which 3 were waited for; matrix products, arithmetic and copies ran while one was open for 14% of the time, Pallas kernels for 0%

commit v1 on v0

v1 whole, which is shorter than its diff:
```python
import functools
import math

import jax
import jax.numpy as jnp
import ml_dtypes
import numpy as np
from jax import lax
from jax.experimental import pallas as pl
from jax.experimental.pallas import tpu as pltpu
from jax.sharding import PartitionSpec as P

SLAB_ROWS = 16
STRIP = 6
RADIUS = 4
LOW = 6
HIGH = 4
PAIR = 2 * SLAB_ROWS + LOW + HIGH
NEED = SLAB_ROWS + LOW + HIGH
LEVEL = 11
LANE = 128
F32 = jnp.float32
BF16 = jnp.bfloat16


def gauss_taps(sigma_value):
    entries = [math.exp(-(j * j) / (2.0 * sigma_value * sigma_value)) for j in range(-RADIUS, RADIUS + 1)]
    weight_sum = sum(entries)
    return np.array([entry / weight_sum for entry in entries], np.float64)


BINOMIAL = np.array([1.0, 4.0, 6.0, 4.0, 1.0], np.float64) / 16.0


def band(weights, source, target):
    reach = len(weights) // 2
    offset = source[None, :] - target[:, None] + reach
    inside = (offset >= 0) & (offset < len(weights))
    return np.where(inside, weights[np.clip(offset, 0, len(weights) - 1)], 0.0)


def two_parts(table):
    high = table.astype(ml_dtypes.bfloat16)
    return high, (table - high.astype(np.float64)).astype(ml_dtypes.bfloat16)


def row_scan_table(row_band, scan_band, groups):
    rows_out, rows_in = row_band.shape
    scans_out = scan_band.shape[0]
    scans = scan_band.reshape(scans_out, groups, 4)
    table = np.einsum("yr,sgp->ysgrp", row_band, scans)
    table = table.reshape(rows_out * scans_out, groups, rows_in * 4)
    table = np.pad(table, ((0, 0), (0, 0), (0, LANE - rows_in * 4)))
    return table.reshape(rows_out * scans_out, groups * LANE)


def tables(scans, columns):
    row_in = np.arange(NEED) - LOW
    own = np.arange(SLAB_ROWS)
    near = np.arange(16) - 4
    block = np.arange(8)
    rowscan, column = [], []
    half = columns // 2
    window = np.arange(half + 2 * LANE) - LANE
    for sigma in (1.0, 1.6):
        taps = gauss_taps(sigma)
        rowscan += list(two_parts(row_scan_table(band(taps, row_in, own), band(taps, near, block), 4)))
        column += list(two_parts(band(taps, window, np.arange(half)).T))
    level_rows = 2 * np.arange(LEVEL) - 4
    level_scans = 2 * np.arange(scans // 2)
    level = row_scan_table(
        band(BINOMIAL, row_in, level_rows), band(BINOMIAL, np.arange(scans), level_scans), scans // 4
    )
    edge_tile = np.where(np.arange(LANE) < LANE // 2, columns, -LANE) + np.arange(LANE)
    places = np.concatenate([edge_tile, np.arange(columns)])
    edges = np.array([-4, -2, columns, columns + 2])
    targets = np.concatenate([2 * np.arange(columns // 2), edges])
    level_column = np.pad(band(BINOMIAL, places, targets).T, ((0, 0), (0, LANE - 4)))
    two = np.einsum(
        "yr,sp->ysrp",
        band(BINOMIAL, np.arange(LEVEL) - 2, 2 * np.arange(4)),
        band(BINOMIAL, np.arange(scans // 2), 2 * np.arange(scans // 4)),
    ).reshape(scans, LEVEL * scans // 2)
    two_column = np.pad(
        band(BINOMIAL, np.floor_divide(targets, 2), 2 * np.arange(columns // 4)).T, ((0, LANE - 4), (0, 0))
    )
    small = ml_dtypes.bfloat16
    return dict(
        rowscan=np.concatenate(rowscan, 0),
        level=level.astype(small),
        column=np.stack(column),
        level_column=level_column.astype(small),
        two=two.astype(small),
        two_column=two_column.astype(small),
    )


def dot(left, right):
    return jnp.dot(left, right, preferred_element_type=F32)


def dot_rows(left, right):
    return lax.dot_general(left, right, (((1,), (1,)), ((), ())), preferred_element_type=F32)


def place_table(shear_ref, group, slots, camera):
    slot = lax.broadcasted_iota(jnp.int32, (slots, 1), 0)
    plane, row = slot & 3, slot >> 2
    shift = jnp.where(plane == 0, shear_ref[0], jnp.where(plane == 1, shear_ref[1], jnp.where(plane == 2, shear_ref[2], shear_ref[3])))
    source = group * (2 * SLAB_ROWS) - LOW + row - shift
    inside = (source >= 0) & (source < camera) & (row < PAIR)
    wanted = jnp.where(inside, plane * camera + source, -1)
    lane = lax.broadcasted_iota(jnp.int32, (slots, 4 * camera), 1)
    return jnp.where(lane == wanted, 1.0, 0.0).astype(BF16)


def pack_first(raw_ref, shear_ref, width_ref, right_ref, left_ref, *out_refs):
    camera = raw_ref.shape[0] // 4
    columns = raw_ref.shape[1]
    tile = lax.axis_index("tile")
    tiles = lax.axis_size("tile")
    mine = lax.axis_index("slab") >> 1
    lane = lax.broadcasted_iota(jnp.int32, (8, columns), 1)
    line = lax.broadcasted_iota(jnp.int32, (8, columns), 0)
    right_width = width_ref[jnp.minimum(tile, tiles - 2)]
    left_width = width_ref[jnp.maximum(tile - 1, 0)]
    toward_right = jnp.where((lane == columns - right_width - 8 + line) & (line >= 2), 1.0, 0.0).astype(BF16)
    toward_left = jnp.where((lane == left_width + line) & (line < 6), 1.0, 0.0).astype(BF16)
    right_ref[...] = dot_rows(toward_right, raw_ref[...]).astype(BF16)
    left_ref[...] = dot_rows(toward_left, raw_ref[...]).astype(BF16)
    for step, out_ref in enumerate(out_refs):
        table = place_table(shear_ref, mine ^ step, PAIR * 4, camera)
        out_ref[...] = dot(table, raw_ref[:, : columns // 2]).astype(BF16)


def pack_second(raw_ref, shear_ref, from_left_ref, from_right_ref, *out_refs):
    camera = raw_ref.shape[0] // 4
    columns = raw_ref.shape[1]
    mine = lax.axis_index("slab") >> 1
    for step, out_ref in enumerate(out_refs):
        table = place_table(shear_ref, mine ^ step, columns // 2, camera)
        out_ref[: PAIR * 4, :] = dot(table[: PAIR * 4], raw_ref[:, columns // 2 :]).astype(BF16)
        strips = jnp.concatenate([from_right_ref[...].astype(F32), from_left_ref[...].astype(F32)], 0)
        out_ref[PAIR * 4 :, :] = dot_rows(strips.astype(BF16), table).astype(BF16)


def collect(in_refs, volume, scans):
    slab = lax.axis_index("slab")
    core = slab & 1
    lanes = volume.shape[-1]
    groups = scans // 4
    volume[0] = jnp.zeros((LANE, lanes), BF16)
    volume[groups + 1] = jnp.zeros((LANE, lanes), BF16)
    for index, in_ref in enumerate(in_refs):
        group = (slab ^ index) + 1
        start = pl.multiple_of(core * (SLAB_ROWS * 4), SLAB_ROWS * 4)
        volume[group, : NEED * 4, :] = in_ref[pl.ds(start, NEED * 4), :]
        volume[group, NEED * 4 :, :] = jnp.zeros((LANE - NEED * 4, lanes), BF16)


def split(value):
    high = value.astype(BF16)
    return high, (value - high.astype(F32)).astype(BF16)


def row_scan(rowscan_ref, operand, product, scans, store):
    rows = 8 * SLAB_ROWS
    for block in range(scans // 8):
        both = product(rowscan_ref[...], operand(block))
        for sigma in range(2):
            total = both[2 * sigma * rows : (2 * sigma + 1) * rows] + both[(2 * sigma + 1) * rows : (2 * sigma + 2) * rows]
            high, low = split(total)
            store(2 * sigma, block * rows, high)
            store(2 * sigma + 1, block * rows, low)


def first_half(count, scans, rowscan_ref, level_ref, *refs):
    in_refs, (wide_ref, coarse_ref), volume = refs[:count], refs[count : count + 2], refs[count + 2]
    collect(in_refs, volume, scans)
    lanes = volume.shape[-1]

    def store(part, start, value):
        wide_ref[part, start : start + value.shape[0], :] = value

    row_scan(rowscan_ref, lambda block: volume[2 * block : 2 * block + 4].reshape(4 * LANE, lanes), dot, scans, store)
    groups = scans // 4
    coarse_ref[...] = dot(level_ref[...], volume[1 : groups + 1].reshape(groups * LANE, lanes))


def second_half(count, scans, *refs):
    rowscan_ref, level_ref, column_ref, level_column_ref, two_ref, two_column_ref, wide_ref, coarse_ref = refs[:8]
    in_refs = refs[8 : 8 + count]
    difference_ref, one_ref, second_ref, volume, edge, wide, rim = refs[8 + count :]
    slab = lax.axis_index("slab")
    slabs = lax.axis_size("slab")
    tile = lax.axis_index("tile")
    tiles = lax.axis_size("tile")
    core = slab & 1
    groups = scans // 4
    lanes = volume.shape[-1]
    collect(in_refs, volume, scans)
    edge[...] = jnp.zeros(edge.shape, BF16)
    for index, in_ref in enumerate(in_refs):
        place = pl.multiple_of(((slab ^ index) + 1) * LANE, LANE)
        strips = in_ref[PAIR * 4 :, :].astype(F32)
        strips = jnp.where(core == 0, strips[:, :LANE], strips[:, SLAB_ROWS * 4 : SLAB_ROWS * 4 + LANE]).astype(BF16)
        edge[0:8, pl.ds(place, LANE)] = strips[:8]
        edge[LANE - 8 :, pl.ds(place, LANE)] = strips[8:]

    def store(part, start, value):
        wide[part, start : start + value.shape[0], :] = value

    def store_rim(part, start, value):
        rim[part, start : start + value.shape[0], :] = value

    row_scan(rowscan_ref, lambda block: volume[2 * block : 2 * block + 4].reshape(4 * LANE, lanes), dot, scans, store)
    row_scan(rowscan_ref, lambda block: edge[:, 2 * block * LANE : (2 * block + 4) * LANE], dot_rows, scans, store_rim)

    for half in range(2):
        total = None
        for sigma in range(2):
            parts = []
            for part in (2 * sigma, 2 * sigma + 1):
                if half == 0:
                    parts.append(jnp.concatenate([rim[part], wide_ref[part], wide[part][:, :LANE]], 1))
                else:
                    parts.append(jnp.concatenate([wide_ref[part][:, lanes - LANE :], wide[part], rim[part]], 1))
            smooth = dot(parts[0], column_ref[2 * sigma]) + dot(parts[1], column_ref[2 * sigma]) + dot(parts[0], column_ref[2 * sigma + 1])
            total = smooth if total is None else total - smooth
        total = total.reshape(scans // 8, SLAB_ROWS, 8, lanes)
        for pair in range(scans // 16):
            joined = jnp.concatenate([total[2 * pair], total[2 * pair + 1]], 1)
            difference_ref[:, 16 * pair : 16 * pair + 16, half * lanes : (half + 1) * lanes] = joined.astype(BF16)

    coarse = jnp.concatenate(
        [
            dot_rows(level_ref[...], edge[:, LANE : (groups + 1) * LANE]),
            coarse_ref[...],
            dot(level_ref[...], volume[1 : groups + 1].reshape(groups * LANE, lanes)),
        ],
        1,
    )
    high, low = split(coarse)
    level = dot(high, level_column_ref[...]) + dot(low, level_column_ref[...])
    shape = (LEVEL, scans // 2, level.shape[-1])
    level = level.reshape(shape)
    row = slab * (SLAB_ROWS // 2) - 2 + lax.broadcasted_iota(jnp.int32, shape, 0)
    lane = lax.broadcasted_iota(jnp.int32, shape, 2) - lanes
    keep = (row >= 0) & (row < slabs * (SLAB_ROWS // 2))
    keep = keep & ((lane < 0) | (lane >= 2) | (tile > 0)) & ((lane < 2) | (tile < tiles - 1))
    level = jnp.where(keep, level, 0.0)
    ready = level.astype(BF16)
    one_ref[...] = ready[2:10, :, :lanes]
    blurred = dot(two_ref[...], ready.reshape(LEVEL * scans // 2, level.shape[-1]))
    high, low = split(blurred)
    second = dot(high, two_column_ref[...]) + dot(low, two_column_ref[...])
    second_ref[...] = second.reshape(second_ref.shape).astype(BF16)


VECTOR = pl.BlockSpec(memory_space=pltpu.VMEM)
SCALAR = pl.BlockSpec(memory_space=pltpu.SMEM)
PARAMS = pltpu.CompilerParams(vmem_limit_bytes=48 * 1024 * 1024)


def exchange(chunks, slabs):
    order = sorted(range(1, len(chunks)), key=lambda step: (-(step & -step), step))
    held = {0: chunks[0]}
    for step in order:
        held[step] = lax.ppermute(chunks[step], "slab", [(i, i ^ (2 * step)) for i in range(slabs)])
    swap = [(i, i ^ 1) for i in range(slabs)]
    result = []
    for step in range(len(chunks)):
        result += [held[step], lax.ppermute(held[step], "slab", swap)]
    return result


def shifted(block, distance):
    devices = range(lax.axis_size("tile"))
    route = [(i - distance, i) for i in devices if i - distance in devices]
    return lax.ppermute(block, "tile", route)


def body(raw_stack, shear_offsets, intersection_widths):
    slabs = lax.axis_size("slab")
    planes, camera, columns = raw_stack.shape
    scans = planes * slabs
    half = columns // 2
    pairs = slabs // 2
    raw = raw_stack.reshape(planes * camera, columns)
    table = {name: jnp.asarray(value) for name, value in tables(scans, columns).items()}
    strip = jax.ShapeDtypeStruct((8, planes * camera), BF16)
    first = jax.ShapeDtypeStruct((PAIR * planes, half), BF16)
    toward_right, toward_left, *chunks = pl.pallas_call(
        pack_first,
        out_shape=[strip, strip] + [first] * pairs,
        in_specs=[VECTOR, SCALAR, SCALAR],
        out_specs=[VECTOR] * (2 + pairs),
        compiler_params=PARAMS,
        name="pack_first",
    )(raw, shear_offsets, intersection_widths)
    from_left = shifted(toward_right, 1)
    from_right = shifted(toward_left, -1)
    got_first = exchange(chunks, slabs)
    second = jax.ShapeDtypeStruct((PAIR * planes + 16, half), BF16)
    chunks = pl.pallas_call(
        pack_second,
        out_shape=[second] * pairs,
        in_specs=[VECTOR, SCALAR, VECTOR, VECTOR],
        out_specs=[VECTOR] * pairs,
        compiler_params=PARAMS,
        name="pack_second",
    )(raw, shear_offsets, from_left, from_right)
    got_second = exchange(chunks, slabs)
    wide = jax.ShapeDtypeStruct((4, scans * SLAB_ROWS, half), BF16)
    coarse = jax.ShapeDtypeStruct((LEVEL * scans // 2, half), F32)
    volume = pltpu.VMEM((slabs + 2, LANE, half), BF16)
    wide_first, coarse_first = pl.pallas_call(
        functools.partial(first_half, slabs, scans),
        out_shape=[wide, coarse],
        in_specs=[VECTOR] * (2 + slabs),
        out_specs=[VECTOR] * 2,
        scratch_shapes=[volume],
        compiler_params=PARAMS,
        name="first_half",
    )(table["rowscan"], table["level"], *got_first)
    return pl.pallas_call(
        functools.partial(second_half, slabs, scans),
        out_shape=[
            jax.ShapeDtypeStruct((SLAB_ROWS, scans, columns), BF16),
            jax.ShapeDtypeStruct((SLAB_ROWS // 2, scans // 2, columns // 2), BF16),
            jax.ShapeDtypeStruct((SLAB_ROWS // 4, scans // 4, columns // 4), BF16),
        ],
        in_specs=[VECTOR] * (8 + slabs),
        out_specs=[VECTOR] * 3,
        scratch_shapes=[
            volume,
            pltpu.VMEM((LANE, (slabs + 2) * LANE), BF16),
            pltpu.VMEM((4, scans * SLAB_ROWS, half), BF16),
            pltpu.VMEM((4, scans * SLAB_ROWS, LANE), BF16),
        ],
        compiler_params=PARAMS,
        name="second_half",
    )(
        table["rowscan"],
        table["level"],
        table["column"],
        table["level_column"],
        table["two"],
        table["two_column"],
        wide_first,
        coarse_first,
        *got_second,
    )


def solution(mesh):
    placed = (P("slab", None, "tile"), P("slab"), P())
    return jax.shard_map(
        body,
        mesh=mesh,
        in_specs=placed,
        out_specs=(P("slab", None, "tile"), P("slab", None, "tile"), P("slab", None, "tile")),
        check_vma=False,
    )
```

time: 148 us -> 40.4 us (0.27)
  the two profiles are of different devices: /device:TPU:1 before, /device:TPU:0 now
where the time goes in v1:
time: 40.4 us; the launch traced here: 39.9 us
  starting transfers between devices  16.2 us (40%)
  waiting for transfers between devices  12.8 us (32%)
  Pallas kernels  7.68 us (19%)
  local copies, waits for them, and re-layouts  2.42 us (6%)
  between operations  0.78 us (2%)
    ppermute x6, starting transfers between devices, exchange(): lax.ppermute(chunks[step], 'slab', [(i, i ^ 2 * step) for i in range(slab...  10.1 us
    ppermute x2, waiting for transfers between devices, shifted(): return lax.ppermute(block, 'tile', route)  5.86 us
    ppermute x6, waiting for transfers between devices, exchange(): lax.ppermute(chunks[step], 'slab', [(i, i ^ 2 * step) for i in range(slab...  5.72 us
    ppermute x2, starting transfers between devices, shifted(): return lax.ppermute(block, 'tile', route)  5.02 us
    pallas_call x1, Pallas kernels, body(): pl.pallas_call(functools.partial(second_half, slabs, scans), out_shape=[j...  4.4 us
    unnamed x18, local copies, waits for them, and re-layouts  2.42 us
    ppermute x8, waiting for transfers between devices, exchange(): result += [held[step], lax.ppermute(held[step], 'slab', swap)]  1.23 us
    pallas_call x1, Pallas kernels, body(): pl.pallas_call(pack_second, out_shape=[second] * pairs, in_specs=[VECTOR,...  1.23 us
  transfers between devices with their start and end apart: 16, of which 6 were waited for; matrix products, arithmetic and copies ran while one was open for 0% of the time, Pallas kernels for 5%

profile of v1, /device:TPU:0, one launch (start us, length us, event | category | flops | bytes accessed | tf_op | source)
XLA Modules:
  0.0 39.9 jit_solution(15051792282172111296)
XLA Ops:
  0.6 0.0 copy-start
  0.7 1.1 %copy-done.1 = bf16[4,120,512]{2,1,0:T(8,128)(2,1)S(1)} copy-done((bf16[4,120,512]{2,1,0:T(8,128)(2,1)S(1)}, bf16[4,120,512]{2,1,0:T(8,128)(2,1)}, u32[]{:S(2)}) %copy-start.1) | copy-done | bytes 491544
  1.7 0.7 %copy-done.7 = s32[4]{0:T(128)S(1)} copy-done((s32[4]{0:T(128)S(1)}, s32[4]{0:T(128)}, u32[]{:S(2)}) %copy-start.7) | copy-done | bytes 40
  2.4 0.7 %copy-done.8 = s32[3]{0:T(128)S(1)} copy-done((s32[3]{0:T(128)S(1)}, s32[3]{0:T(128)}, u32[]{:S(2)}) %copy-start.8) | copy-done | bytes 36
  3.0 1.2 %pack_first.1 = (bf16[8,480]{1,0:T(8,128)(2,1)S(1)}, bf16[8,480]{1,0:T(8,128)(2,1)S(1)}, bf16[168,256]{1,0:T(8,128)(2,1)S(1)}, bf16[168,256]{1,0:T(8,128)(2,1)S(...) custom-call(bf16[480,512]{1,0:T(8,128)(2,1)S(1)} %bitcast.1, s32[4]{0:T(128)S(1)} %copy-done.7, s32[3]{0:T(128)S(1)} %copy-done.8), custom_call_target="tpu_custom_call" | custom-call | tf_op jit(solution)/shard_map/pack_first/pallas_call | solution.py:293
  4.3 3.1 %collective-permute-start.1 = (bf16[168,256]{1,0:T(8,128)(2,1)S(1)}, bf16[168,256]{1,0:T(8,128)(2,1)S(1)}, u32[]{:S(2)}, u32[]{:S(2)}) collective-permute-start(bf16[168,256]{1,0:T(8,128)(2,1)S(1)} %get-tuple-element.16), channel_id=1, source_target_pairs={{0,2},{1,3},{2,0},{3,1},{4,6},{5,7},{6,4},{7,5},{8,10},{9,11},{10,... | collective-permute-start | bytes 258056 | tf_op jit(solution)/shard_map/ppermute | solution.py:269
  7.4 2.6 %collective-permute-start.3 = (bf16[168,256]{1,0:T(8,128)(2,1)S(1)}, bf16[168,256]{1,0:T(8,128)(2,1)S(1)}, u32[]{:S(2)}, u32[]{:S(2)}) collective-permute-start(bf16[168,256]{1,0:T(8,128)(2,1)S(1)} %get-tuple-element.17), channel_id=1, source_target_pairs={{0,4},{1,5},{2,6},{3,7},{4,0},{5,1},{6,2},{7,3},{8,12},{9,13},{10,... | collective-permute-start | bytes 258056 | tf_op jit(solution)/shard_map/ppermute | solution.py:269
  10.0 3.7 %collective-permute-start.7 = (bf16[8,480]{1,0:T(8,128)(2,1)S(1)}, bf16[8,480]{1,0:T(8,128)(2,1)S(1)}, u32[]{:S(2)}, u32[]{:S(2)}) collective-permute-start(bf16[8,480]{1,0:T(8,128)(2,1)S(1)} %get-tuple-element.21), channel_id=1, source_target_pairs={{0,8},{8,16},{16,24},{1,9},{9,17},{17,25},{2,10},{10,18},{18,26},{... | collective-permute-start | bytes 23048 | tf_op jit(solution)/shard_map/ppermute | solution.py:280
  13.7 1.3 %collective-permute-done.7.from_left_ref = bf16[8,480]{1,0:T(8,128)(2,1)S(1)} collective-permute-done((bf16[8,480]{1,0:T(8,128)(2,1)S(1)}, bf16[8,480]{1,0:T(8,128)(2,1)S(1)}, u32[]{:S(2)}, u32[]{:S(2)}) %collective-permute-start.7) | collective-permute-done | bytes 7712 | tf_op jit(solution)/shard_map/ppermute | solution.py:280
  15.1 1.3 %collective-permute-start.8 = (bf16[8,480]{1,0:T(8,128)(2,1)S(1)}, bf16[8,480]{1,0:T(8,128)(2,1)S(1)}, u32[]{:S(2)}, u32[]{:S(2)}) collective-permute-start(bf16[8,480]{1,0:T(8,128)(2,1)S(1)} %get-tuple-element.22), channel_id=1, source_target_pairs={{8,0},{16,8},{24,16},{9,1},{17,9},{25,17},{10,2},{18,10},{26,18},{... | collective-permute-start | bytes 23048 | tf_op jit(solution)/shard_map/ppermute | solution.py:280
  16.4 4.5 %collective-permute-done.8.from_right_ref = bf16[8,480]{1,0:T(8,128)(2,1)S(1)} collective-permute-done((bf16[8,480]{1,0:T(8,128)(2,1)S(1)}, bf16[8,480]{1,0:T(8,128)(2,1)S(1)}, u32[]{:S(2)}, u32[]{:S(2)}) %collective-permute-start.8) | collective-permute-done | bytes 7712 | tf_op jit(solution)/shard_map/ppermute | solution.py:280
  20.9 1.2 %pack_second.1 = (bf16[184,256]{1,0:T(8,128)(2,1)S(1)}, bf16[184,256]{1,0:T(8,128)(2,1)S(1)}, bf16[184,256]{1,0:T(8,128)(2,1)S(1)}, bf16[184,256]{1,0:T(8,128)(2,1)S(1)}) custom-call(bf16[480,512]{1,0:T(8,128)(2,1)S(1)} %bitcast.2, s32[4]{0:T(128)S(1)} %copy-done.7, bf16[8,480]{1,0:T(8,128)(2,1)S(1)} %collective-permute-done.7.from_left_ref, ...), custom_call_target="tpu_custom_call" | custom-call | tf_op jit(solution)/shard_map/pack_second/pallas_call | solution.py:305
  22.1 0.7 %collective-permute-start.10 = (bf16[184,256]{1,0:T(8,128)(2,1)S(1)}, bf16[184,256]{1,0:T(8,128)(2,1)S(1)}, u32[]{:S(2)}, u32[]{:S(2)}) collective-permute-start(bf16[184,256]{1,0:T(8,128)(2,1)S(1)} %get-tuple-element.24), channel_id=1, source_target_pairs={{0,2},{1,3},{2,0},{3,1},{4,6},{5,7},{6,4},{7,5},{8,10},{9,11},{10,... | collective-permute-start | bytes 282632 | tf_op jit(solution)/shard_map/ppermute | solution.py:269
  22.8 3.5 %collective-permute-start.12 = (bf16[184,256]{1,0:T(8,128)(2,1)S(1)}, bf16[184,256]{1,0:T(8,128)(2,1)S(1)}, u32[]{:S(2)}, u32[]{:S(2)}) collective-permute-start(bf16[184,256]{1,0:T(8,128)(2,1)S(1)} %get-tuple-element.25), channel_id=1, source_target_pairs={{0,4},{1,5},{2,6},{3,7},{4,0},{5,1},{6,2},{7,3},{8,12},{9,13},{10,... | collective-permute-start | bytes 282632 | tf_op jit(solution)/shard_map/ppermute | solution.py:269
  26.3 0.2 collective-permute-start.14
  26.5 0.5 %collective-permute-start.4 = (bf16[168,256]{1,0:T(8,128)(2,1)S(1)}, bf16[168,256]{1,0:T(8,128)(2,1)S(1)}, u32[]{:S(2)}, u32[]{:S(2)}) collective-permute-start(bf16[168,256]{1,0:T(8,128)(2,1)S(1)} %collective-permute-done.3.refs_4_), channel_id=1, source_target_pairs={{0,1},{1,0},{2,3},{3,2},{4,5},{5,4},{6,7},{7,6},{8,9},{9,8},{10,11... | collective-permute-start | bytes 258056 | tf_op jit(solution)/shard_map/ppermute | solution.py:273
  27.1 0.3 collective-permute-done.10.refs_10_
  27.4 4.2 %collective-permute-done.12.refs_12_ = bf16[184,256]{1,0:T(8,128)(2,1)S(1)} collective-permute-done((bf16[184,256]{1,0:T(8,128)(2,1)S(1)}, bf16[184,256]{1,0:T(8,128)(2,1)S(1)}, u32[]{:S(2)}, u32[]{:S(2)}) %collective-permute-start.12) | collective-permute-done | bytes 94240 | tf_op jit(solution)/shard_map/ppermute | solution.py:269
  31.6 1.2 %collective-permute-done.14.refs_14_ = bf16[184,256]{1,0:T(8,128)(2,1)S(1)} collective-permute-done((bf16[184,256]{1,0:T(8,128)(2,1)S(1)}, bf16[184,256]{1,0:T(8,128)(2,1)S(1)}, u32[]{:S(2)}, u32[]{:S(2)}) %collective-permute-start.14) | collective-permute-done | bytes 94240 | tf_op jit(solution)/shard_map/ppermute | solution.py:269
  32.8 0.5 %collective-permute-start.15 = (bf16[184,256]{1,0:T(8,128)(2,1)S(1)}, bf16[184,256]{1,0:T(8,128)(2,1)S(1)}, u32[]{:S(2)}, u32[]{:S(2)}) collective-permute-start(bf16[184,256]{1,0:T(8,128)(2,1)S(1)} %collective-permute-done.14.refs_14_), channel_id=1, source_target_pairs={{0,1},{1,0},{2,3},{3,2},{4,5},{5,4},{6,7},{7,6},{8,9},{9,8},{10,11... | collective-permute-start | bytes 282632 | tf_op jit(solution)/shard_map/ppermute | solution.py:273
  33.3 0.1 collective-permute-start.6
  33.4 1.2 %collective-permute-done.6.refs_7_ = bf16[168,256]{1,0:T(8,128)(2,1)S(1)} collective-permute-done((bf16[168,256]{1,0:T(8,128)(2,1)S(1)}, bf16[168,256]{1,0:T(8,128)(2,1)S(1)}, u32[]{:S(2)}, u32[]{:S(2)}) %collective-permute-start.6) | collective-permute-done | bytes 86048 | tf_op jit(solution)/shard_map/ppermute | solution.py:273
  34.6 0.9 %first_half.1 = (bf16[4,512,256]{2,1,0:T(8,128)(2,1)S(1)}, f32[176,256]{1,0:T(8,128)S(1)}) custom-call(bf16[512,512]{1,0:T(8,128)(2,1)S(1)} %copy-done, bf16[176,1024]{1,0:T(8,128)(2,1)S(1)} %copy-done.2, bf16[168,256]{1,0:T(8,128)(2,1)S(1)} %get-tuple-element.15.refs_0_, bf16[168,256]{1,0:T(8,128)(2,1)S(1)} %collective-permute-done.refs_1_, ...), custom_call_target="tpu_custom_call" | custom-call | tf_op jit(solution)/shard_map/first_half/pallas_call | solution.py:317
  35.5 4.4 %second_half.1 = (bf16[16,32,512]{2,1,0:T(8,128)(2,1)}, bf16[8,16,256]{2,1,0:T(8,128)(2,1)}, bf16[4,8,128]{2,1,0:T(8,128)(2,1)}) custom-call(bf16[512,512]{1,0:T(8,128)(2,1)S(1)} %copy-done, bf16[176,1024]{1,0:T(8,128)(2,1)S(1)} %copy-done.2, bf16[4,512,256]{2,1,0:T(8,128)(2,1)S(1)} %copy-done.3, bf16[640,384]{1,0:T(8,128)(2,1)S(1)} %copy-done.4, ...), custom_call_target="tpu_custom_call" | custom-call | tf_op jit(solution)/shard_map/second_half/pallas_call | solution.py:326
  (30 shorter events, 0.1 us)
Async XLA Ops:
  0.6 34.0 %copy-start = (bf16[512,512]{1,0:T(8,128)(2,1)S(1)}, bf16[512,512]{1,0:T(8,128)(2,1)}, u32[]{:S(2)}) copy-start(bf16[512,512]{1,0:T(8,128)(2,1)} %constant.12.clone.rowscan_ref.refs_0_) | copy-start | bytes 1572868
  0.6 1.1 %copy-start.1 = (bf16[4,120,512]{2,1,0:T(8,128)(2,1)S(1)}, bf16[4,120,512]{2,1,0:T(8,128)(2,1)}, u32[]{:S(2)}) copy-start(bf16[4,120,512]{2,1,0:T(8,128)(2,1)} %param.9) | copy-start | bytes 1474564
  1.7 0.7 %copy-start.7 = (s32[4]{0:T(128)S(1)}, s32[4]{0:T(128)}, u32[]{:S(2)}) copy-start(s32[4]{0:T(128)} %shear_ref.3) | copy-start | bytes 52
  4.3 30.3 %copy-start.2 = (bf16[176,1024]{1,0:T(8,128)(2,1)S(1)}, bf16[176,1024]{1,0:T(8,128)(2,1)}, u32[]{:S(2)}) copy-start(bf16[176,1024]{1,0:T(8,128)(2,1)} %constant.13.clone.level_ref.refs_1_) | copy-start | bytes 1081348
  4.3 18.5 %collective-permute-start.1 = (bf16[168,256]{1,0:T(8,128)(2,1)S(1)}, bf16[168,256]{1,0:T(8,128)(2,1)S(1)}, u32[]{:S(2)}, u32[]{:S(2)}) collective-permute-start(bf16[168,256]{1,0:T(8,128)(2,1)S(1)} %get-tuple-element.16), channel_id=1, source_target_pairs={{0,2},{1,3},{2,0},{3,1},{4,6},{5,7},{6,4},{7,5},{8,10},{9,11},{10,... | collective-permute-start | bytes 258056 | tf_op jit(solution)/shard_map/ppermute | solution.py:269
  7.4 18.9 %collective-permute-start.3 = (bf16[168,256]{1,0:T(8,128)(2,1)S(1)}, bf16[168,256]{1,0:T(8,128)(2,1)S(1)}, u32[]{:S(2)}, u32[]{:S(2)}) collective-permute-start(bf16[168,256]{1,0:T(8,128)(2,1)S(1)} %get-tuple-element.17), channel_id=1, source_target_pairs={{0,4},{1,5},{2,6},{3,7},{4,0},{5,1},{6,2},{7,3},{8,12},{9,13},{10,... | collective-permute-start | bytes 258056 | tf_op jit(solution)/shard_map/ppermute | solution.py:269
  9.9 16.6 %collective-permute-start.5 = (bf16[168,256]{1,0:T(8,128)(2,1)S(1)}, bf16[168,256]{1,0:T(8,128)(2,1)S(1)}, u32[]{:S(2)}, u32[]{:S(2)}) collective-permute-start(bf16[168,256]{1,0:T(8,128)(2,1)S(1)} %get-tuple-element.18), channel_id=1, source_target_pairs={{0,6},{1,7},{2,4},{3,5},{4,2},{5,3},{6,0},{7,1},{8,14},{9,15},{10,... | collective-permute-start | bytes 258056 | tf_op jit(solution)/shard_map/ppermute | solution.py:269
  10.0 25.5 %copy-start.3 = (bf16[4,512,256]{2,1,0:T(8,128)(2,1)S(1)}, bf16[4,512,256]{2,1,0:T(8,128)(2,1)}, u32[]{:S(2)}) copy-start(bf16[4,512,256]{2,1,0:T(8,128)(2,1)} %constant.14.clone.refs_2_) | copy-start | bytes 3145732
  10.0 16.6 %collective-permute-start = (bf16[168,256]{1,0:T(8,128)(2,1)S(1)}, bf16[168,256]{1,0:T(8,128)(2,1)S(1)}, u32[]{:S(2)}, u32[]{:S(2)}) collective-permute-start(bf16[168,256]{1,0:T(8,128)(2,1)S(1)} %get-tuple-element.15.refs_0_), channel_id=1, source_target_pairs={{0,1},{1,0},{2,3},{3,2},{4,5},{5,4},{6,7},{7,6},{8,9},{9,8},{10,11... | collective-permute-start | bytes 258056 | tf_op jit(solution)/shard_map/ppermute | solution.py:273
  10.0 5.1 %collective-permute-start.7 = (bf16[8,480]{1,0:T(8,128)(2,1)S(1)}, bf16[8,480]{1,0:T(8,128)(2,1)S(1)}, u32[]{:S(2)}, u32[]{:S(2)}) collective-permute-start(bf16[8,480]{1,0:T(8,128)(2,1)S(1)} %get-tuple-element.21), channel_id=1, source_target_pairs={{0,8},{8,16},{16,24},{1,9},{9,17},{17,25},{2,10},{10,18},{18,26},{... | collective-permute-start | bytes 23048 | tf_op jit(solution)/shard_map/ppermute | solution.py:280
  15.1 5.8 %collective-permute-start.8 = (bf16[8,480]{1,0:T(8,128)(2,1)S(1)}, bf16[8,480]{1,0:T(8,128)(2,1)S(1)}, u32[]{:S(2)}, u32[]{:S(2)}) collective-permute-start(bf16[8,480]{1,0:T(8,128)(2,1)S(1)} %get-tuple-element.22), channel_id=1, source_target_pairs={{8,0},{16,8},{24,16},{9,1},{17,9},{25,17},{10,2},{18,10},{26,18},{... | collective-permute-start | bytes 23048 | tf_op jit(solution)/shard_map/ppermute | solution.py:280
  22.1 5.3 %collective-permute-start.10 = (bf16[184,256]{1,0:T(8,128)(2,1)S(1)}, bf16[184,256]{1,0:T(8,128)(2,1)S(1)}, u32[]{:S(2)}, u32[]{:S(2)}) collective-permute-start(bf16[184,256]{1,0:T(8,128)(2,1)S(1)} %get-tuple-element.24), channel_id=1, source_target_pairs={{0,2},{1,3},{2,0},{3,1},{4,6},{5,7},{6,4},{7,5},{8,10},{9,11},{10,... | collective-permute-start | bytes 282632 | tf_op jit(solution)/shard_map/ppermute | solution.py:269
  22.8 8.8 %collective-permute-start.12 = (bf16[184,256]{1,0:T(8,128)(2,1)S(1)}, bf16[184,256]{1,0:T(8,128)(2,1)S(1)}, u32[]{:S(2)}, u32[]{:S(2)}) collective-permute-start(bf16[184,256]{1,0:T(8,128)(2,1)S(1)} %get-tuple-element.25), channel_id=1, source_target_pairs={{0,4},{1,5},{2,6},{3,7},{4,0},{5,1},{6,2},{7,3},{8,12},{9,13},{10,... | collective-permute-start | bytes 282632 | tf_op jit(solution)/shard_map/ppermute | solution.py:269
  26.3 6.5 %collective-permute-start.14 = (bf16[184,256]{1,0:T(8,128)(2,1)S(1)}, bf16[184,256]{1,0:T(8,128)(2,1)S(1)}, u32[]{:S(2)}, u32[]{:S(2)}) collective-permute-start(bf16[184,256]{1,0:T(8,128)(2,1)S(1)} %get-tuple-element.26), channel_id=1, source_target_pairs={{0,6},{1,7},{2,4},{3,5},{4,2},{5,3},{6,0},{7,1},{8,14},{9,15},{10,... | collective-permute-start | bytes 282632 | tf_op jit(solution)/shard_map/ppermute | solution.py:269
  26.5 6.3 %collective-permute-start.2 = (bf16[168,256]{1,0:T(8,128)(2,1)S(1)}, bf16[168,256]{1,0:T(8,128)(2,1)S(1)}, u32[]{:S(2)}, u32[]{:S(2)}) collective-permute-start(bf16[168,256]{1,0:T(8,128)(2,1)S(1)} %collective-permute-done.1.refs_2_), channel_id=1, source_target_pairs={{0,1},{1,0},{2,3},{3,2},{4,5},{5,4},{6,7},{7,6},{8,9},{9,8},{10,11... | collective-permute-start | bytes 258056 | tf_op jit(solution)/shard_map/ppermute | solution.py:273
  26.5 6.8 %collective-permute-start.4 = (bf16[168,256]{1,0:T(8,128)(2,1)S(1)}, bf16[168,256]{1,0:T(8,128)(2,1)S(1)}, u32[]{:S(2)}, u32[]{:S(2)}) collective-permute-start(bf16[168,256]{1,0:T(8,128)(2,1)S(1)} %collective-permute-done.3.refs_4_), channel_id=1, source_target_pairs={{0,1},{1,0},{2,3},{3,2},{4,5},{5,4},{6,7},{7,6},{8,9},{9,8},{10,11... | collective-permute-start | bytes 258056 | tf_op jit(solution)/shard_map/ppermute | solution.py:273
  27.4 8.2 %copy-start.4 = (bf16[640,384]{1,0:T(8,128)(2,1)S(1)}, bf16[640,384]{1,0:T(8,128)(2,1)}, u32[]{:S(2)}) copy-start(bf16[640,384]{1,0:T(8,128)(2,1)} %constant.15.clone.refs_3_) | copy-start | bytes 1474564
  27.4 8.2 %copy-start.5 = (bf16[384,128]{1,0:T(8,128)(2,1)S(1)}, bf16[384,128]{1,0:T(8,128)(2,1)}, u32[]{:S(2)}) copy-start(bf16[384,128]{1,0:T(8,128)(2,1)} %constant.17.clone.refs_5_) | copy-start | bytes 294916
  27.4 8.2 %copy-start.6 = (bf16[32,176]{1,0:T(8,128)(2,1)S(1)}, bf16[32,176]{1,0:T(8,128)(2,1)}, u32[]{:S(2)}) copy-start(bf16[32,176]{1,0:T(8,128)(2,1)} %constant.16.clone.refs_4_) | copy-start | bytes 33796
  27.4 8.1 %collective-permute-start.9 = (bf16[184,256]{1,0:T(8,128)(2,1)S(1)}, bf16[184,256]{1,0:T(8,128)(2,1)S(1)}, u32[]{:S(2)}, u32[]{:S(2)}) collective-permute-start(bf16[184,256]{1,0:T(8,128)(2,1)S(1)} %get-tuple-element.23.refs_8_), channel_id=1, source_target_pairs={{0,1},{1,0},{2,3},{3,2},{4,5},{5,4},{6,7},{7,6},{8,9},{9,8},{10,11... | collective-permute-start | bytes 282632 | tf_op jit(solution)/shard_map/ppermute | solution.py:273
  31.6 3.9 %collective-permute-start.11 = (bf16[184,256]{1,0:T(8,128)(2,1)S(1)}, bf16[184,256]{1,0:T(8,128)(2,1)S(1)}, u32[]{:S(2)}, u32[]{:S(2)}) collective-permute-start(bf16[184,256]{1,0:T(8,128)(2,1)S(1)} %collective-permute-done.10.refs_10_), channel_id=1, source_target_pairs={{0,1},{1,0},{2,3},{3,2},{4,5},{5,4},{6,7},{7,6},{8,9},{9,8},{10,11... | collective-permute-start | bytes 282632 | tf_op jit(solution)/shard_map/ppermute | solution.py:273
  32.8 2.7 %collective-permute-start.13 = (bf16[184,256]{1,0:T(8,128)(2,1)S(1)}, bf16[184,256]{1,0:T(8,128)(2,1)S(1)}, u32[]{:S(2)}, u32[]{:S(2)}) collective-permute-start(bf16[184,256]{1,0:T(8,128)(2,1)S(1)} %collective-permute-done.12.refs_12_), channel_id=1, source_target_pairs={{0,1},{1,0},{2,3},{3,2},{4,5},{5,4},{6,7},{7,6},{8,9},{9,8},{10,11... | collective-permute-start | bytes 282632 | tf_op jit(solution)/shard_map/ppermute | solution.py:273
  32.8 2.7 %collective-permute-start.15 = (bf16[184,256]{1,0:T(8,128)(2,1)S(1)}, bf16[184,256]{1,0:T(8,128)(2,1)S(1)}, u32[]{:S(2)}, u32[]{:S(2)}) collective-permute-start(bf16[184,256]{1,0:T(8,128)(2,1)S(1)} %collective-permute-done.14.refs_14_), channel_id=1, source_target_pairs={{0,1},{1,0},{2,3},{3,2},{4,5},{5,4},{6,7},{7,6},{8,9},{9,8},{10,11... | collective-permute-start | bytes 282632 | tf_op jit(solution)/shard_map/ppermute | solution.py:273
  33.3 1.3 %collective-permute-start.6 = (bf16[168,256]{1,0:T(8,128)(2,1)S(1)}, bf16[168,256]{1,0:T(8,128)(2,1)S(1)}, u32[]{:S(2)}, u32[]{:S(2)}) collective-permute-start(bf16[168,256]{1,0:T(8,128)(2,1)S(1)} %collective-permute-done.5.refs_6_), channel_id=1, source_target_pairs={{0,1},{1,0},{2,3},{3,2},{4,5},{5,4},{6,7},{7,6},{8,9},{9,8},{10,11... | collective-permute-start | bytes 258056 | tf_op jit(solution)/shard_map/ppermute | solution.py:273
  (1 other events, 0.7 us)

commit v2 on v1

v2 whole, which is shorter than its diff:
```python
import functools
import math

import jax
import jax.numpy as jnp
import ml_dtypes
import numpy as np
from jax import lax
from jax.experimental import pallas as pl
from jax.experimental.pallas import tpu as pltpu
from jax.sharding import PartitionSpec as P

SLAB_ROWS = 16
STRIP = 6
RADIUS = 4
LOW = 6
HIGH = 4
PAIR = 2 * SLAB_ROWS + LOW + HIGH
NEED = SLAB_ROWS + LOW + HIGH
LEVEL = 11
LANE = 128
F32 = jnp.float32
BF16 = jnp.bfloat16


def gauss_taps(sigma_value):
    entries = [math.exp(-(j * j) / (2.0 * sigma_value * sigma_value)) for j in range(-RADIUS, RADIUS + 1)]
    weight_sum = sum(entries)
    return np.array([entry / weight_sum for entry in entries], np.float64)


BINOMIAL = np.array([1.0, 4.0, 6.0, 4.0, 1.0], np.float64) / 16.0


def band(weights, source, target):
    reach = len(weights) // 2
    offset = source[None, :] - target[:, None] + reach
    inside = (offset >= 0) & (offset < len(weights))
    return np.where(inside, weights[np.clip(offset, 0, len(weights) - 1)], 0.0)


def two_parts(table):
    high = table.astype(ml_dtypes.bfloat16)
    return [high, (table - high.astype(np.float64)).astype(ml_dtypes.bfloat16)]


def row_scan_table(row_band, scan_band, groups):
    rows_out, rows_in = row_band.shape
    scans_out = scan_band.shape[0]
    scans = scan_band.reshape(scans_out, groups, 4)
    table = np.einsum("yr,sgp->ysgrp", row_band, scans)
    table = table.reshape(rows_out * scans_out, groups, rows_in * 4)
    table = np.pad(table, ((0, 0), (0, 0), (0, LANE - rows_in * 4)))
    return table.reshape(rows_out * scans_out, groups * LANE)


def tables(scans, columns):
    row_in = np.arange(NEED) - LOW
    own = np.arange(SLAB_ROWS)
    near = np.arange(16) - 4
    block = np.arange(8)
    cut = columns - LANE
    rim = np.where(np.arange(LANE) < LANE // 2, columns, -LANE) + np.arange(LANE)
    last = np.concatenate([np.arange(cut, columns), rim])
    touched = np.concatenate([np.arange(cut, columns), np.arange(LANE // 2), np.arange(cut - LANE // 2, cut)])
    rowscan, column_first, column_last = [], [], []
    for sigma, sign in ((1.0, 1.0), (1.6, -1.0)):
        taps = gauss_taps(sigma)
        rowscan += two_parts(row_scan_table(band(taps, row_in, own), band(taps, near, block), 4))
        column_first += two_parts(sign * band(taps, np.arange(4 * LANE) - LANE, np.arange(2 * LANE)).T)
        column_last += two_parts(sign * band(taps, last, touched).T)
    level_rows = 2 * np.arange(LEVEL) - 4
    level_scans = 2 * np.arange(scans // 2)
    level = row_scan_table(
        band(BINOMIAL, row_in, level_rows), band(BINOMIAL, np.arange(scans), level_scans), scans // 4
    )
    edges = np.array([-4, -2, columns, columns + 2])
    targets = np.concatenate([2 * np.arange(columns // 2), edges])
    two = np.einsum(
        "yr,sp->ysrp",
        band(BINOMIAL, np.arange(LEVEL) - 2, 2 * np.arange(4)),
        band(BINOMIAL, np.arange(scans // 2), 2 * np.arange(scans // 4)),
    ).reshape(scans, LEVEL * scans // 2)
    fill = ((0, 0), (0, LANE - 4))
    small = ml_dtypes.bfloat16
    return dict(
        rowscan=np.concatenate(rowscan, 0),
        level=level.astype(small),
        column_first=np.stack(column_first),
        column_last=np.stack(column_last),
        level_first=np.pad(band(BINOMIAL, np.arange(cut), targets).T, fill).astype(small),
        level_last=np.pad(band(BINOMIAL, last, targets).T, fill).astype(small),
        two=two.astype(small),
        two_column=np.pad(band(BINOMIAL, targets // 2, 2 * np.arange(columns // 4)), fill).T.astype(small),
    )


def dot(left, right):
    return jnp.dot(left, right, preferred_element_type=F32)


def dot_rows(left, right):
    return lax.dot_general(left, right, (((1,), (1,)), ((), ())), preferred_element_type=F32)


def place_table(shift, group, camera):
    slots = shift.shape[0]
    slot = lax.broadcasted_iota(jnp.int32, (slots, 1), 0)
    plane, row = slot & 3, slot >> 2
    source = group * (2 * SLAB_ROWS) - LOW + row - shift
    inside = (source >= 0) & (source < camera) & (row < PAIR)
    wanted = jnp.where(inside, plane * camera + source, -1)
    lane = lax.broadcasted_iota(jnp.int32, (slots, 4 * camera), 1)
    return jnp.where(lane == wanted, 1.0, 0.0).astype(BF16)


def pack_first(raw_ref, shear_ref, width_ref, right_ref, left_ref, kept_ref, shift_ref, *refs):
    out_refs, (shears, widths, raw_sem, shear_sem, width_sem) = refs[:-5], refs[-5:]
    load_raw = pltpu.make_async_copy(raw_ref, kept_ref, raw_sem)
    load_shear = pltpu.make_async_copy(shear_ref, shears, shear_sem)
    load_width = pltpu.make_async_copy(width_ref, widths, width_sem)
    load_raw.start()
    load_shear.start()
    load_width.start()
    camera = raw_ref.shape[0] // 4
    columns = raw_ref.shape[1]
    tile = lax.axis_index("tile")
    tiles = lax.axis_size("tile")
    mine = lax.axis_index("slab") >> 1
    lane = lax.broadcasted_iota(jnp.int32, (8, columns), 1)
    line = lax.broadcasted_iota(jnp.int32, (8, columns), 0)
    load_shear.wait()
    load_width.wait()
    right_width = widths[jnp.minimum(tile, tiles - 2)]
    left_width = widths[jnp.maximum(tile - 1, 0)]
    toward_right = jnp.where((lane == columns - right_width - 8 + line) & (line >= 2), 1.0, 0.0).astype(BF16)
    toward_left = jnp.where((lane == left_width + line) & (line < 6), 1.0, 0.0).astype(BF16)
    plane = lax.broadcasted_iota(jnp.int32, shift_ref.shape, 0) & 3
    shift_ref[...] = jnp.where(plane < 2, jnp.where(plane == 0, shears[0], shears[1]), jnp.where(plane == 2, shears[2], shears[3]))
    load_raw.wait()
    for step, out_ref in enumerate(out_refs):
        table = place_table(shift_ref[: PAIR * 4, :1], mine ^ step, camera)
        out_ref[...] = dot(table, kept_ref[:, : columns - LANE]).astype(BF16)
    right_ref[...] = dot_rows(toward_right, kept_ref[...]).astype(BF16)
    left_ref[...] = dot_rows(toward_left, kept_ref[...]).astype(BF16)


def stage(order_ref, *refs):
    sems, refs = refs[-1], refs[:-1]
    count = len(refs) // 2
    loads = [pltpu.make_async_copy(refs[index], refs[count + index], sems.at[index]) for index in range(count)]
    for load in loads:
        load.start()
    for load in loads:
        load.wait()


def pack_second(raw_ref, shift_ref, from_left_ref, from_right_ref, order_ref, *out_refs):
    camera = raw_ref.shape[0] // 4
    columns = raw_ref.shape[1]
    mine = lax.axis_index("slab") >> 1
    tile = lax.axis_index("tile")
    right = jnp.where(tile < lax.axis_size("tile") - 1, from_right_ref[...].astype(F32), 0.0)
    left = jnp.where(tile > 0, from_left_ref[...].astype(F32), 0.0)
    strips = jnp.concatenate([right, left], 0).astype(BF16)
    for step, out_ref in enumerate(out_refs):
        table = place_table(shift_ref[:, :1], mine ^ step, camera)
        out_ref[: PAIR * 4, :] = dot(table[: PAIR * 4], raw_ref[:, columns - LANE :]).astype(BF16)
        placed = dot_rows(strips, table).astype(BF16)
        out_ref[PAIR * 4 : PAIR * 4 + 16, :] = placed[:, :LANE]
        out_ref[PAIR * 4 + 16 :, :] = placed[:, LANE:]


def collect(in_refs, volume, scans):
    slab = lax.axis_index("slab")
    core = slab & 1
    lanes = in_refs[0].shape[-1]
    groups = scans // 4
    outside = jnp.zeros((LANE,) + volume.shape[2:], BF16)
    volume[0] = outside
    volume[groups + 1] = outside
    for index, in_ref in enumerate(in_refs):
        group = (slab ^ index) + 1
        start = pl.multiple_of(core * (SLAB_ROWS * 4), SLAB_ROWS * 4)
        volume[group, : NEED * 4, :lanes] = in_ref[pl.ds(start, NEED * 4), :]
        volume[group, NEED * 4 :, :lanes] = jnp.zeros((LANE - NEED * 4, lanes), BF16)


def split(value):
    high = value.astype(BF16)
    return high, (value - high.astype(F32)).astype(BF16)


def row_scan(rowscan_ref, volume, block, wide):
    rows = 8 * SLAB_ROWS
    both = dot(rowscan_ref[...], volume[2 * block : 2 * block + 4].reshape(4 * LANE, volume.shape[-1]))
    for sigma in range(2):
        total = both[2 * sigma * rows : (2 * sigma + 1) * rows] + both[(2 * sigma + 1) * rows : (2 * sigma + 2) * rows]
        high, low = split(total)
        wide[2 * sigma, block * rows : (block + 1) * rows, :] = high
        wide[2 * sigma + 1, block * rows : (block + 1) * rows, :] = low


def across(wide, rows, lanes, column_ref, taken):
    total = None
    for sigma in range(2):
        high, low = wide[2 * sigma, rows, lanes], wide[2 * sigma + 1, rows, lanes]
        part = dot(high, column_ref[2 * sigma, taken]) + dot(low, column_ref[2 * sigma, taken])
        part = part + dot(high, column_ref[2 * sigma + 1, taken])
        total = part if total is None else total + part
    return total


def level_part(level_ref, level_column_ref, volume, scans):
    groups = scans // 4
    high, low = split(dot(level_ref[...], volume[1 : groups + 1].reshape(groups * LANE, volume.shape[-1])))
    return dot(high, level_column_ref[...]) + dot(low, level_column_ref[...])


def first_half(count, scans, rowscan_ref, level_ref, column_ref, level_column_ref, *refs):
    in_refs, (partial_ref, coarse_ref, volume, wide) = refs[:count], refs[count:]
    collect(in_refs, volume, scans)
    for block in range(scans // 8):
        row_scan(rowscan_ref, volume, block, wide)
    cut = wide.shape[-1]
    for start in range(0, partial_ref.shape[1], 2 * LANE):
        low, high = max(start - LANE, 0), min(start + 3 * LANE, cut)
        taken = slice(low - start + LANE, high - start + LANE)
        partial_ref[:, start : start + 2 * LANE] = across(wide, slice(None), slice(low, high), column_ref, taken)
    coarse_ref[...] = level_part(level_ref, level_column_ref, volume, scans)


def second_half(count, scans, rowscan_ref, level_ref, column_ref, level_column_ref, two_ref, two_column_ref, *refs):
    partial_ref, coarse_ref, *in_refs = refs[: 2 + count]
    difference_ref, one_ref, second_ref, volume, strips, wide, held, sems = refs[2 + count :]
    slab = lax.axis_index("slab")
    slabs = lax.axis_size("slab")
    tile = lax.axis_index("tile")
    tiles = lax.axis_size("tile")
    core = slab & 1
    groups = scans // 4
    columns = partial_ref.shape[1]
    cut = columns - LANE
    collect(in_refs, volume, scans)
    for index, in_ref in enumerate(in_refs):
        place = pl.multiple_of((slab ^ index) * LANE, LANE)
        both = jnp.concatenate([in_ref[PAIR * 4 : PAIR * 4 + 16, :], in_ref[PAIR * 4 + 16 :, :]], 1).astype(F32)
        both = jnp.where(core == 0, both[:, :LANE], both[:, SLAB_ROWS * 4 : SLAB_ROWS * 4 + LANE])
        strips[:, pl.ds(place, LANE)] = both.astype(BF16)
    line = lax.broadcasted_iota(jnp.int32, (16, LANE), 0)
    lane = lax.broadcasted_iota(jnp.int32, (16, LANE), 1)
    spread = jnp.where(lane == jnp.where(line < 8, line, line + LANE - 16), 1.0, 0.0).astype(BF16)
    rim = lax.dot_general(strips[...], spread, (((0,), (0,)), ((), ())), preferred_element_type=F32)
    volume[1 : groups + 1, :, LANE:] = rim.astype(BF16).reshape(groups, LANE, LANE)

    level = coarse_ref[...] + level_part(level_ref, level_column_ref, volume, scans)
    half = columns // 2
    shape = (LEVEL, scans // 2, level.shape[-1])
    level = level.reshape(shape)
    row = slab * (SLAB_ROWS // 2) - 2 + lax.broadcasted_iota(jnp.int32, shape, 0)
    place = lax.broadcasted_iota(jnp.int32, shape, 2) - half
    keep = (row >= 0) & (row < slabs * (SLAB_ROWS // 2))
    keep = keep & ((place < 0) | (place >= 2) | (tile > 0)) & ((place < 2) | (tile < tiles - 1))
    ready = jnp.where(keep, level, 0.0).astype(BF16)
    one_ref[...] = ready[2:10, :, :half]
    high, low = split(dot(two_ref[...], ready.reshape(LEVEL * scans // 2, level.shape[-1])))
    second = dot(high, two_column_ref[...]) + dot(low, two_column_ref[...])
    second_ref[...] = second.reshape(second_ref.shape).astype(BF16)

    copies = []
    rows = 8 * SLAB_ROWS
    left = lax.broadcasted_iota(jnp.int32, (2 * rows, LANE), 1) < LANE // 2
    for pair in range(scans // 16):
        for block in (2 * pair, 2 * pair + 1):
            row_scan(rowscan_ref, volume, block, wide)
        here = slice(2 * pair * rows, 2 * (pair + 1) * rows)
        late = across(wide, here, slice(None), column_ref, slice(None))
        ends = late[:, LANE:]
        for start in range(0, columns, LANE):
            total = partial_ref[here, start : start + LANE]
            if start == cut:
                total = total + late[:, :LANE]
            if start == 0:
                total = total + jnp.where(left, ends, 0.0)
            if start == cut - LANE:
                total = total + jnp.where(left, 0.0, ends)
            total = total.reshape(2, SLAB_ROWS, 8, LANE)
            joined = jnp.concatenate([total[0], total[1]], 1)
            held[:, 16 * pair : 16 * pair + 16, start : start + LANE] = joined.astype(BF16)
        copy = pltpu.make_async_copy(
            held.at[:, 16 * pair : 16 * pair + 16, :], difference_ref.at[:, 16 * pair : 16 * pair + 16, :], sems.at[pair]
        )
        copy.start()
        copies.append(copy)
    for copy in copies:
        copy.wait()


VECTOR = pl.BlockSpec(memory_space=pltpu.VMEM)
ANYWHERE = pl.BlockSpec(memory_space=pl.ANY)
OUTSIDE = pl.BlockSpec(memory_space=pltpu.HBM)
PARAMS = pltpu.CompilerParams(vmem_limit_bytes=20 * 1024 * 1024)


def along(chunks, slabs):
    held = {}
    for step in sorted(range(1, len(chunks)), key=lambda step: (-(step & -step), step)):
        held[step] = lax.ppermute(chunks[step], "slab", [(i, i ^ (2 * step)) for i in range(slabs)])
    return held


def within(held, slabs):
    result = []
    for step in range(len(held)):
        result += [held[step], lax.ppermute(held[step], "slab", [(i, i ^ 1) for i in range(slabs)])]
    return result


def shifted(block, distance):
    count = lax.axis_size("tile")
    return lax.ppermute(block, "tile", [(i, (i + distance) % count) for i in range(count)])


def body(raw_stack, shear_offsets, intersection_widths):
    slabs = lax.axis_size("slab")
    planes, camera, columns = raw_stack.shape
    scans = planes * slabs
    cut = columns - LANE
    pairs = slabs // 2
    table = {name: jnp.asarray(value) for name, value in tables(scans, columns).items()}
    outside = [raw_stack.reshape(planes * camera, columns), shear_offsets, intersection_widths]
    outside = [pltpu.with_memory_space_constraint(each, pltpu.HBM) for each in outside]
    strip = jax.ShapeDtypeStruct((8, planes * camera), BF16)
    first = jax.ShapeDtypeStruct((PAIR * planes, cut), BF16)
    toward_right, toward_left, raw, shift, *chunks = pl.pallas_call(
        pack_first,
        out_shape=[strip, strip, jax.ShapeDtypeStruct((planes * camera, columns), BF16), jax.ShapeDtypeStruct((2 * LANE, LANE), jnp.int32)]
        + [first] * pairs,
        in_specs=[OUTSIDE] * 3,
        out_specs=[VECTOR] * (4 + pairs),
        scratch_shapes=[pltpu.SMEM(shear_offsets.shape, jnp.int32), pltpu.SMEM(intersection_widths.shape, jnp.int32)]
        + [pltpu.SemaphoreType.DMA] * 3,
        compiler_params=PARAMS,
        name="pack_first",
    )(*outside)
    first_held = along(chunks, slabs)
    from_left = shifted(toward_right, 1)
    from_right = shifted(toward_left, -1)
    own = chunks[0]
    second = jax.ShapeDtypeStruct((PAIR * planes + 32, LANE), BF16)
    names = list(table)
    staged = pl.pallas_call(
        stage,
        out_shape=[jax.ShapeDtypeStruct(table[name].shape, BF16) for name in names],
        in_specs=[ANYWHERE] + [OUTSIDE] * len(names),
        out_specs=[VECTOR] * len(names),
        scratch_shapes=[pltpu.SemaphoreType.DMA((len(names),))],
        compiler_params=PARAMS,
        name="stage",
    )(toward_left, *[pltpu.with_memory_space_constraint(table[name], pltpu.HBM) for name in names])
    table = dict(zip(names, staged))
    chunks = pl.pallas_call(
        pack_second,
        out_shape=[second] * pairs,
        in_specs=[VECTOR] * 4 + [ANYWHERE],
        out_specs=[VECTOR] * pairs,
        compiler_params=PARAMS,
        name="pack_second",
    )(raw, shift, from_left, from_right, table["two"])
    second_held = along(chunks, slabs)
    first_held[0] = own
    first_held = lax.optimization_barrier((first_held, chunks))[0]
    got_first = within(first_held, slabs)
    partial, coarse = pl.pallas_call(
        functools.partial(first_half, slabs, scans),
        out_shape=[
            jax.ShapeDtypeStruct((scans * SLAB_ROWS, columns), F32),
            jax.ShapeDtypeStruct((LEVEL * scans // 2, columns // 2 + LANE), F32),
        ],
        in_specs=[VECTOR] * (4 + slabs),
        out_specs=[VECTOR] * 2,
        scratch_shapes=[
            pltpu.VMEM((slabs + 2, LANE, cut), BF16),
            pltpu.VMEM((4, scans * SLAB_ROWS, cut), BF16),
        ],
        compiler_params=PARAMS,
        name="first_half",
    )(table["rowscan"], table["level"], table["column_first"], table["level_first"], *got_first)
    second_held[0] = chunks[0]
    second_held, partial = lax.optimization_barrier((second_held, partial))
    got_second = within(second_held, slabs)
    return pl.pallas_call(
        functools.partial(second_half, slabs, scans),
        out_shape=[
            jax.ShapeDtypeStruct((SLAB_ROWS, scans, columns), BF16),
            jax.ShapeDtypeStruct((SLAB_ROWS // 2, scans // 2, columns // 2), BF16),
            jax.ShapeDtypeStruct((SLAB_ROWS // 4, scans // 4, columns // 4), BF16),
        ],
        in_specs=[VECTOR] * (8 + slabs),
        out_specs=[OUTSIDE, VECTOR, VECTOR],
        scratch_shapes=[
            pltpu.VMEM((slabs + 2, LANE, 2 * LANE), BF16),
            pltpu.VMEM((16, slabs * LANE), BF16),
            pltpu.VMEM((4, scans * SLAB_ROWS, 2 * LANE), BF16),
            pltpu.VMEM((SLAB_ROWS, scans, columns), BF16),
            pltpu.SemaphoreType.DMA((scans // 16,)),
        ],
        compiler_params=PARAMS,
        name="second_half",
    )(
        table["rowscan"],
        table["level"],
        table["column_last"],
        table["level_last"],
        table["two"],
        table["two_column"],
        partial,
        coarse,
        *got_second,
    )


def solution(mesh):
    placed = (P("slab", None, "tile"), P("slab"), P())
    return jax.shard_map(
        body,
        mesh=mesh,
        in_specs=placed,
        out_specs=(P("slab", None, "tile"), P("slab", None, "tile"), P("slab", None, "tile")),
        check_vma=False,
    )
```

time: 40.4 us -> 34.7 us (0.86)
  waiting for transfers between devices: 12.8 us -> 7.23 us
  Pallas kernels: 7.68 us -> 11.3 us
  local copies, waits for them, and re-layouts: 2.42 us -> 0 us
  starting transfers between devices: 16.2 us -> 15.3 us
    ppermute x16, waiting for transfers between devices: 12.8 us -> 7.23 us  [the longest x6 5.79 us: along(): lax.ppermute(chunks[step], 'slab', [(i, i ^ 2 * step) for i in range(slab...]
    pallas_call x3 -> x4, Pallas kernels: 3.29 us -> 7.45 us  [the longest x1 2.98 us: body(): pl.pallas_call(functools.partial(first_half, slabs, scans), out_shape=[ja...]
    unnamed x18 -> x0, local copies, waits for them, and re-layouts: 2.42 us -> none
    ppermute x16, starting transfers between devices: 16.2 us -> 15.3 us  [the longest x6 10.3 us: along(): lax.ppermute(chunks[step], 'slab', [(i, i ^ 2 * step) for i in range(slab...]
    pallas_call x1, Pallas kernels: 4.4 us -> 3.88 us  [body(): pl.pallas_call(functools.partial(second_half, slabs, scans), out_shape=[j...]
  transfers between devices with their start and end apart: 16 -> 16, of which waited for: 6 -> 8; matrix products, arithmetic and copies ran while one was open for 0% -> 0% of each run, Pallas kernels for 5% -> 16%
where the time goes in v2:
time: 34.7 us; the launch traced here: 34.5 us
  starting transfers between devices  15.3 us (44%)
  Pallas kernels  11.3 us (33%)
  waiting for transfers between devices  7.23 us (21%)
  between operations  0.68 us (2%)
    ppermute x6, starting transfers between devices, along(): lax.ppermute(chunks[step], 'slab', [(i, i ^ 2 * step) for i in range(slab...  10.3 us
    ppermute x6, waiting for transfers between devices, along(): lax.ppermute(chunks[step], 'slab', [(i, i ^ 2 * step) for i in range(slab...  5.79 us
    pallas_call x1, Pallas kernels, body(): pl.pallas_call(functools.partial(second_half, slabs, scans), out_shape=[j...  3.88 us
    pallas_call x1, Pallas kernels, body(): pl.pallas_call(functools.partial(first_half, slabs, scans), out_shape=[ja...  2.98 us
    ppermute x2, starting transfers between devices, shifted(): lax.ppermute(block, 'tile', [(i, (i + distance) % count) for i in range(c...  2.92 us
    ppermute x8, starting transfers between devices, within(): lax.ppermute(held[step], 'slab', [(i, i ^ 1) for i in range(slabs)])  2.04 us
    pallas_call x1, Pallas kernels, body(): pl.pallas_call(pack_first, out_shape=[strip, strip, jax.ShapeDtypeStruct(...  1.9 us
    pallas_call x1, Pallas kernels, body(): pl.pallas_call(stage, out_shape=[jax.ShapeDtypeStruct(table[name].shape,...  1.86 us
  transfers between devices with their start and end apart: 16, of which 8 were waited for; matrix products, arithmetic and copies ran while one was open for 0% of the time, Pallas kernels for 16%

profile of v2, /device:TPU:0, one launch (start us, length us, event | category | flops | bytes accessed | tf_op | source)
XLA Modules:
  0.0 34.5 jit_solution(18162697813621958910)
XLA Ops:
  0.6 1.9 %pack_first.1 = (bf16[8,480]{1,0:T(8,128)(2,1)S(1)}, bf16[8,480]{1,0:T(8,128)(2,1)S(1)}, bf16[480,512]{1,0:T(8,128)(2,1)S(1)}, s32[256,128]{1,0:T(8,128)S(1)}, b...) custom-call(bf16[480,512]{1,0:T(8,128)(2,1)} %bitcast.1, ...), custom_call_target="tpu_custom_call" | custom-call | tf_op jit(solution)/shard_map/pack_first/pallas_call | solution.py:335
  2.5 3.1 %collective-permute-start.5 = (bf16[168,384]{1,0:T(8,128)(2,1)S(1)}, bf16[168,384]{1,0:T(8,128)(2,1)S(1)}, u32[]{:S(2)}, u32[]{:S(2)}) collective-permute-start(bf16[168,384]{1,0:T(8,128)(2,1)S(1)} %get-tuple-element.51), channel_id=1, source_target_pairs={{0,2},{1,3},{2,0},{3,1},{4,6},{5,7},{6,4},{7,5},{8,10},{9,11},{10,... | collective-permute-start | bytes 387080 | tf_op jit(solution)/shard_map/ppermute | solution.py:308
  5.6 2.6 %collective-permute-start.6 = (bf16[168,384]{1,0:T(8,128)(2,1)S(1)}, bf16[168,384]{1,0:T(8,128)(2,1)S(1)}, u32[]{:S(2)}, u32[]{:S(2)}) collective-permute-start(bf16[168,384]{1,0:T(8,128)(2,1)S(1)} %get-tuple-element.52), channel_id=1, source_target_pairs={{0,4},{1,5},{2,6},{3,7},{4,0},{5,1},{6,2},{7,3},{8,12},{9,13},{10,... | collective-permute-start | bytes 387080 | tf_op jit(solution)/shard_map/ppermute | solution.py:308
  8.2 1.7 %collective-permute-start = (bf16[8,480]{1,0:T(8,128)(2,1)S(1)}, bf16[8,480]{1,0:T(8,128)(2,1)S(1)}, u32[]{:S(2)}, u32[]{:S(2)}) collective-permute-start(bf16[8,480]{1,0:T(8,128)(2,1)S(1)} %get-tuple-element.43), channel_id=1, source_target_pairs={{0,8},{8,16},{16,24},{24,0},{1,9},{9,17},{17,25},{25,1},{2,10},{10... | collective-permute-start | bytes 23048 | tf_op jit(solution)/shard_map/ppermute | solution.py:321
  9.9 1.2 %collective-permute-start.1 = (bf16[8,480]{1,0:T(8,128)(2,1)S(1)}, bf16[8,480]{1,0:T(8,128)(2,1)S(1)}, u32[]{:S(2)}, u32[]{:S(2)}) collective-permute-start(bf16[8,480]{1,0:T(8,128)(2,1)S(1)} %get-tuple-element.34.order_ref), channel_id=1, source_target_pairs={{0,24},{8,0},{16,8},{24,16},{1,25},{9,1},{17,9},{25,17},{2,26},{10... | collective-permute-start | bytes 23048 | tf_op jit(solution)/shard_map/ppermute | solution.py:321
  11.2 1.9 %stage.1 = (bf16[512,512]{1,0:T(8,128)(2,1)S(1)}, bf16[176,1024]{1,0:T(8,128)(2,1)S(1)}, bf16[4,512,256]{2,1,0:T(8,128)(2,1)S(1)}, bf16[4,256,256]{2,1,0:T(8,128...) custom-call(bf16[8,480]{1,0:T(8,128)(2,1)S(1)} %get-tuple-element.34, ...), custom_call_target="tpu_custom_call" | custom-call | tf_op jit(solution)/shard_map/stage/pallas_call | solution.py:352
  13.0 0.5 %collective-permute-done.1.from_right_ref = bf16[8,480]{1,0:T(8,128)(2,1)S(1)} collective-permute-done((bf16[8,480]{1,0:T(8,128)(2,1)S(1)}, bf16[8,480]{1,0:T(8,128)(2,1)S(1)}, u32[]{:S(2)}, u32[]{:S(2)}) %collective-permute-start.1) | collective-permute-done | bytes 7712 | tf_op jit(solution)/shard_map/ppermute | solution.py:321
  13.6 0.7 %pack_second.1 = (bf16[200,128]{1,0:T(8,128)(2,1)S(1)}, bf16[200,128]{1,0:T(8,128)(2,1)S(1)}, bf16[200,128]{1,0:T(8,128)(2,1)S(1)}, bf16[200,128]{1,0:T(8,128)(2,1)S(1)}) custom-call(bf16[480,512]{1,0:T(8,128)(2,1)S(1)} %get-tuple-element.41.raw_ref, s32[256,128]{1,0:T(8,128)S(1)} %get-tuple-element.42.shift_ref, ...), custom_call_target="tpu_custom_call" | custom-call | tf_op jit(solution)/shard_map/pack_second/pallas_call | solution.py:362
  14.3 4.1 %collective-permute-done.6.refs_4_ = bf16[168,384]{1,0:T(8,128)(2,1)S(1)} collective-permute-done((bf16[168,384]{1,0:T(8,128)(2,1)S(1)}, bf16[168,384]{1,0:T(8,128)(2,1)S(1)}, u32[]{:S(2)}, u32[]{:S(2)}) %collective-permute-start.6) | collective-permute-done | bytes 129056 | tf_op jit(solution)/shard_map/ppermute | solution.py:308
  18.4 0.5 %collective-permute-start.9 = (bf16[168,384]{1,0:T(8,128)(2,1)S(1)}, bf16[168,384]{1,0:T(8,128)(2,1)S(1)}, u32[]{:S(2)}, u32[]{:S(2)}) collective-permute-start(bf16[168,384]{1,0:T(8,128)(2,1)S(1)} %collective-permute-done.5.refs_2_), channel_id=1, source_target_pairs={{0,1},{1,0},{2,3},{3,2},{4,5},{5,4},{6,7},{7,6},{8,9},{9,8},{10,11... | collective-permute-start | bytes 387080 | tf_op jit(solution)/shard_map/ppermute | solution.py:315
  18.9 0.5 %collective-permute-start.11 = (bf16[168,384]{1,0:T(8,128)(2,1)S(1)}, bf16[168,384]{1,0:T(8,128)(2,1)S(1)}, u32[]{:S(2)}, u32[]{:S(2)}) collective-permute-start(bf16[168,384]{1,0:T(8,128)(2,1)S(1)} %collective-permute-done.7.refs_6_), channel_id=1, source_target_pairs={{0,1},{1,0},{2,3},{3,2},{4,5},{5,4},{6,7},{7,6},{8,9},{9,8},{10,11... | collective-permute-start | bytes 387080 | tf_op jit(solution)/shard_map/ppermute | solution.py:315
  19.4 1.9 %collective-permute-start.2 = (bf16[200,128]{1,0:T(8,128)(2,1)S(1)}, bf16[200,128]{1,0:T(8,128)(2,1)S(1)}, u32[]{:S(2)}, u32[]{:S(2)}) collective-permute-start(bf16[200,128]{1,0:T(8,128)(2,1)S(1)} %get-tuple-element.45), channel_id=1, source_target_pairs={{0,2},{1,3},{2,0},{3,1},{4,6},{5,7},{6,4},{7,5},{8,10},{9,11},{10,... | collective-permute-start | bytes 153608 | tf_op jit(solution)/shard_map/ppermute | solution.py:308
  21.4 1.3 %collective-permute-start.3 = (bf16[200,128]{1,0:T(8,128)(2,1)S(1)}, bf16[200,128]{1,0:T(8,128)(2,1)S(1)}, u32[]{:S(2)}, u32[]{:S(2)}) collective-permute-start(bf16[200,128]{1,0:T(8,128)(2,1)S(1)} %get-tuple-element.46), channel_id=1, source_target_pairs={{0,4},{1,5},{2,6},{3,7},{4,0},{5,1},{6,2},{7,3},{8,12},{9,13},{10,... | collective-permute-start | bytes 153608 | tf_op jit(solution)/shard_map/ppermute | solution.py:308
  22.7 1.4 %collective-permute-start.4 = (bf16[200,128]{1,0:T(8,128)(2,1)S(1)}, bf16[200,128]{1,0:T(8,128)(2,1)S(1)}, u32[]{:S(2)}, u32[]{:S(2)}) collective-permute-start(bf16[200,128]{1,0:T(8,128)(2,1)S(1)} %get-tuple-element.47), channel_id=1, source_target_pairs={{0,6},{1,7},{2,4},{3,5},{4,2},{5,3},{6,0},{7,1},{8,14},{9,15},{10,... | collective-permute-start | bytes 153608 | tf_op jit(solution)/shard_map/ppermute | solution.py:308
  24.1 3.0 %first_half.1 = (f32[512,512]{1,0:T(8,128)S(1)}, f32[176,384]{1,0:T(8,128)S(1)}) custom-call(bf16[512,512]{1,0:T(8,128)(2,1)S(1)} %get-tuple-element.35.rowscan_ref, bf16[176,1024]{1,0:T(8,128)(2,1)S(1)} %get-tuple-element.36.level_ref, bf16[4,512,256]{2,1,0:T(8,128)(2,1)S(1)} %get-tuple-element.48.column_ref, ...), custom_call_target="tpu_custom_call" | custom-call | tf_op jit(solution)/shard_map/first_half/pallas_call | solution.py:374
  27.1 0.9 %collective-permute-done.3.refs_6_ = bf16[200,128]{1,0:T(8,128)(2,1)S(1)} collective-permute-done((bf16[200,128]{1,0:T(8,128)(2,1)S(1)}, bf16[200,128]{1,0:T(8,128)(2,1)S(1)}, u32[]{:S(2)}, u32[]{:S(2)}) %collective-permute-start.3) | collective-permute-done | bytes 51232 | tf_op jit(solution)/shard_map/ppermute | solution.py:308
  28.0 0.7 %collective-permute-done.4.refs_8_ = bf16[200,128]{1,0:T(8,128)(2,1)S(1)} collective-permute-done((bf16[200,128]{1,0:T(8,128)(2,1)S(1)}, bf16[200,128]{1,0:T(8,128)(2,1)S(1)}, u32[]{:S(2)}, u32[]{:S(2)}) %collective-permute-start.4) | collective-permute-done | bytes 51232 | tf_op jit(solution)/shard_map/ppermute | solution.py:308
  28.7 0.5 %collective-permute-start.13 = (bf16[200,128]{1,0:T(8,128)(2,1)S(1)}, bf16[200,128]{1,0:T(8,128)(2,1)S(1)}, u32[]{:S(2)}, u32[]{:S(2)}) collective-permute-start(bf16[200,128]{1,0:T(8,128)(2,1)S(1)} %collective-permute-done.2.refs_4_), channel_id=1, source_target_pairs={{0,1},{1,0},{2,3},{3,2},{4,5},{5,4},{6,7},{7,6},{8,9},{9,8},{10,11... | collective-permute-start | bytes 153608 | tf_op jit(solution)/shard_map/ppermute | solution.py:315
  29.2 0.5 %collective-permute-start.15 = (bf16[200,128]{1,0:T(8,128)(2,1)S(1)}, bf16[200,128]{1,0:T(8,128)(2,1)S(1)}, u32[]{:S(2)}, u32[]{:S(2)}) collective-permute-start(bf16[200,128]{1,0:T(8,128)(2,1)S(1)} %collective-permute-done.4.refs_8_), channel_id=1, source_target_pairs={{0,1},{1,0},{2,3},{3,2},{4,5},{5,4},{6,7},{7,6},{8,9},{9,8},{10,11... | collective-permute-start | bytes 153608 | tf_op jit(solution)/shard_map/ppermute | solution.py:315
  29.7 0.2 collective-permute-done.12.refs_3_
  30.0 0.2 collective-permute-done.13.refs_5_
  30.1 0.3 %collective-permute-done.14.refs_7_ = bf16[200,128]{1,0:T(8,128)(2,1)S(1)} collective-permute-done((bf16[200,128]{1,0:T(8,128)(2,1)S(1)}, bf16[200,128]{1,0:T(8,128)(2,1)S(1)}, u32[]{:S(2)}, u32[]{:S(2)}) %collective-permute-start.14) | collective-permute-done | bytes 51232 | tf_op jit(solution)/shard_map/ppermute | solution.py:315
  30.5 0.2 collective-permute-done.15.refs_9_
  30.6 3.9 %second_half.1 = (bf16[16,32,512]{2,1,0:T(8,128)(2,1)}, bf16[8,16,256]{2,1,0:T(8,128)(2,1)}, bf16[4,8,128]{2,1,0:T(8,128)(2,1)}) custom-call(bf16[512,512]{1,0:T(8,128)(2,1)S(1)} %get-tuple-element.35.rowscan_ref, bf16[176,1024]{1,0:T(8,128)(2,1)S(1)} %get-tuple-element.36.level_ref, bf16[4,256,256]{2,1,0:T(8,128)(2,1)S(1)} %get-tuple-element.37.column_ref, ...), custom_call_target="tpu_custom_call" | custom-call | tf_op jit(solution)/shard_map/second_half/pallas_call | solution.py:392
  (13 shorter events, 0.0 us)
Async XLA Ops:
  2.5 11.7 %collective-permute-start.5 = (bf16[168,384]{1,0:T(8,128)(2,1)S(1)}, bf16[168,384]{1,0:T(8,128)(2,1)S(1)}, u32[]{:S(2)}, u32[]{:S(2)}) collective-permute-start(bf16[168,384]{1,0:T(8,128)(2,1)S(1)} %get-tuple-element.51), channel_id=1, source_target_pairs={{0,2},{1,3},{2,0},{3,1},{4,6},{5,7},{6,4},{7,5},{8,10},{9,11},{10,... | collective-permute-start | bytes 387080 | tf_op jit(solution)/shard_map/ppermute | solution.py:308
  5.6 12.8 %collective-permute-start.6 = (bf16[168,384]{1,0:T(8,128)(2,1)S(1)}, bf16[168,384]{1,0:T(8,128)(2,1)S(1)}, u32[]{:S(2)}, u32[]{:S(2)}) collective-permute-start(bf16[168,384]{1,0:T(8,128)(2,1)S(1)} %get-tuple-element.52), channel_id=1, source_target_pairs={{0,4},{1,5},{2,6},{3,7},{4,0},{5,1},{6,2},{7,3},{8,12},{9,13},{10,... | collective-permute-start | bytes 387080 | tf_op jit(solution)/shard_map/ppermute | solution.py:308
  8.2 10.2 %collective-permute-start.7 = (bf16[168,384]{1,0:T(8,128)(2,1)S(1)}, bf16[168,384]{1,0:T(8,128)(2,1)S(1)}, u32[]{:S(2)}, u32[]{:S(2)}) collective-permute-start(bf16[168,384]{1,0:T(8,128)(2,1)S(1)} %get-tuple-element.53), channel_id=1, source_target_pairs={{0,6},{1,7},{2,4},{3,5},{4,2},{5,3},{6,0},{7,1},{8,14},{9,15},{10,... | collective-permute-start | bytes 387080 | tf_op jit(solution)/shard_map/ppermute | solution.py:308
  8.2 4.8 %collective-permute-start = (bf16[8,480]{1,0:T(8,128)(2,1)S(1)}, bf16[8,480]{1,0:T(8,128)(2,1)S(1)}, u32[]{:S(2)}, u32[]{:S(2)}) collective-permute-start(bf16[8,480]{1,0:T(8,128)(2,1)S(1)} %get-tuple-element.43), channel_id=1, source_target_pairs={{0,8},{8,16},{16,24},{24,0},{1,9},{9,17},{17,25},{25,1},{2,10},{10... | collective-permute-start | bytes 23048 | tf_op jit(solution)/shard_map/ppermute | solution.py:321
  9.9 3.7 %collective-permute-start.1 = (bf16[8,480]{1,0:T(8,128)(2,1)S(1)}, bf16[8,480]{1,0:T(8,128)(2,1)S(1)}, u32[]{:S(2)}, u32[]{:S(2)}) collective-permute-start(bf16[8,480]{1,0:T(8,128)(2,1)S(1)} %get-tuple-element.34.order_ref), channel_id=1, source_target_pairs={{0,24},{8,0},{16,8},{24,16},{1,25},{9,1},{17,9},{25,17},{2,26},{10... | collective-permute-start | bytes 23048 | tf_op jit(solution)/shard_map/ppermute | solution.py:321
  18.4 3.0 %collective-permute-start.8 = (bf16[168,384]{1,0:T(8,128)(2,1)S(1)}, bf16[168,384]{1,0:T(8,128)(2,1)S(1)}, u32[]{:S(2)}, u32[]{:S(2)}) collective-permute-start(bf16[168,384]{1,0:T(8,128)(2,1)S(1)} %get-tuple-element.54.refs_0_), channel_id=1, source_target_pairs={{0,1},{1,0},{2,3},{3,2},{4,5},{5,4},{6,7},{7,6},{8,9},{9,8},{10,11... | collective-permute-start | bytes 387080 | tf_op jit(solution)/shard_map/ppermute | solution.py:315
  18.4 4.3 %collective-permute-start.9 = (bf16[168,384]{1,0:T(8,128)(2,1)S(1)}, bf16[168,384]{1,0:T(8,128)(2,1)S(1)}, u32[]{:S(2)}, u32[]{:S(2)}) collective-permute-start(bf16[168,384]{1,0:T(8,128)(2,1)S(1)} %collective-permute-done.5.refs_2_), channel_id=1, source_target_pairs={{0,1},{1,0},{2,3},{3,2},{4,5},{5,4},{6,7},{7,6},{8,9},{9,8},{10,11... | collective-permute-start | bytes 387080 | tf_op jit(solution)/shard_map/ppermute | solution.py:315
  18.9 5.1 %collective-permute-start.10 = (bf16[168,384]{1,0:T(8,128)(2,1)S(1)}, bf16[168,384]{1,0:T(8,128)(2,1)S(1)}, u32[]{:S(2)}, u32[]{:S(2)}) collective-permute-start(bf16[168,384]{1,0:T(8,128)(2,1)S(1)} %collective-permute-done.6.refs_4_), channel_id=1, source_target_pairs={{0,1},{1,0},{2,3},{3,2},{4,5},{5,4},{6,7},{7,6},{8,9},{9,8},{10,11... | collective-permute-start | bytes 387080 | tf_op jit(solution)/shard_map/ppermute | solution.py:315
  18.9 5.1 %collective-permute-start.11 = (bf16[168,384]{1,0:T(8,128)(2,1)S(1)}, bf16[168,384]{1,0:T(8,128)(2,1)S(1)}, u32[]{:S(2)}, u32[]{:S(2)}) collective-permute-start(bf16[168,384]{1,0:T(8,128)(2,1)S(1)} %collective-permute-done.7.refs_6_), channel_id=1, source_target_pairs={{0,1},{1,0},{2,3},{3,2},{4,5},{5,4},{6,7},{7,6},{8,9},{9,8},{10,11... | collective-permute-start | bytes 387080 | tf_op jit(solution)/shard_map/ppermute | solution.py:315
  19.4 7.6 %collective-permute-start.2 = (bf16[200,128]{1,0:T(8,128)(2,1)S(1)}, bf16[200,128]{1,0:T(8,128)(2,1)S(1)}, u32[]{:S(2)}, u32[]{:S(2)}) collective-permute-start(bf16[200,128]{1,0:T(8,128)(2,1)S(1)} %get-tuple-element.45), channel_id=1, source_target_pairs={{0,2},{1,3},{2,0},{3,1},{4,6},{5,7},{6,4},{7,5},{8,10},{9,11},{10,... | collective-permute-start | bytes 153608 | tf_op jit(solution)/shard_map/ppermute | solution.py:308
  21.4 6.6 %collective-permute-start.3 = (bf16[200,128]{1,0:T(8,128)(2,1)S(1)}, bf16[200,128]{1,0:T(8,128)(2,1)S(1)}, u32[]{:S(2)}, u32[]{:S(2)}) collective-permute-start(bf16[200,128]{1,0:T(8,128)(2,1)S(1)} %get-tuple-element.46), channel_id=1, source_target_pairs={{0,4},{1,5},{2,6},{3,7},{4,0},{5,1},{6,2},{7,3},{8,12},{9,13},{10,... | collective-permute-start | bytes 153608 | tf_op jit(solution)/shard_map/ppermute | solution.py:308
  22.7 6.0 %collective-permute-start.4 = (bf16[200,128]{1,0:T(8,128)(2,1)S(1)}, bf16[200,128]{1,0:T(8,128)(2,1)S(1)}, u32[]{:S(2)}, u32[]{:S(2)}) collective-permute-start(bf16[200,128]{1,0:T(8,128)(2,1)S(1)} %get-tuple-element.47), channel_id=1, source_target_pairs={{0,6},{1,7},{2,4},{3,5},{4,2},{5,3},{6,0},{7,1},{8,14},{9,15},{10,... | collective-permute-start | bytes 153608 | tf_op jit(solution)/shard_map/ppermute | solution.py:308
  28.7 1.2 %collective-permute-start.12 = (bf16[200,128]{1,0:T(8,128)(2,1)S(1)}, bf16[200,128]{1,0:T(8,128)(2,1)S(1)}, u32[]{:S(2)}, u32[]{:S(2)}) collective-permute-start(bf16[200,128]{1,0:T(8,128)(2,1)S(1)} %get-tuple-element.61.refs_2_), channel_id=1, source_target_pairs={{0,1},{1,0},{2,3},{3,2},{4,5},{5,4},{6,7},{7,6},{8,9},{9,8},{10,11... | collective-permute-start | bytes 153608 | tf_op jit(solution)/shard_map/ppermute | solution.py:315
  28.7 1.4 %collective-permute-start.13 = (bf16[200,128]{1,0:T(8,128)(2,1)S(1)}, bf16[200,128]{1,0:T(8,128)(2,1)S(1)}, u32[]{:S(2)}, u32[]{:S(2)}) collective-permute-start(bf16[200,128]{1,0:T(8,128)(2,1)S(1)} %collective-permute-done.2.refs_4_), channel_id=1, source_target_pairs={{0,1},{1,0},{2,3},{3,2},{4,5},{5,4},{6,7},{7,6},{8,9},{9,8},{10,11... | collective-permute-start | bytes 153608 | tf_op jit(solution)/shard_map/ppermute | solution.py:315
  29.2 1.2 %collective-permute-start.14 = (bf16[200,128]{1,0:T(8,128)(2,1)S(1)}, bf16[200,128]{1,0:T(8,128)(2,1)S(1)}, u32[]{:S(2)}, u32[]{:S(2)}) collective-permute-start(bf16[200,128]{1,0:T(8,128)(2,1)S(1)} %collective-permute-done.3.refs_6_), channel_id=1, source_target_pairs={{0,1},{1,0},{2,3},{3,2},{4,5},{5,4},{6,7},{7,6},{8,9},{9,8},{10,11... | collective-permute-start | bytes 153608 | tf_op jit(solution)/shard_map/ppermute | solution.py:315
  29.2 1.4 %collective-permute-start.15 = (bf16[200,128]{1,0:T(8,128)(2,1)S(1)}, bf16[200,128]{1,0:T(8,128)(2,1)S(1)}, u32[]{:S(2)}, u32[]{:S(2)}) collective-permute-start(bf16[200,128]{1,0:T(8,128)(2,1)S(1)} %collective-permute-done.4.refs_8_), channel_id=1, source_target_pairs={{0,1},{1,0},{2,3},{3,2},{4,5},{5,4},{6,7},{7,6},{8,9},{9,8},{10,11... | collective-permute-start | bytes 153608 | tf_op jit(solution)/shard_map/ppermute | solution.py:315

commit v3 on v2

--- a/solution.py
+++ b/solution.py
@@ -369,7 +369,7 @@
     )(raw, shift, from_left, from_right, table["two"])
     second_held = along(chunks, slabs)
     first_held[0] = own
-    first_held = lax.optimization_barrier((first_held, chunks))[0]
+    first_held[0] = lax.optimization_barrier((first_held[0], chunks))[0]
     got_first = within(first_held, slabs)
     partial, coarse = pl.pallas_call(
         functools.partial(first_half, slabs, scans),

time: 34.7 us -> 33.7 us (0.971)
  waiting for transfers between devices: 7.23 us -> 6.47 us
    ppermute x6, waiting for transfers between devices: 5.79 us -> 5.03 us  [along(): lax.ppermute(chunks[step], 'slab', [(i, i ^ 2 * step) for i in range(slab...]
  transfers between devices with their start and end apart: 16 -> 16, of which waited for: 8 -> 7; matrix products, arithmetic and copies ran while one was open for 0% -> 0% of each run, Pallas kernels for 16% -> 17%
where the time goes in v3:
time: 33.7 us; the launch traced here: 33.5 us
  starting transfers between devices  15 us (45%)
  Pallas kernels  11.3 us (34%)
  waiting for transfers between devices  6.47 us (19%)
  between operations  0.69 us (2%)
    ppermute x6, starting transfers between devices, along(): lax.ppermute(chunks[step], 'slab', [(i, i ^ 2 * step) for i in range(slab...  10.1 us
    ppermute x6, waiting for transfers between devices, along(): lax.ppermute(chunks[step], 'slab', [(i, i ^ 2 * step) for i in range(slab...  5.03 us
    pallas_call x1, Pallas kernels, body(): pl.pallas_call(functools.partial(second_half, slabs, scans), out_shape=[j...  3.87 us
    pallas_call x1, Pallas kernels, body(): pl.pallas_call(functools.partial(first_half, slabs, scans), out_shape=[ja...  2.98 us
    ppermute x2, starting transfers between devices, shifted(): lax.ppermute(block, 'tile', [(i, (i + distance) % count) for i in range(c...  2.92 us
    ppermute x8, starting transfers between devices, within(): lax.ppermute(held[step], 'slab', [(i, i ^ 1) for i in range(slabs)])  2.04 us
    pallas_call x1, Pallas kernels, body(): pl.pallas_call(pack_first, out_shape=[strip, strip, jax.ShapeDtypeStruct(...  1.9 us
    pallas_call x1, Pallas kernels, body(): pl.pallas_call(stage, out_shape=[jax.ShapeDtypeStruct(table[name].shape,...  1.86 us
  transfers between devices with their start and end apart: 16, of which 7 were waited for; matrix products, arithmetic and copies ran while one was open for 0% of the time, Pallas kernels for 17%

profile of v3, /device:TPU:0, one launch (start us, length us, event | category | flops | bytes accessed | tf_op | source)
XLA Modules:
  0.0 33.5 jit_solution(386373191966609596)
XLA Ops:
  0.6 1.9 %pack_first.1 = (bf16[8,480]{1,0:T(8,128)(2,1)S(1)}, bf16[8,480]{1,0:T(8,128)(2,1)S(1)}, bf16[480,512]{1,0:T(8,128)(2,1)S(1)}, s32[256,128]{1,0:T(8,128)S(1)}, b...) custom-call(bf16[480,512]{1,0:T(8,128)(2,1)} %bitcast.1, ...), custom_call_target="tpu_custom_call" | custom-call | tf_op jit(solution)/shard_map/pack_first/pallas_call | solution.py:335
  2.5 3.1 %collective-permute-start.6 = (bf16[168,384]{1,0:T(8,128)(2,1)S(1)}, bf16[168,384]{1,0:T(8,128)(2,1)S(1)}, u32[]{:S(2)}, u32[]{:S(2)}) collective-permute-start(bf16[168,384]{1,0:T(8,128)(2,1)S(1)} %get-tuple-element.49), channel_id=1, source_target_pairs={{0,2},{1,3},{2,0},{3,1},{4,6},{5,7},{6,4},{7,5},{8,10},{9,11},{10,... | collective-permute-start | bytes 387080 | tf_op jit(solution)/shard_map/ppermute | solution.py:308
  5.6 2.6 %collective-permute-start.8 = (bf16[168,384]{1,0:T(8,128)(2,1)S(1)}, bf16[168,384]{1,0:T(8,128)(2,1)S(1)}, u32[]{:S(2)}, u32[]{:S(2)}) collective-permute-start(bf16[168,384]{1,0:T(8,128)(2,1)S(1)} %get-tuple-element.50), channel_id=1, source_target_pairs={{0,4},{1,5},{2,6},{3,7},{4,0},{5,1},{6,2},{7,3},{8,12},{9,13},{10,... | collective-permute-start | bytes 387080 | tf_op jit(solution)/shard_map/ppermute | solution.py:308
  8.2 1.7 %collective-permute-start = (bf16[8,480]{1,0:T(8,128)(2,1)S(1)}, bf16[8,480]{1,0:T(8,128)(2,1)S(1)}, u32[]{:S(2)}, u32[]{:S(2)}) collective-permute-start(bf16[8,480]{1,0:T(8,128)(2,1)S(1)} %get-tuple-element.40), channel_id=1, source_target_pairs={{0,8},{8,16},{16,24},{24,0},{1,9},{9,17},{17,25},{25,1},{2,10},{10... | collective-permute-start | bytes 23048 | tf_op jit(solution)/shard_map/ppermute | solution.py:321
  9.9 1.2 %collective-permute-start.1 = (bf16[8,480]{1,0:T(8,128)(2,1)S(1)}, bf16[8,480]{1,0:T(8,128)(2,1)S(1)}, u32[]{:S(2)}, u32[]{:S(2)}) collective-permute-start(bf16[8,480]{1,0:T(8,128)(2,1)S(1)} %get-tuple-element.31.order_ref), channel_id=1, source_target_pairs={{0,24},{8,0},{16,8},{24,16},{1,25},{9,1},{17,9},{25,17},{2,26},{10... | collective-permute-start | bytes 23048 | tf_op jit(solution)/shard_map/ppermute | solution.py:321
  11.2 1.9 %stage.1 = (bf16[512,512]{1,0:T(8,128)(2,1)S(1)}, bf16[176,1024]{1,0:T(8,128)(2,1)S(1)}, bf16[4,512,256]{2,1,0:T(8,128)(2,1)S(1)}, bf16[4,256,256]{2,1,0:T(8,128...) custom-call(bf16[8,480]{1,0:T(8,128)(2,1)S(1)} %get-tuple-element.31, ...), custom_call_target="tpu_custom_call" | custom-call | tf_op jit(solution)/shard_map/stage/pallas_call | solution.py:352
  13.0 0.5 %collective-permute-done.1.from_right_ref = bf16[8,480]{1,0:T(8,128)(2,1)S(1)} collective-permute-done((bf16[8,480]{1,0:T(8,128)(2,1)S(1)}, bf16[8,480]{1,0:T(8,128)(2,1)S(1)}, u32[]{:S(2)}, u32[]{:S(2)}) %collective-permute-start.1) | collective-permute-done | bytes 7712 | tf_op jit(solution)/shard_map/ppermute | solution.py:321
  13.6 0.7 %pack_second.1 = (bf16[200,128]{1,0:T(8,128)(2,1)S(1)}, bf16[200,128]{1,0:T(8,128)(2,1)S(1)}, bf16[200,128]{1,0:T(8,128)(2,1)S(1)}, bf16[200,128]{1,0:T(8,128)(2,1)S(1)}) custom-call(bf16[480,512]{1,0:T(8,128)(2,1)S(1)} %get-tuple-element.38.raw_ref, s32[256,128]{1,0:T(8,128)S(1)} %get-tuple-element.39.shift_ref, ...), custom_call_target="tpu_custom_call" | custom-call | tf_op jit(solution)/shard_map/pack_second/pallas_call | solution.py:362
  14.3 0.0 collective-permute-done.6.refs_2_
  14.3 0.5 %collective-permute-start.7 = (bf16[168,384]{1,0:T(8,128)(2,1)S(1)}, bf16[168,384]{1,0:T(8,128)(2,1)S(1)}, u32[]{:S(2)}, u32[]{:S(2)}) collective-permute-start(bf16[168,384]{1,0:T(8,128)(2,1)S(1)} %collective-permute-done.6.refs_2_), channel_id=1, source_target_pairs={{0,1},{1,0},{2,3},{3,2},{4,5},{5,4},{6,7},{7,6},{8,9},{9,8},{10,11... | collective-permute-start | bytes 387080 | tf_op jit(solution)/shard_map/ppermute | solution.py:315
  14.8 3.6 %collective-permute-done.8.refs_4_ = bf16[168,384]{1,0:T(8,128)(2,1)S(1)} collective-permute-done((bf16[168,384]{1,0:T(8,128)(2,1)S(1)}, bf16[168,384]{1,0:T(8,128)(2,1)S(1)}, u32[]{:S(2)}, u32[]{:S(2)}) %collective-permute-start.8) | collective-permute-done | bytes 129056 | tf_op jit(solution)/shard_map/ppermute | solution.py:308
  18.4 0.5 %collective-permute-start.11 = (bf16[168,384]{1,0:T(8,128)(2,1)S(1)}, bf16[168,384]{1,0:T(8,128)(2,1)S(1)}, u32[]{:S(2)}, u32[]{:S(2)}) collective-permute-start(bf16[168,384]{1,0:T(8,128)(2,1)S(1)} %collective-permute-done.10.refs_6_), channel_id=1, source_target_pairs={{0,1},{1,0},{2,3},{3,2},{4,5},{5,4},{6,7},{7,6},{8,9},{9,8},{10,11... | collective-permute-start | bytes 387080 | tf_op jit(solution)/shard_map/ppermute | solution.py:315
  18.9 1.4 %collective-permute-start.2 = (bf16[200,128]{1,0:T(8,128)(2,1)S(1)}, bf16[200,128]{1,0:T(8,128)(2,1)S(1)}, u32[]{:S(2)}, u32[]{:S(2)}) collective-permute-start(bf16[200,128]{1,0:T(8,128)(2,1)S(1)} %get-tuple-element.42), channel_id=1, source_target_pairs={{0,2},{1,3},{2,0},{3,1},{4,6},{5,7},{6,4},{7,5},{8,10},{9,11},{10,... | collective-permute-start | bytes 153608 | tf_op jit(solution)/shard_map/ppermute | solution.py:308
  20.4 1.4 %collective-permute-start.3 = (bf16[200,128]{1,0:T(8,128)(2,1)S(1)}, bf16[200,128]{1,0:T(8,128)(2,1)S(1)}, u32[]{:S(2)}, u32[]{:S(2)}) collective-permute-start(bf16[200,128]{1,0:T(8,128)(2,1)S(1)} %get-tuple-element.43), channel_id=1, source_target_pairs={{0,4},{1,5},{2,6},{3,7},{4,0},{5,1},{6,2},{7,3},{8,12},{9,13},{10,... | collective-permute-start | bytes 153608 | tf_op jit(solution)/shard_map/ppermute | solution.py:308
  21.8 1.5 %collective-permute-start.4 = (bf16[200,128]{1,0:T(8,128)(2,1)S(1)}, bf16[200,128]{1,0:T(8,128)(2,1)S(1)}, u32[]{:S(2)}, u32[]{:S(2)}) collective-permute-start(bf16[200,128]{1,0:T(8,128)(2,1)S(1)} %get-tuple-element.44), channel_id=1, source_target_pairs={{0,6},{1,7},{2,4},{3,5},{4,2},{5,3},{6,0},{7,1},{8,14},{9,15},{10,... | collective-permute-start | bytes 153608 | tf_op jit(solution)/shard_map/ppermute | solution.py:308
  23.3 3.0 %first_half.1 = (f32[512,512]{1,0:T(8,128)S(1)}, f32[176,384]{1,0:T(8,128)S(1)}) custom-call(bf16[512,512]{1,0:T(8,128)(2,1)S(1)} %get-tuple-element.32.rowscan_ref, bf16[176,1024]{1,0:T(8,128)(2,1)S(1)} %get-tuple-element.33.level_ref, bf16[4,512,256]{2,1,0:T(8,128)(2,1)S(1)} %get-tuple-element.45.column_ref, ...), custom_call_target="tpu_custom_call" | custom-call | tf_op jit(solution)/shard_map/first_half/pallas_call | solution.py:374
  26.3 1.4 %collective-permute-done.3.refs_6_ = bf16[200,128]{1,0:T(8,128)(2,1)S(1)} collective-permute-done((bf16[200,128]{1,0:T(8,128)(2,1)S(1)}, bf16[200,128]{1,0:T(8,128)(2,1)S(1)}, u32[]{:S(2)}, u32[]{:S(2)}) %collective-permute-start.3) | collective-permute-done | bytes 51232 | tf_op jit(solution)/shard_map/ppermute | solution.py:308
  27.7 0.5 %collective-permute-start.13 = (bf16[200,128]{1,0:T(8,128)(2,1)S(1)}, bf16[200,128]{1,0:T(8,128)(2,1)S(1)}, u32[]{:S(2)}, u32[]{:S(2)}) collective-permute-start(bf16[200,128]{1,0:T(8,128)(2,1)S(1)} %collective-permute-done.2.refs_4_), channel_id=1, source_target_pairs={{0,1},{1,0},{2,3},{3,2},{4,5},{5,4},{6,7},{7,6},{8,9},{9,8},{10,11... | collective-permute-start | bytes 153608 | tf_op jit(solution)/shard_map/ppermute | solution.py:315
  28.2 0.5 %collective-permute-start.15 = (bf16[200,128]{1,0:T(8,128)(2,1)S(1)}, bf16[200,128]{1,0:T(8,128)(2,1)S(1)}, u32[]{:S(2)}, u32[]{:S(2)}) collective-permute-start(bf16[200,128]{1,0:T(8,128)(2,1)S(1)} %collective-permute-done.4.refs_8_), channel_id=1, source_target_pairs={{0,1},{1,0},{2,3},{3,2},{4,5},{5,4},{6,7},{7,6},{8,9},{9,8},{10,11... | collective-permute-start | bytes 153608 | tf_op jit(solution)/shard_map/ppermute | solution.py:315
  28.8 0.2 collective-permute-done.12.refs_3_
  29.0 0.2 collective-permute-done.13.refs_5_
  29.1 0.3 %collective-permute-done.14.refs_7_ = bf16[200,128]{1,0:T(8,128)(2,1)S(1)} collective-permute-done((bf16[200,128]{1,0:T(8,128)(2,1)S(1)}, bf16[200,128]{1,0:T(8,128)(2,1)S(1)}, u32[]{:S(2)}, u32[]{:S(2)}) %collective-permute-start.14) | collective-permute-done | bytes 51232 | tf_op jit(solution)/shard_map/ppermute | solution.py:315
  29.5 0.2 collective-permute-done.15.refs_9_
  29.6 3.9 %second_half.1 = (bf16[16,32,512]{2,1,0:T(8,128)(2,1)}, bf16[8,16,256]{2,1,0:T(8,128)(2,1)}, bf16[4,8,128]{2,1,0:T(8,128)(2,1)}) custom-call(bf16[512,512]{1,0:T(8,128)(2,1)S(1)} %get-tuple-element.32.rowscan_ref, bf16[176,1024]{1,0:T(8,128)(2,1)S(1)} %get-tuple-element.33.level_ref, bf16[4,256,256]{2,1,0:T(8,128)(2,1)S(1)} %get-tuple-element.34.column_ref, ...), custom_call_target="tpu_custom_call" | custom-call | tf_op jit(solution)/shard_map/second_half/pallas_call | solution.py:392
  (13 shorter events, 0.0 us)
Async XLA Ops:
  2.5 11.8 %collective-permute-start.6 = (bf16[168,384]{1,0:T(8,128)(2,1)S(1)}, bf16[168,384]{1,0:T(8,128)(2,1)S(1)}, u32[]{:S(2)}, u32[]{:S(2)}) collective-permute-start(bf16[168,384]{1,0:T(8,128)(2,1)S(1)} %get-tuple-element.49), channel_id=1, source_target_pairs={{0,2},{1,3},{2,0},{3,1},{4,6},{5,7},{6,4},{7,5},{8,10},{9,11},{10,... | collective-permute-start | bytes 387080 | tf_op jit(solution)/shard_map/ppermute | solution.py:308
  5.6 12.8 %collective-permute-start.8 = (bf16[168,384]{1,0:T(8,128)(2,1)S(1)}, bf16[168,384]{1,0:T(8,128)(2,1)S(1)}, u32[]{:S(2)}, u32[]{:S(2)}) collective-permute-start(bf16[168,384]{1,0:T(8,128)(2,1)S(1)} %get-tuple-element.50), channel_id=1, source_target_pairs={{0,4},{1,5},{2,6},{3,7},{4,0},{5,1},{6,2},{7,3},{8,12},{9,13},{10,... | collective-permute-start | bytes 387080 | tf_op jit(solution)/shard_map/ppermute | solution.py:308
  8.2 10.2 %collective-permute-start.10 = (bf16[168,384]{1,0:T(8,128)(2,1)S(1)}, bf16[168,384]{1,0:T(8,128)(2,1)S(1)}, u32[]{:S(2)}, u32[]{:S(2)}) collective-permute-start(bf16[168,384]{1,0:T(8,128)(2,1)S(1)} %get-tuple-element.51), channel_id=1, source_target_pairs={{0,6},{1,7},{2,4},{3,5},{4,2},{5,3},{6,0},{7,1},{8,14},{9,15},{10,... | collective-permute-start | bytes 387080 | tf_op jit(solution)/shard_map/ppermute | solution.py:308
  8.2 4.8 %collective-permute-start = (bf16[8,480]{1,0:T(8,128)(2,1)S(1)}, bf16[8,480]{1,0:T(8,128)(2,1)S(1)}, u32[]{:S(2)}, u32[]{:S(2)}) collective-permute-start(bf16[8,480]{1,0:T(8,128)(2,1)S(1)} %get-tuple-element.40), channel_id=1, source_target_pairs={{0,8},{8,16},{16,24},{24,0},{1,9},{9,17},{17,25},{25,1},{2,10},{10... | collective-permute-start | bytes 23048 | tf_op jit(solution)/shard_map/ppermute | solution.py:321
  9.9 3.7 %collective-permute-start.1 = (bf16[8,480]{1,0:T(8,128)(2,1)S(1)}, bf16[8,480]{1,0:T(8,128)(2,1)S(1)}, u32[]{:S(2)}, u32[]{:S(2)}) collective-permute-start(bf16[8,480]{1,0:T(8,128)(2,1)S(1)} %get-tuple-element.31.order_ref), channel_id=1, source_target_pairs={{0,24},{8,0},{16,8},{24,16},{1,25},{9,1},{17,9},{25,17},{2,26},{10... | collective-permute-start | bytes 23048 | tf_op jit(solution)/shard_map/ppermute | solution.py:321
  14.3 6.1 %collective-permute-start.5 = (bf16[168,384]{1,0:T(8,128)(2,1)S(1)}, bf16[168,384]{1,0:T(8,128)(2,1)S(1)}, u32[]{:S(2)}, u32[]{:S(2)}) collective-permute-start(bf16[168,384]{1,0:T(8,128)(2,1)S(1)} %get-tuple-element.48.refs_0_), channel_id=1, source_target_pairs={{0,1},{1,0},{2,3},{3,2},{4,5},{5,4},{6,7},{7,6},{8,9},{9,8},{10,11... | collective-permute-start | bytes 387080 | tf_op jit(solution)/shard_map/ppermute | solution.py:315
  14.3 7.5 %collective-permute-start.7 = (bf16[168,384]{1,0:T(8,128)(2,1)S(1)}, bf16[168,384]{1,0:T(8,128)(2,1)S(1)}, u32[]{:S(2)}, u32[]{:S(2)}) collective-permute-start(bf16[168,384]{1,0:T(8,128)(2,1)S(1)} %collective-permute-done.6.refs_2_), channel_id=1, source_target_pairs={{0,1},{1,0},{2,3},{3,2},{4,5},{5,4},{6,7},{7,6},{8,9},{9,8},{10,11... | collective-permute-start | bytes 387080 | tf_op jit(solution)/shard_map/ppermute | solution.py:315
  18.4 4.9 %collective-permute-start.9 = (bf16[168,384]{1,0:T(8,128)(2,1)S(1)}, bf16[168,384]{1,0:T(8,128)(2,1)S(1)}, u32[]{:S(2)}, u32[]{:S(2)}) collective-permute-start(bf16[168,384]{1,0:T(8,128)(2,1)S(1)} %collective-permute-done.8.refs_4_), channel_id=1, source_target_pairs={{0,1},{1,0},{2,3},{3,2},{4,5},{5,4},{6,7},{7,6},{8,9},{9,8},{10,11... | collective-permute-start | bytes 387080 | tf_op jit(solution)/shard_map/ppermute | solution.py:315
  18.4 4.9 %collective-permute-start.11 = (bf16[168,384]{1,0:T(8,128)(2,1)S(1)}, bf16[168,384]{1,0:T(8,128)(2,1)S(1)}, u32[]{:S(2)}, u32[]{:S(2)}) collective-permute-start(bf16[168,384]{1,0:T(8,128)(2,1)S(1)} %collective-permute-done.10.refs_6_), channel_id=1, source_target_pairs={{0,1},{1,0},{2,3},{3,2},{4,5},{5,4},{6,7},{7,6},{8,9},{9,8},{10,11... | collective-permute-start | bytes 387080 | tf_op jit(solution)/shard_map/ppermute | solution.py:315
  18.9 7.4 %collective-permute-start.2 = (bf16[200,128]{1,0:T(8,128)(2,1)S(1)}, bf16[200,128]{1,0:T(8,128)(2,1)S(1)}, u32[]{:S(2)}, u32[]{:S(2)}) collective-permute-start(bf16[200,128]{1,0:T(8,128)(2,1)S(1)} %get-tuple-element.42), channel_id=1, source_target_pairs={{0,2},{1,3},{2,0},{3,1},{4,6},{5,7},{6,4},{7,5},{8,10},{9,11},{10,... | collective-permute-start | bytes 153608 | tf_op jit(solution)/shard_map/ppermute | solution.py:308
  20.4 7.4 %collective-permute-start.3 = (bf16[200,128]{1,0:T(8,128)(2,1)S(1)}, bf16[200,128]{1,0:T(8,128)(2,1)S(1)}, u32[]{:S(2)}, u32[]{:S(2)}) collective-permute-start(bf16[200,128]{1,0:T(8,128)(2,1)S(1)} %get-tuple-element.43), channel_id=1, source_target_pairs={{0,4},{1,5},{2,6},{3,7},{4,0},{5,1},{6,2},{7,3},{8,12},{9,13},{10,... | collective-permute-start | bytes 153608 | tf_op jit(solution)/shard_map/ppermute | solution.py:308
  21.8 5.9 %collective-permute-start.4 = (bf16[200,128]{1,0:T(8,128)(2,1)S(1)}, bf16[200,128]{1,0:T(8,128)(2,1)S(1)}, u32[]{:S(2)}, u32[]{:S(2)}) collective-permute-start(bf16[200,128]{1,0:T(8,128)(2,1)S(1)} %get-tuple-element.44), channel_id=1, source_target_pairs={{0,6},{1,7},{2,4},{3,5},{4,2},{5,3},{6,0},{7,1},{8,14},{9,15},{10,... | collective-permute-start | bytes 153608 | tf_op jit(solution)/shard_map/ppermute | solution.py:308
  27.7 1.2 %collective-permute-start.12 = (bf16[200,128]{1,0:T(8,128)(2,1)S(1)}, bf16[200,128]{1,0:T(8,128)(2,1)S(1)}, u32[]{:S(2)}, u32[]{:S(2)}) collective-permute-start(bf16[200,128]{1,0:T(8,128)(2,1)S(1)} %get-tuple-element.55.refs_2_), channel_id=1, source_target_pairs={{0,1},{1,0},{2,3},{3,2},{4,5},{5,4},{6,7},{7,6},{8,9},{9,8},{10,11... | collective-permute-start | bytes 153608 | tf_op jit(solution)/shard_map/ppermute | solution.py:315
  27.7 1.4 %collective-permute-start.13 = (bf16[200,128]{1,0:T(8,128)(2,1)S(1)}, bf16[200,128]{1,0:T(8,128)(2,1)S(1)}, u32[]{:S(2)}, u32[]{:S(2)}) collective-permute-start(bf16[200,128]{1,0:T(8,128)(2,1)S(1)} %collective-permute-done.2.refs_4_), channel_id=1, source_target_pairs={{0,1},{1,0},{2,3},{3,2},{4,5},{5,4},{6,7},{7,6},{8,9},{9,8},{10,11... | collective-permute-start | bytes 153608 | tf_op jit(solution)/shard_map/ppermute | solution.py:315
  28.2 1.2 %collective-permute-start.14 = (bf16[200,128]{1,0:T(8,128)(2,1)S(1)}, bf16[200,128]{1,0:T(8,128)(2,1)S(1)}, u32[]{:S(2)}, u32[]{:S(2)}) collective-permute-start(bf16[200,128]{1,0:T(8,128)(2,1)S(1)} %collective-permute-done.3.refs_6_), channel_id=1, source_target_pairs={{0,1},{1,0},{2,3},{3,2},{4,5},{5,4},{6,7},{7,6},{8,9},{9,8},{10,11... | collective-permute-start | bytes 153608 | tf_op jit(solution)/shard_map/ppermute | solution.py:315
  28.2 1.4 %collective-permute-start.15 = (bf16[200,128]{1,0:T(8,128)(2,1)S(1)}, bf16[200,128]{1,0:T(8,128)(2,1)S(1)}, u32[]{:S(2)}, u32[]{:S(2)}) collective-permute-start(bf16[200,128]{1,0:T(8,128)(2,1)S(1)} %collective-permute-done.4.refs_8_), channel_id=1, source_target_pairs={{0,1},{1,0},{2,3},{3,2},{4,5},{5,4},{6,7},{7,6},{8,9},{9,8},{10,11... | collective-permute-start | bytes 153608 | tf_op jit(solution)/shard_map/ppermute | solution.py:315

commit v4 on v3

--- a/solution.py
+++ b/solution.py
@@ -15,8 +15,8 @@
 RADIUS = 4
 LOW = 6
 HIGH = 4
-PAIR = 2 * SLAB_ROWS + LOW + HIGH
 NEED = SLAB_ROWS + LOW + HIGH
+SLOTS = 4 * NEED
 LEVEL = 11
 LANE = 128
 F32 = jnp.float32
@@ -103,46 +103,54 @@
     return lax.dot_general(left, right, (((1,), (1,)), ((), ())), preferred_element_type=F32)
 
 
-def place_table(shift, group, camera):
+def place_table(shift, slab, camera):
     slots = shift.shape[0]
     slot = lax.broadcasted_iota(jnp.int32, (slots, 1), 0)
     plane, row = slot & 3, slot >> 2
-    source = group * (2 * SLAB_ROWS) - LOW + row - shift
-    inside = (source >= 0) & (source < camera) & (row < PAIR)
+    source = slab * SLAB_ROWS - LOW + row - shift
+    inside = (source >= 0) & (source < camera) & (row < NEED)
     wanted = jnp.where(inside, plane * camera + source, -1)
     lane = lax.broadcasted_iota(jnp.int32, (slots, 4 * camera), 1)
     return jnp.where(lane == wanted, 1.0, 0.0).astype(BF16)
 
 
-def pack_first(raw_ref, shear_ref, width_ref, right_ref, left_ref, kept_ref, shift_ref, *refs):
-    out_refs, (shears, widths, raw_sem, shear_sem, width_sem) = refs[:-5], refs[-5:]
-    load_raw = pltpu.make_async_copy(raw_ref, kept_ref, raw_sem)
-    load_shear = pltpu.make_async_copy(shear_ref, shears, shear_sem)
-    load_width = pltpu.make_async_copy(width_ref, widths, width_sem)
-    load_raw.start()
-    load_shear.start()
-    load_width.start()
+def pack_first(raw_ref, other_ref, shear_ref, other_shear_ref, width_ref, right_ref, left_ref, kept_ref, shift_ref, *refs):
+    out_refs, (shears, other_shears, widths, sems) = refs[:-4], refs[-4:]
+    loads = [
+        pltpu.make_async_copy(source, target, sems.at[index])
+        for index, (source, target) in enumerate(
+            ((raw_ref, kept_ref), (shear_ref, shears), (other_shear_ref, other_shears), (width_ref, widths))
+        )
+    ]
+    for load in loads:
+        load.start()
     camera = raw_ref.shape[0] // 4
     columns = raw_ref.shape[1]
     tile = lax.axis_index("tile")
     tiles = lax.axis_size("tile")
-    mine = lax.axis_index("slab") >> 1
+    slab = lax.axis_index("slab")
     lane = lax.broadcasted_iota(jnp.int32, (8, columns), 1)
     line = lax.broadcasted_iota(jnp.int32, (8, columns), 0)
-    load_shear.wait()
-    load_width.wait()
+    for load in loads[1:]:
+        load.wait()
     right_width = widths[jnp.minimum(tile, tiles - 2)]
     left_width = widths[jnp.maximum(tile - 1, 0)]
     toward_right = jnp.where((lane == columns - right_width - 8 + line) & (line >= 2), 1.0, 0.0).astype(BF16)
     toward_left = jnp.where((lane == left_width + line) & (line < 6), 1.0, 0.0).astype(BF16)
-    plane = lax.broadcasted_iota(jnp.int32, shift_ref.shape, 0) & 3
-    shift_ref[...] = jnp.where(plane < 2, jnp.where(plane == 0, shears[0], shears[1]), jnp.where(plane == 2, shears[2], shears[3]))
-    load_raw.wait()
+    plane = lax.broadcasted_iota(jnp.int32, shift_ref.shape[1:], 0) & 3
+    for owner, values in enumerate((shears, other_shears)):
+        shift_ref[owner] = jnp.where(
+            plane < 2, jnp.where(plane == 0, values[0], values[1]), jnp.where(plane == 2, values[2], values[3])
+        )
+    loads[0].wait()
     for step, out_ref in enumerate(out_refs):
-        table = place_table(shift_ref[: PAIR * 4, :1], mine ^ step, camera)
-        out_ref[...] = dot(table, kept_ref[:, : columns - LANE]).astype(BF16)
-    right_ref[...] = dot_rows(toward_right, kept_ref[...]).astype(BF16)
-    left_ref[...] = dot_rows(toward_left, kept_ref[...]).astype(BF16)
+        for owner, planes_ref in enumerate((kept_ref, other_ref)):
+            table = place_table(shift_ref[owner, :SLOTS, :1], slab ^ (2 * step), camera)
+            placed = dot(table, planes_ref[:, : columns - LANE])
+            out_ref[owner * SLOTS : (owner + 1) * SLOTS, :] = placed.astype(BF16)
+    for owner, planes_ref in enumerate((kept_ref, other_ref)):
+        right_ref[8 * owner : 8 * owner + 8, :] = dot_rows(toward_right, planes_ref[...]).astype(BF16)
+        left_ref[8 * owner : 8 * owner + 8, :] = dot_rows(toward_left, planes_ref[...]).astype(BF16)
 
 
 def stage(order_ref, *refs):
@@ -155,35 +163,36 @@
         load.wait()
 
 
-def pack_second(raw_ref, shift_ref, from_left_ref, from_right_ref, order_ref, *out_refs):
+def pack_second(raw_ref, other_ref, shift_ref, from_left_ref, from_right_ref, order_ref, *out_refs):
     camera = raw_ref.shape[0] // 4
     columns = raw_ref.shape[1]
-    mine = lax.axis_index("slab") >> 1
+    slab = lax.axis_index("slab")
     tile = lax.axis_index("tile")
     right = jnp.where(tile < lax.axis_size("tile") - 1, from_right_ref[...].astype(F32), 0.0)
     left = jnp.where(tile > 0, from_left_ref[...].astype(F32), 0.0)
-    strips = jnp.concatenate([right, left], 0).astype(BF16)
     for step, out_ref in enumerate(out_refs):
-        table = place_table(shift_ref[:, :1], mine ^ step, camera)
-        out_ref[: PAIR * 4, :] = dot(table[: PAIR * 4], raw_ref[:, columns - LANE :]).astype(BF16)
-        placed = dot_rows(strips, table).astype(BF16)
-        out_ref[PAIR * 4 : PAIR * 4 + 16, :] = placed[:, :LANE]
-        out_ref[PAIR * 4 + 16 :, :] = placed[:, LANE:]
+        for owner, planes_ref in enumerate((raw_ref, other_ref)):
+            table = place_table(shift_ref[owner, :, :1], slab ^ (2 * step), camera)
+            placed = dot(table[:SLOTS], planes_ref[:, columns - LANE :])
+            out_ref[owner * SLOTS : (owner + 1) * SLOTS, :] = placed.astype(BF16)
+            own = slice(8 * owner, 8 * owner + 8)
+            strips = jnp.concatenate([right[own], left[own]], 0).astype(BF16)
+            start = 2 * SLOTS + 16 * owner
+            out_ref[start : start + 16, :] = dot_rows(strips, table).astype(BF16)
 
 
 def collect(in_refs, volume, scans):
     slab = lax.axis_index("slab")
-    core = slab & 1
     lanes = in_refs[0].shape[-1]
     groups = scans // 4
     outside = jnp.zeros((LANE,) + volume.shape[2:], BF16)
     volume[0] = outside
     volume[groups + 1] = outside
-    for index, in_ref in enumerate(in_refs):
+    for index in range(groups):
         group = (slab ^ index) + 1
-        start = pl.multiple_of(core * (SLAB_ROWS * 4), SLAB_ROWS * 4)
-        volume[group, : NEED * 4, :lanes] = in_ref[pl.ds(start, NEED * 4), :]
-        volume[group, NEED * 4 :, :lanes] = jnp.zeros((LANE - NEED * 4, lanes), BF16)
+        start = (index & 1) * SLOTS
+        volume[group, :SLOTS, :lanes] = in_refs[index >> 1][start : start + SLOTS, :]
+        volume[group, SLOTS:, :lanes] = jnp.zeros((LANE - SLOTS, lanes), BF16)
 
 
 def split(value):
@@ -237,16 +246,14 @@
     slabs = lax.axis_size("slab")
     tile = lax.axis_index("tile")
     tiles = lax.axis_size("tile")
-    core = slab & 1
     groups = scans // 4
     columns = partial_ref.shape[1]
     cut = columns - LANE
     collect(in_refs, volume, scans)
-    for index, in_ref in enumerate(in_refs):
+    for index in range(groups):
         place = pl.multiple_of((slab ^ index) * LANE, LANE)
-        both = jnp.concatenate([in_ref[PAIR * 4 : PAIR * 4 + 16, :], in_ref[PAIR * 4 + 16 :, :]], 1).astype(F32)
-        both = jnp.where(core == 0, both[:, :LANE], both[:, SLAB_ROWS * 4 : SLAB_ROWS * 4 + LANE])
-        strips[:, pl.ds(place, LANE)] = both.astype(BF16)
+        start = 2 * SLOTS + 16 * (index & 1)
+        strips[:, pl.ds(place, LANE)] = in_refs[index >> 1][start : start + 16, :]
     line = lax.broadcasted_iota(jnp.int32, (16, LANE), 0)
     lane = lax.broadcasted_iota(jnp.int32, (16, LANE), 1)
     spread = jnp.where(lane == jnp.where(line < 8, line, line + LANE - 16), 1.0, 0.0).astype(BF16)
@@ -303,17 +310,10 @@
 
 
 def along(chunks, slabs):
-    held = {}
+    got = list(chunks)
     for step in sorted(range(1, len(chunks)), key=lambda step: (-(step & -step), step)):
-        held[step] = lax.ppermute(chunks[step], "slab", [(i, i ^ (2 * step)) for i in range(slabs)])
-    return held
-
-
-def within(held, slabs):
-    result = []
-    for step in range(len(held)):
-        result += [held[step], lax.ppermute(held[step], "slab", [(i, i ^ 1) for i in range(slabs)])]
-    return result
+        got[step] = lax.ppermute(chunks[step], "slab", [(i, i ^ (2 * step)) for i in range(slabs)])
+    return got
 
 
 def shifted(block, distance):
@@ -328,26 +328,37 @@
     cut = columns - LANE
     pairs = slabs // 2
     table = {name: jnp.asarray(value) for name, value in tables(scans, columns).items()}
-    outside = [raw_stack.reshape(planes * camera, columns), shear_offsets, intersection_widths]
-    outside = [pltpu.with_memory_space_constraint(each, pltpu.HBM) for each in outside]
-    strip = jax.ShapeDtypeStruct((8, planes * camera), BF16)
-    first = jax.ShapeDtypeStruct((PAIR * planes, cut), BF16)
+    raw = raw_stack.reshape(planes * camera, columns)
+    swap = [(i, i ^ 1) for i in range(slabs)]
+    other = lax.ppermute(raw, "slab", swap)
+    other_shear = lax.ppermute(shear_offsets, "slab", swap)
+    outside = [pltpu.with_memory_space_constraint(each, pltpu.HBM) for each in (raw, shear_offsets, intersection_widths)]
+    strip = jax.ShapeDtypeStruct((16, planes * camera), BF16)
+    first = jax.ShapeDtypeStruct((2 * SLOTS, cut), BF16)
     toward_right, toward_left, raw, shift, *chunks = pl.pallas_call(
         pack_first,
-        out_shape=[strip, strip, jax.ShapeDtypeStruct((planes * camera, columns), BF16), jax.ShapeDtypeStruct((2 * LANE, LANE), jnp.int32)]
+        out_shape=[
+            strip,
+            strip,
+            jax.ShapeDtypeStruct((planes * camera, columns), BF16),
+            jax.ShapeDtypeStruct((2, LANE, LANE), jnp.int32),
+        ]
         + [first] * pairs,
-        in_specs=[OUTSIDE] * 3,
+        in_specs=[OUTSIDE, VECTOR, OUTSIDE, ANYWHERE, OUTSIDE],
         out_specs=[VECTOR] * (4 + pairs),
-        scratch_shapes=[pltpu.SMEM(shear_offsets.shape, jnp.int32), pltpu.SMEM(intersection_widths.shape, jnp.int32)]
-        + [pltpu.SemaphoreType.DMA] * 3,
+        scratch_shapes=[
+            pltpu.SMEM(shear_offsets.shape, jnp.int32),
+            pltpu.SMEM(shear_offsets.shape, jnp.int32),
+            pltpu.SMEM(intersection_widths.shape, jnp.int32),
+            pltpu.SemaphoreType.DMA((4,)),
+        ],
         compiler_params=PARAMS,
         name="pack_first",
-    )(*outside)
-    first_held = along(chunks, slabs)
+    )(outside[0], other, outside[1], other_shear, outside[2])
+    got_first = along(chunks, slabs)
     from_left = shifted(toward_right, 1)
     from_right = shifted(toward_left, -1)
-    own = chunks[0]
-    second = jax.ShapeDtypeStruct((PAIR * planes + 32, LANE), BF16)
+    second = jax.ShapeDtypeStruct((2 * SLOTS + 32, LANE), BF16)
     names = list(table)
     staged = pl.pallas_call(
         stage,
@@ -362,22 +373,20 @@
     chunks = pl.pallas_call(
         pack_second,
         out_shape=[second] * pairs,
-        in_specs=[VECTOR] * 4 + [ANYWHERE],
+        in_specs=[VECTOR] * 5 + [ANYWHERE],
         out_specs=[VECTOR] * pairs,
         compiler_params=PARAMS,
         name="pack_second",
-    )(raw, shift, from_left, from_right, table["two"])
-    second_held = along(chunks, slabs)
-    first_held[0] = own
-    first_held[0] = lax.optimization_barrier((first_held[0], chunks))[0]
-    got_first = within(first_held, slabs)
+    )(raw, other, shift, from_left, from_right, table["two"])
+    chunks, got_first[2] = lax.optimization_barrier((chunks, got_first[2]))
+    got_second = along(chunks, slabs)
     partial, coarse = pl.pallas_call(
-        functools.partial(first_half, slabs, scans),
+        functools.partial(first_half, pairs, scans),
         out_shape=[
             jax.ShapeDtypeStruct((scans * SLAB_ROWS, columns), F32),
             jax.ShapeDtypeStruct((LEVEL * scans // 2, columns // 2 + LANE), F32),
         ],
-        in_specs=[VECTOR] * (4 + slabs),
+        in_specs=[VECTOR] * (4 + pairs),
         out_specs=[VECTOR] * 2,
         scratch_shapes=[
             pltpu.VMEM((slabs + 2, LANE, cut), BF16),
@@ -386,17 +395,15 @@
         compiler_params=PARAMS,
         name="first_half",
     )(table["rowscan"], table["level"], table["column_first"], table["level_first"], *got_first)
-    second_held[0] = chunks[0]
-    second_held, partial = lax.optimization_barrier((second_held, partial))
-    got_second = within(second_held, slabs)
+    got_second, partial = lax.optimization_barrier((got_second, partial))
     return pl.pallas_call(
-        functools.partial(second_half, slabs, scans),
+        functools.partial(second_half, pairs, scans),
         out_shape=[
             jax.ShapeDtypeStruct((SLAB_ROWS, scans, columns), BF16),
             jax.ShapeDtypeStruct((SLAB_ROWS // 2, scans // 2, columns // 2), BF16),
             jax.ShapeDtypeStruct((SLAB_ROWS // 4, scans // 4, columns // 4), BF16),
         ],
-        in_specs=[VECTOR] * (8 + slabs),
+        in_specs=[VECTOR] * (8 + pairs),
         out_specs=[OUTSIDE, VECTOR, VECTOR],
         scratch_shapes=[
             pltpu.VMEM((slabs + 2, LANE, 2 * LANE), BF16),

time: 33.7 us -> 32.3 us (0.958)
  starting transfers between devices: 15 us -> 13.9 us
  waiting for transfers between devices: 6.47 us -> 5.76 us
  Pallas kernels: 11.3 us -> 11.7 us
    ppermute x8 -> x2, starting transfers between devices: 2.04 us -> 0.97 us  [the longest x1 0.52 us: body(): other = lax.ppermute(raw, 'slab', swap)]
    ppermute x6, waiting for transfers between devices: 5.03 us -> 4 us  [along(): lax.ppermute(chunks[step], 'slab', [(i, i ^ 2 * step) for i in range(slab...]
    pallas_call x1, Pallas kernels: 1.9 us -> 2.3 us  [body(): pl.pallas_call(pack_first, out_shape=[strip, strip, jax.ShapeDtypeStruct(...]
    ppermute x8 -> x2, waiting for transfers between devices: 0.89 us -> 1.12 us  [the longest x1 0.91 us: body(): other_shear = lax.ppermute(shear_offsets, 'slab', swap)]
  transfers between devices with their start and end apart: 16 -> 10, of which waited for: 7 -> 5; matrix products, arithmetic and copies ran while one was open for 0% -> 0% of each run, Pallas kernels for 17% -> 17%
where the time goes in v4:
time: 32.3 us; the launch traced here: 32.1 us
  starting transfers between devices  13.9 us (43%)
  Pallas kernels  11.7 us (36%)
  waiting for transfers between devices  5.76 us (18%)
  between operations  0.68 us (2%)
    ppermute x6, starting transfers between devices, along(): lax.ppermute(chunks[step], 'slab', [(i, i ^ 2 * step) for i in range(slab...  9.98 us
    ppermute x6, waiting for transfers between devices, along(): lax.ppermute(chunks[step], 'slab', [(i, i ^ 2 * step) for i in range(slab...  4 us
    pallas_call x1, Pallas kernels, body(): pl.pallas_call(functools.partial(second_half, pairs, scans), out_shape=[j...  3.8 us
    pallas_call x1, Pallas kernels, body(): pl.pallas_call(functools.partial(first_half, pairs, scans), out_shape=[ja...  3 us
    ppermute x2, starting transfers between devices, shifted(): lax.ppermute(block, 'tile', [(i, (i + distance) % count) for i in range(c...  2.92 us
    pallas_call x1, Pallas kernels, body(): pl.pallas_call(pack_first, out_shape=[strip, strip, jax.ShapeDtypeStruct(...  2.3 us
    pallas_call x1, Pallas kernels, body(): pl.pallas_call(stage, out_shape=[jax.ShapeDtypeStruct(table[name].shape,...  1.86 us
    ppermute x1, waiting for transfers between devices, body(): other_shear = lax.ppermute(shear_offsets, 'slab', swap)  0.91 us
  transfers between devices with their start and end apart: 10, of which 5 were waited for; matrix products, arithmetic and copies ran while one was open for 0% of the time, Pallas kernels for 17%

profile of v4, /device:TPU:0, one launch (start us, length us, event | category | flops | bytes accessed | tf_op | source)
XLA Modules:
  0.0 32.1 jit_solution(15856650712898144607)
XLA Ops:
  0.6 0.5 %collective-permute-start = (bf16[480,512]{1,0:T(8,128)(2,1)}, bf16[480,512]{1,0:T(8,128)(2,1)S(1)}, u32[]{:S(2)}, u32[]{:S(2)}) collective-permute-start(bf16[480,512]{1,0:T(8,128)(2,1)} %bitcast.1), channel_id=1, source_target_pairs={{0,1},{1,0},{2,3},{3,2},{4,5},{5,4},{6,7},{7,6},{8,9},{9,8},{10,11... | collective-permute-start | bytes 1474568 | tf_op jit(solution)/shard_map/ppermute | solution.py:333
  1.2 0.1 copy-done
  1.3 0.5 %collective-permute-start.1 = (s32[4]{0:T(128)S(1)}, s32[4]{0:T(128)S(1)}, u32[]{:S(2)}, u32[]{:S(2)}) collective-permute-start(s32[4]{0:T(128)S(1)} %copy-done), channel_id=1, source_target_pairs={{0,1},{1,0},{2,3},{3,2},{4,5},{5,4},{6,7},{7,6},{8,9},{9,8},{10,11... | collective-permute-start | bytes 56 | tf_op jit(solution)/shard_map/ppermute | solution.py:334
  1.7 0.9 %collective-permute-done.1.other_shear_ref = s32[4]{0:T(128)S(1)} collective-permute-done((s32[4]{0:T(128)S(1)}, s32[4]{0:T(128)S(1)}, u32[]{:S(2)}, u32[]{:S(2)}) %collective-permute-start.1) | collective-permute-done | bytes 48 | tf_op jit(solution)/shard_map/ppermute | solution.py:334
  2.6 0.2 collective-permute-done.other_ref
  2.9 2.3 %pack_first.1 = (bf16[16,480]{1,0:T(8,128)(2,1)S(1)}, bf16[16,480]{1,0:T(8,128)(2,1)S(1)}, bf16[480,512]{1,0:T(8,128)(2,1)S(1)}, s32[2,128,128]{2,1,0:T(8,128)S(...) custom-call(bf16[480,512]{1,0:T(8,128)(2,1)} %bitcast.2, ...), custom_call_target="tpu_custom_call" | custom-call | tf_op jit(solution)/shard_map/pack_first/pallas_call | solution.py:338
  5.2 4.0 %collective-permute-start.4 = (bf16[208,384]{1,0:T(8,128)(2,1)S(1)}, bf16[208,384]{1,0:T(8,128)(2,1)S(1)}, u32[]{:S(2)}, u32[]{:S(2)}) collective-permute-start(bf16[208,384]{1,0:T(8,128)(2,1)S(1)} %get-tuple-element.49), channel_id=1, source_target_pairs={{0,4},{1,5},{2,6},{3,7},{4,0},{5,1},{6,2},{7,3},{8,12},{9,13},{10,... | collective-permute-start | bytes 479240 | tf_op jit(solution)/shard_map/ppermute | solution.py:315
  9.2 1.6 %collective-permute-start.8 = (bf16[208,384]{1,0:T(8,128)(2,1)S(1)}, bf16[208,384]{1,0:T(8,128)(2,1)S(1)}, u32[]{:S(2)}, u32[]{:S(2)}) collective-permute-start(bf16[208,384]{1,0:T(8,128)(2,1)S(1)} %get-tuple-element.57), channel_id=1, source_target_pairs={{0,2},{1,3},{2,0},{3,1},{4,6},{5,7},{6,4},{7,5},{8,10},{9,11},{10,... | collective-permute-start | bytes 479240 | tf_op jit(solution)/shard_map/ppermute | solution.py:315
  10.8 0.0 collective-permute-start.9
  10.8 1.7 %collective-permute-start.2 = (bf16[16,480]{1,0:T(8,128)(2,1)S(1)}, bf16[16,480]{1,0:T(8,128)(2,1)S(1)}, u32[]{:S(2)}, u32[]{:S(2)}) collective-permute-start(bf16[16,480]{1,0:T(8,128)(2,1)S(1)} %get-tuple-element.44), channel_id=1, source_target_pairs={{0,8},{8,16},{16,24},{24,0},{1,9},{9,17},{17,25},{25,1},{2,10},{10... | collective-permute-start | bytes 46088 | tf_op jit(solution)/shard_map/ppermute | solution.py:321
  12.5 1.2 %collective-permute-start.3 = (bf16[16,480]{1,0:T(8,128)(2,1)S(1)}, bf16[16,480]{1,0:T(8,128)(2,1)S(1)}, u32[]{:S(2)}, u32[]{:S(2)}) collective-permute-start(bf16[16,480]{1,0:T(8,128)(2,1)S(1)} %get-tuple-element.35.order_ref), channel_id=1, source_target_pairs={{0,24},{8,0},{16,8},{24,16},{1,25},{9,1},{17,9},{25,17},{2,26},{10... | collective-permute-start | bytes 46088 | tf_op jit(solution)/shard_map/ppermute | solution.py:321
  13.7 1.9 %stage.1 = (bf16[512,512]{1,0:T(8,128)(2,1)S(1)}, bf16[176,1024]{1,0:T(8,128)(2,1)S(1)}, bf16[4,512,256]{2,1,0:T(8,128)(2,1)S(1)}, bf16[4,256,256]{2,1,0:T(8,128...) custom-call(bf16[16,480]{1,0:T(8,128)(2,1)S(1)} %get-tuple-element.3, ...), custom_call_target="tpu_custom_call" | custom-call | tf_op jit(solution)/shard_map/stage/pallas_call | solution.py:363
  15.6 0.6 %collective-permute-done.3.from_right_ref = bf16[16,480]{1,0:T(8,128)(2,1)S(1)} collective-permute-done((bf16[16,480]{1,0:T(8,128)(2,1)S(1)}, bf16[16,480]{1,0:T(8,128)(2,1)S(1)}, u32[]{:S(2)}, u32[]{:S(2)}) %collective-permute-start.3) | collective-permute-done | bytes 15392 | tf_op jit(solution)/shard_map/ppermute | solution.py:321
  16.2 0.7 %pack_second.1 = (bf16[240,128]{1,0:T(8,128)(2,1)S(1)}, bf16[240,128]{1,0:T(8,128)(2,1)S(1)}, bf16[240,128]{1,0:T(8,128)(2,1)S(1)}, bf16[240,128]{1,0:T(8,128)(2,1)S(1)}) custom-call(bf16[480,512]{1,0:T(8,128)(2,1)S(1)} %get-tuple-element.42.raw_ref, bf16[480,512]{1,0:T(8,128)(2,1)S(1)} %collective-permute-done.other_ref, ...), custom_call_target="tpu_custom_call" | custom-call | tf_op jit(solution)/shard_map/pack_second/pallas_call | solution.py:373
  16.9 0.8 %collective-permute-done.4.refs_2_ = bf16[208,384]{1,0:T(8,128)(2,1)S(1)} collective-permute-done((bf16[208,384]{1,0:T(8,128)(2,1)S(1)}, bf16[208,384]{1,0:T(8,128)(2,1)S(1)}, u32[]{:S(2)}, u32[]{:S(2)}) %collective-permute-start.4) | collective-permute-done | bytes 159776 | tf_op jit(solution)/shard_map/ppermute | solution.py:315
  17.8 0.6 %collective-permute-start.5 = (bf16[240,128]{1,0:T(8,128)(2,1)S(1)}, bf16[240,128]{1,0:T(8,128)(2,1)S(1)}, u32[]{:S(2)}, u32[]{:S(2)}) collective-permute-start(bf16[240,128]{1,0:T(8,128)(2,1)S(1)} %get-tuple-element.51), channel_id=1, source_target_pairs={{0,2},{1,3},{2,0},{3,1},{4,6},{5,7},{6,4},{7,5},{8,10},{9,11},{10,... | collective-permute-start | bytes 184328 | tf_op jit(solution)/shard_map/ppermute | solution.py:315
  18.4 3.7 %collective-permute-start.6 = (bf16[240,128]{1,0:T(8,128)(2,1)S(1)}, bf16[240,128]{1,0:T(8,128)(2,1)S(1)}, u32[]{:S(2)}, u32[]{:S(2)}) collective-permute-start(bf16[240,128]{1,0:T(8,128)(2,1)S(1)} %get-tuple-element.52), channel_id=1, source_target_pairs={{0,4},{1,5},{2,6},{3,7},{4,0},{5,1},{6,2},{7,3},{8,12},{9,13},{10,... | collective-permute-start | bytes 184328 | tf_op jit(solution)/shard_map/ppermute | solution.py:315
  22.0 0.1 collective-permute-start.7
  22.1 0.0 collective-permute-done.8.refs_1_
  22.1 0.0 collective-permute-done.9.refs_3_
  22.2 3.0 %first_half.1 = (f32[512,512]{1,0:T(8,128)S(1)}, f32[176,384]{1,0:T(8,128)S(1)}) custom-call(bf16[512,512]{1,0:T(8,128)(2,1)S(1)} %get-tuple-element.36.rowscan_ref, bf16[176,1024]{1,0:T(8,128)(2,1)S(1)} %get-tuple-element.37.level_ref, bf16[4,512,256]{2,1,0:T(8,128)(2,1)S(1)} %get-tuple-element.54.column_ref, ...), custom_call_target="tpu_custom_call" | custom-call | tf_op jit(solution)/shard_map/first_half/pallas_call | solution.py:383
  25.2 0.0 collective-permute-done.5.refs_3_
  25.2 3.2 %collective-permute-done.6.refs_4_ = bf16[240,128]{1,0:T(8,128)(2,1)S(1)} collective-permute-done((bf16[240,128]{1,0:T(8,128)(2,1)S(1)}, bf16[240,128]{1,0:T(8,128)(2,1)S(1)}, u32[]{:S(2)}, u32[]{:S(2)}) %collective-permute-start.6) | collective-permute-done | bytes 61472 | tf_op jit(solution)/shard_map/ppermute | solution.py:315
  28.3 3.8 %second_half.1 = (bf16[16,32,512]{2,1,0:T(8,128)(2,1)}, bf16[8,16,256]{2,1,0:T(8,128)(2,1)}, bf16[4,8,128]{2,1,0:T(8,128)(2,1)}) custom-call(bf16[512,512]{1,0:T(8,128)(2,1)S(1)} %get-tuple-element.36.rowscan_ref, bf16[176,1024]{1,0:T(8,128)(2,1)S(1)} %get-tuple-element.37.level_ref, bf16[4,256,256]{2,1,0:T(8,128)(2,1)S(1)} %get-tuple-element.38.column_ref, ...), custom_call_target="tpu_custom_call" | custom-call | tf_op jit(solution)/shard_map/second_half/pallas_call | solution.py:399
  (3 shorter events, 0.0 us)
Async XLA Ops:
  0.6 0.7 %copy-start = (s32[4]{0:T(128)S(1)}, s32[4]{0:T(128)}, u32[]{:S(2)}) copy-start(s32[4]{0:T(128)} %shear_ref.1) | copy-start | bytes 52
  0.6 2.2 %collective-permute-start = (bf16[480,512]{1,0:T(8,128)(2,1)}, bf16[480,512]{1,0:T(8,128)(2,1)S(1)}, u32[]{:S(2)}, u32[]{:S(2)}) collective-permute-start(bf16[480,512]{1,0:T(8,128)(2,1)} %bitcast.1), channel_id=1, source_target_pairs={{0,1},{1,0},{2,3},{3,2},{4,5},{5,4},{6,7},{7,6},{8,9},{9,8},{10,11... | collective-permute-start | bytes 1474568 | tf_op jit(solution)/shard_map/ppermute | solution.py:333
  1.3 1.4 %collective-permute-start.1 = (s32[4]{0:T(128)S(1)}, s32[4]{0:T(128)S(1)}, u32[]{:S(2)}, u32[]{:S(2)}) collective-permute-start(s32[4]{0:T(128)S(1)} %copy-done), channel_id=1, source_target_pairs={{0,1},{1,0},{2,3},{3,2},{4,5},{5,4},{6,7},{7,6},{8,9},{9,8},{10,11... | collective-permute-start | bytes 56 | tf_op jit(solution)/shard_map/ppermute | solution.py:334
  5.2 12.6 %collective-permute-start.4 = (bf16[208,384]{1,0:T(8,128)(2,1)S(1)}, bf16[208,384]{1,0:T(8,128)(2,1)S(1)}, u32[]{:S(2)}, u32[]{:S(2)}) collective-permute-start(bf16[208,384]{1,0:T(8,128)(2,1)S(1)} %get-tuple-element.49), channel_id=1, source_target_pairs={{0,4},{1,5},{2,6},{3,7},{4,0},{5,1},{6,2},{7,3},{8,12},{9,13},{10,... | collective-permute-start | bytes 479240 | tf_op jit(solution)/shard_map/ppermute | solution.py:315
  9.2 13.0 %collective-permute-start.8 = (bf16[208,384]{1,0:T(8,128)(2,1)S(1)}, bf16[208,384]{1,0:T(8,128)(2,1)S(1)}, u32[]{:S(2)}, u32[]{:S(2)}) collective-permute-start(bf16[208,384]{1,0:T(8,128)(2,1)S(1)} %get-tuple-element.57), channel_id=1, source_target_pairs={{0,2},{1,3},{2,0},{3,1},{4,6},{5,7},{6,4},{7,5},{8,10},{9,11},{10,... | collective-permute-start | bytes 479240 | tf_op jit(solution)/shard_map/ppermute | solution.py:315
  10.8 11.4 %collective-permute-start.9 = (bf16[208,384]{1,0:T(8,128)(2,1)S(1)}, bf16[208,384]{1,0:T(8,128)(2,1)S(1)}, u32[]{:S(2)}, u32[]{:S(2)}) collective-permute-start(bf16[208,384]{1,0:T(8,128)(2,1)S(1)} %get-tuple-element.59), channel_id=1, source_target_pairs={{0,6},{1,7},{2,4},{3,5},{4,2},{5,3},{6,0},{7,1},{8,14},{9,15},{10,... | collective-permute-start | bytes 479240 | tf_op jit(solution)/shard_map/ppermute | solution.py:315
  10.8 4.8 %collective-permute-start.2 = (bf16[16,480]{1,0:T(8,128)(2,1)S(1)}, bf16[16,480]{1,0:T(8,128)(2,1)S(1)}, u32[]{:S(2)}, u32[]{:S(2)}) collective-permute-start(bf16[16,480]{1,0:T(8,128)(2,1)S(1)} %get-tuple-element.44), channel_id=1, source_target_pairs={{0,8},{8,16},{16,24},{24,0},{1,9},{9,17},{17,25},{25,1},{2,10},{10... | collective-permute-start | bytes 46088 | tf_op jit(solution)/shard_map/ppermute | solution.py:321
  12.5 3.7 %collective-permute-start.3 = (bf16[16,480]{1,0:T(8,128)(2,1)S(1)}, bf16[16,480]{1,0:T(8,128)(2,1)S(1)}, u32[]{:S(2)}, u32[]{:S(2)}) collective-permute-start(bf16[16,480]{1,0:T(8,128)(2,1)S(1)} %get-tuple-element.35.order_ref), channel_id=1, source_target_pairs={{0,24},{8,0},{16,8},{24,16},{1,25},{9,1},{17,9},{25,17},{2,26},{10... | collective-permute-start | bytes 46088 | tf_op jit(solution)/shard_map/ppermute | solution.py:321
  17.8 7.4 %collective-permute-start.5 = (bf16[240,128]{1,0:T(8,128)(2,1)S(1)}, bf16[240,128]{1,0:T(8,128)(2,1)S(1)}, u32[]{:S(2)}, u32[]{:S(2)}) collective-permute-start(bf16[240,128]{1,0:T(8,128)(2,1)S(1)} %get-tuple-element.51), channel_id=1, source_target_pairs={{0,2},{1,3},{2,0},{3,1},{4,6},{5,7},{6,4},{7,5},{8,10},{9,11},{10,... | collective-permute-start | bytes 184328 | tf_op jit(solution)/shard_map/ppermute | solution.py:315
  18.4 10.0 %collective-permute-start.6 = (bf16[240,128]{1,0:T(8,128)(2,1)S(1)}, bf16[240,128]{1,0:T(8,128)(2,1)S(1)}, u32[]{:S(2)}, u32[]{:S(2)}) collective-permute-start(bf16[240,128]{1,0:T(8,128)(2,1)S(1)} %get-tuple-element.52), channel_id=1, source_target_pairs={{0,4},{1,5},{2,6},{3,7},{4,0},{5,1},{6,2},{7,3},{8,12},{9,13},{10,... | collective-permute-start | bytes 184328 | tf_op jit(solution)/shard_map/ppermute | solution.py:315
  22.0 6.3 %collective-permute-start.7 = (bf16[240,128]{1,0:T(8,128)(2,1)S(1)}, bf16[240,128]{1,0:T(8,128)(2,1)S(1)}, u32[]{:S(2)}, u32[]{:S(2)}) collective-permute-start(bf16[240,128]{1,0:T(8,128)(2,1)S(1)} %get-tuple-element.53), channel_id=1, source_target_pairs={{0,6},{1,7},{2,4},{3,5},{4,2},{5,3},{6,0},{7,1},{8,14},{9,15},{10,... | collective-permute-start | bytes 184328 | tf_op jit(solution)/shard_map/ppermute | solution.py:315

commit v5 on v4

--- a/solution.py
+++ b/solution.py
@@ -241,7 +241,7 @@
 
 def second_half(count, scans, rowscan_ref, level_ref, column_ref, level_column_ref, two_ref, two_column_ref, *refs):
     partial_ref, coarse_ref, *in_refs = refs[: 2 + count]
-    difference_ref, one_ref, second_ref, volume, strips, wide, held, sems = refs[2 + count :]
+    difference_ref, one_ref, second_ref, volume, strips, wide, held, held_one, held_second, sems = refs[2 + count :]
     slab = lax.axis_index("slab")
     slabs = lax.axis_size("slab")
     tile = lax.axis_index("tile")
@@ -259,20 +259,6 @@
     spread = jnp.where(lane == jnp.where(line < 8, line, line + LANE - 16), 1.0, 0.0).astype(BF16)
     rim = lax.dot_general(strips[...], spread, (((0,), (0,)), ((), ())), preferred_element_type=F32)
     volume[1 : groups + 1, :, LANE:] = rim.astype(BF16).reshape(groups, LANE, LANE)
-
-    level = coarse_ref[...] + level_part(level_ref, level_column_ref, volume, scans)
-    half = columns // 2
-    shape = (LEVEL, scans // 2, level.shape[-1])
-    level = level.reshape(shape)
-    row = slab * (SLAB_ROWS // 2) - 2 + lax.broadcasted_iota(jnp.int32, shape, 0)
-    place = lax.broadcasted_iota(jnp.int32, shape, 2) - half
-    keep = (row >= 0) & (row < slabs * (SLAB_ROWS // 2))
-    keep = keep & ((place < 0) | (place >= 2) | (tile > 0)) & ((place < 2) | (tile < tiles - 1))
-    ready = jnp.where(keep, level, 0.0).astype(BF16)
-    one_ref[...] = ready[2:10, :, :half]
-    high, low = split(dot(two_ref[...], ready.reshape(LEVEL * scans // 2, level.shape[-1])))
-    second = dot(high, two_column_ref[...]) + dot(low, two_column_ref[...])
-    second_ref[...] = second.reshape(second_ref.shape).astype(BF16)
 
     copies = []
     rows = 8 * SLAB_ROWS
@@ -299,6 +285,27 @@
         )
         copy.start()
         copies.append(copy)
+    level = coarse_ref[...] + level_part(level_ref, level_column_ref, volume, scans)
+    half = columns // 2
+    shape = (LEVEL, scans // 2, level.shape[-1])
+    level = level.reshape(shape)
+    row = slab * (SLAB_ROWS // 2) - 2 + lax.broadcasted_iota(jnp.int32, shape, 0)
+    place = lax.broadcasted_iota(jnp.int32, shape, 2) - half
+    keep = (row >= 0) & (row < slabs * (SLAB_ROWS // 2))
+    keep = keep & ((place < 0) | (place >= 2) | (tile > 0)) & ((place < 2) | (tile < tiles - 1))
+    ready = jnp.where(keep, level, 0.0).astype(BF16)
+    held_one[...] = ready[2:10, :, :half]
+    copy = pltpu.make_async_copy(held_one, one_ref, sems.at[scans // 16])
+    copy.start()
+    copies.append(copy)
+
+    high, low = split(dot(two_ref[...], ready.reshape(LEVEL * scans // 2, level.shape[-1])))
+    second = dot(high, two_column_ref[...]) + dot(low, two_column_ref[...])
+    held_second[...] = second.reshape(second_ref.shape).astype(BF16)
+    copy = pltpu.make_async_copy(held_second, second_ref, sems.at[scans // 16 + 1])
+    copy.start()
+    copies.append(copy)
+
     for copy in copies:
         copy.wait()
 
@@ -404,13 +411,15 @@
             jax.ShapeDtypeStruct((SLAB_ROWS // 4, scans // 4, columns // 4), BF16),
         ],
         in_specs=[VECTOR] * (8 + pairs),
-        out_specs=[OUTSIDE, VECTOR, VECTOR],
+        out_specs=[OUTSIDE] * 3,
         scratch_shapes=[
             pltpu.VMEM((slabs + 2, LANE, 2 * LANE), BF16),
             pltpu.VMEM((16, slabs * LANE), BF16),
             pltpu.VMEM((4, scans * SLAB_ROWS, 2 * LANE), BF16),
             pltpu.VMEM((SLAB_ROWS, scans, columns), BF16),
-            pltpu.SemaphoreType.DMA((scans // 16,)),
+            pltpu.VMEM((SLAB_ROWS // 2, scans // 2, columns // 2), BF16),
+            pltpu.VMEM((SLAB_ROWS // 4, scans // 4, columns // 4), BF16),
+            pltpu.SemaphoreType.DMA((scans // 16 + 2,)),
         ],
         compiler_params=PARAMS,
         name="second_half",

time: 32.3 us -> 31.2 us (0.966)
  Pallas kernels: 11.7 us -> 10.6 us
    pallas_call x1, Pallas kernels: 3.8 us -> 2.67 us  [body(): pl.pallas_call(functools.partial(second_half, pairs, scans), out_shape=[j...]
  transfers between devices with their start and end apart: 10 -> 10, of which waited for: 5 -> 5; matrix products, arithmetic and copies ran while one was open for 0% -> 0% of each run, Pallas kernels for 17% -> 18%
where the time goes in v5:
time: 31.2 us; the launch traced here: 31 us
  starting transfers between devices  13.9 us (45%)
  Pallas kernels  10.6 us (34%)
  waiting for transfers between devices  5.76 us (18%)
  between operations  0.68 us (2%)
    ppermute x6, starting transfers between devices, along(): lax.ppermute(chunks[step], 'slab', [(i, i ^ 2 * step) for i in range(slab...  9.98 us
    ppermute x6, waiting for transfers between devices, along(): lax.ppermute(chunks[step], 'slab', [(i, i ^ 2 * step) for i in range(slab...  4 us
    pallas_call x1, Pallas kernels, body(): pl.pallas_call(functools.partial(first_half, pairs, scans), out_shape=[ja...  3 us
    ppermute x2, starting transfers between devices, shifted(): lax.ppermute(block, 'tile', [(i, (i + distance) % count) for i in range(c...  2.92 us
    pallas_call x1, Pallas kernels, body(): pl.pallas_call(functools.partial(second_half, pairs, scans), out_shape=[j...  2.67 us
    pallas_call x1, Pallas kernels, body(): pl.pallas_call(pack_first, out_shape=[strip, strip, jax.ShapeDtypeStruct(...  2.3 us
    pallas_call x1, Pallas kernels, body(): pl.pallas_call(stage, out_shape=[jax.ShapeDtypeStruct(table[name].shape,...  1.86 us
    ppermute x1, waiting for transfers between devices, body(): other_shear = lax.ppermute(shear_offsets, 'slab', swap)  0.91 us
  transfers between devices with their start and end apart: 10, of which 5 were waited for; matrix products, arithmetic and copies ran while one was open for 0% of the time, Pallas kernels for 18%

profile of v5, /device:TPU:0, one launch (start us, length us, event | category | flops | bytes accessed | tf_op | source)
XLA Modules:
  0.0 31.0 jit_solution(15313688126160707724)
XLA Ops:
  0.6 0.5 %collective-permute-start = (bf16[480,512]{1,0:T(8,128)(2,1)}, bf16[480,512]{1,0:T(8,128)(2,1)S(1)}, u32[]{:S(2)}, u32[]{:S(2)}) collective-permute-start(bf16[480,512]{1,0:T(8,128)(2,1)} %bitcast.1), channel_id=1, source_target_pairs={{0,1},{1,0},{2,3},{3,2},{4,5},{5,4},{6,7},{7,6},{8,9},{9,8},{10,11... | collective-permute-start | bytes 1474568 | tf_op jit(solution)/shard_map/ppermute | solution.py:340
  1.2 0.1 copy-done
  1.3 0.5 %collective-permute-start.1 = (s32[4]{0:T(128)S(1)}, s32[4]{0:T(128)S(1)}, u32[]{:S(2)}, u32[]{:S(2)}) collective-permute-start(s32[4]{0:T(128)S(1)} %copy-done), channel_id=1, source_target_pairs={{0,1},{1,0},{2,3},{3,2},{4,5},{5,4},{6,7},{7,6},{8,9},{9,8},{10,11... | collective-permute-start | bytes 56 | tf_op jit(solution)/shard_map/ppermute | solution.py:341
  1.7 0.9 %collective-permute-done.1.other_shear_ref = s32[4]{0:T(128)S(1)} collective-permute-done((s32[4]{0:T(128)S(1)}, s32[4]{0:T(128)S(1)}, u32[]{:S(2)}, u32[]{:S(2)}) %collective-permute-start.1) | collective-permute-done | bytes 48 | tf_op jit(solution)/shard_map/ppermute | solution.py:341
  2.6 0.2 collective-permute-done.other_ref
  2.9 2.3 %pack_first.1 = (bf16[16,480]{1,0:T(8,128)(2,1)S(1)}, bf16[16,480]{1,0:T(8,128)(2,1)S(1)}, bf16[480,512]{1,0:T(8,128)(2,1)S(1)}, s32[2,128,128]{2,1,0:T(8,128)S(...) custom-call(bf16[480,512]{1,0:T(8,128)(2,1)} %bitcast.2, ...), custom_call_target="tpu_custom_call" | custom-call | tf_op jit(solution)/shard_map/pack_first/pallas_call | solution.py:345
  5.2 4.0 %collective-permute-start.4 = (bf16[208,384]{1,0:T(8,128)(2,1)S(1)}, bf16[208,384]{1,0:T(8,128)(2,1)S(1)}, u32[]{:S(2)}, u32[]{:S(2)}) collective-permute-start(bf16[208,384]{1,0:T(8,128)(2,1)S(1)} %get-tuple-element.49), channel_id=1, source_target_pairs={{0,4},{1,5},{2,6},{3,7},{4,0},{5,1},{6,2},{7,3},{8,12},{9,13},{10,... | collective-permute-start | bytes 479240 | tf_op jit(solution)/shard_map/ppermute | solution.py:322
  9.2 1.6 %collective-permute-start.8 = (bf16[208,384]{1,0:T(8,128)(2,1)S(1)}, bf16[208,384]{1,0:T(8,128)(2,1)S(1)}, u32[]{:S(2)}, u32[]{:S(2)}) collective-permute-start(bf16[208,384]{1,0:T(8,128)(2,1)S(1)} %get-tuple-element.57), channel_id=1, source_target_pairs={{0,2},{1,3},{2,0},{3,1},{4,6},{5,7},{6,4},{7,5},{8,10},{9,11},{10,... | collective-permute-start | bytes 479240 | tf_op jit(solution)/shard_map/ppermute | solution.py:322
  10.8 1.7 %collective-permute-start.2 = (bf16[16,480]{1,0:T(8,128)(2,1)S(1)}, bf16[16,480]{1,0:T(8,128)(2,1)S(1)}, u32[]{:S(2)}, u32[]{:S(2)}) collective-permute-start(bf16[16,480]{1,0:T(8,128)(2,1)S(1)} %get-tuple-element.44), channel_id=1, source_target_pairs={{0,8},{8,16},{16,24},{24,0},{1,9},{9,17},{17,25},{25,1},{2,10},{10... | collective-permute-start | bytes 46088 | tf_op jit(solution)/shard_map/ppermute | solution.py:328
  12.5 1.2 %collective-permute-start.3 = (bf16[16,480]{1,0:T(8,128)(2,1)S(1)}, bf16[16,480]{1,0:T(8,128)(2,1)S(1)}, u32[]{:S(2)}, u32[]{:S(2)}) collective-permute-start(bf16[16,480]{1,0:T(8,128)(2,1)S(1)} %get-tuple-element.35.order_ref), channel_id=1, source_target_pairs={{0,24},{8,0},{16,8},{24,16},{1,25},{9,1},{17,9},{25,17},{2,26},{10... | collective-permute-start | bytes 46088 | tf_op jit(solution)/shard_map/ppermute | solution.py:328
  13.7 1.9 %stage.1 = (bf16[512,512]{1,0:T(8,128)(2,1)S(1)}, bf16[176,1024]{1,0:T(8,128)(2,1)S(1)}, bf16[4,512,256]{2,1,0:T(8,128)(2,1)S(1)}, bf16[4,256,256]{2,1,0:T(8,128...) custom-call(bf16[16,480]{1,0:T(8,128)(2,1)S(1)} %get-tuple-element.3, ...), custom_call_target="tpu_custom_call" | custom-call | tf_op jit(solution)/shard_map/stage/pallas_call | solution.py:370
  15.6 0.0 collective-permute-done.2.from_left_ref
  15.6 0.6 %collective-permute-done.3.from_right_ref = bf16[16,480]{1,0:T(8,128)(2,1)S(1)} collective-permute-done((bf16[16,480]{1,0:T(8,128)(2,1)S(1)}, bf16[16,480]{1,0:T(8,128)(2,1)S(1)}, u32[]{:S(2)}, u32[]{:S(2)}) %collective-permute-start.3) | collective-permute-done | bytes 15392 | tf_op jit(solution)/shard_map/ppermute | solution.py:328
  16.2 0.7 %pack_second.1 = (bf16[240,128]{1,0:T(8,128)(2,1)S(1)}, bf16[240,128]{1,0:T(8,128)(2,1)S(1)}, bf16[240,128]{1,0:T(8,128)(2,1)S(1)}, bf16[240,128]{1,0:T(8,128)(2,1)S(1)}) custom-call(bf16[480,512]{1,0:T(8,128)(2,1)S(1)} %get-tuple-element.42.raw_ref, bf16[480,512]{1,0:T(8,128)(2,1)S(1)} %collective-permute-done.other_ref, ...), custom_call_target="tpu_custom_call" | custom-call | tf_op jit(solution)/shard_map/pack_second/pallas_call | solution.py:380
  16.9 0.8 %collective-permute-done.4.refs_2_ = bf16[208,384]{1,0:T(8,128)(2,1)S(1)} collective-permute-done((bf16[208,384]{1,0:T(8,128)(2,1)S(1)}, bf16[208,384]{1,0:T(8,128)(2,1)S(1)}, u32[]{:S(2)}, u32[]{:S(2)}) %collective-permute-start.4) | collective-permute-done | bytes 159776 | tf_op jit(solution)/shard_map/ppermute | solution.py:322
  17.8 0.6 %collective-permute-start.5 = (bf16[240,128]{1,0:T(8,128)(2,1)S(1)}, bf16[240,128]{1,0:T(8,128)(2,1)S(1)}, u32[]{:S(2)}, u32[]{:S(2)}) collective-permute-start(bf16[240,128]{1,0:T(8,128)(2,1)S(1)} %get-tuple-element.51), channel_id=1, source_target_pairs={{0,2},{1,3},{2,0},{3,1},{4,6},{5,7},{6,4},{7,5},{8,10},{9,11},{10,... | collective-permute-start | bytes 184328 | tf_op jit(solution)/shard_map/ppermute | solution.py:322
  18.4 3.7 %collective-permute-start.6 = (bf16[240,128]{1,0:T(8,128)(2,1)S(1)}, bf16[240,128]{1,0:T(8,128)(2,1)S(1)}, u32[]{:S(2)}, u32[]{:S(2)}) collective-permute-start(bf16[240,128]{1,0:T(8,128)(2,1)S(1)} %get-tuple-element.52), channel_id=1, source_target_pairs={{0,4},{1,5},{2,6},{3,7},{4,0},{5,1},{6,2},{7,3},{8,12},{9,13},{10,... | collective-permute-start | bytes 184328 | tf_op jit(solution)/shard_map/ppermute | solution.py:322
  22.0 0.1 collective-permute-start.7
  22.1 0.0 collective-permute-done.8.refs_1_
  22.1 0.0 collective-permute-done.9.refs_3_
  22.2 3.0 %first_half.1 = (f32[512,512]{1,0:T(8,128)S(1)}, f32[176,384]{1,0:T(8,128)S(1)}) custom-call(bf16[512,512]{1,0:T(8,128)(2,1)S(1)} %get-tuple-element.36.rowscan_ref, bf16[176,1024]{1,0:T(8,128)(2,1)S(1)} %get-tuple-element.37.level_ref, bf16[4,512,256]{2,1,0:T(8,128)(2,1)S(1)} %get-tuple-element.54.column_ref, ...), custom_call_target="tpu_custom_call" | custom-call | tf_op jit(solution)/shard_map/first_half/pallas_call | solution.py:390
  25.2 3.2 %collective-permute-done.6.refs_4_ = bf16[240,128]{1,0:T(8,128)(2,1)S(1)} collective-permute-done((bf16[240,128]{1,0:T(8,128)(2,1)S(1)}, bf16[240,128]{1,0:T(8,128)(2,1)S(1)}, u32[]{:S(2)}, u32[]{:S(2)}) %collective-permute-start.6) | collective-permute-done | bytes 61472 | tf_op jit(solution)/shard_map/ppermute | solution.py:322
  28.3 0.0 collective-permute-done.7.refs_5_
  28.3 2.7 %second_half.1 = (bf16[16,32,512]{2,1,0:T(8,128)(2,1)}, bf16[8,16,256]{2,1,0:T(8,128)(2,1)}, bf16[4,8,128]{2,1,0:T(8,128)(2,1)}) custom-call(bf16[512,512]{1,0:T(8,128)(2,1)S(1)} %get-tuple-element.36.rowscan_ref, bf16[176,1024]{1,0:T(8,128)(2,1)S(1)} %get-tuple-element.37.level_ref, bf16[4,256,256]{2,1,0:T(8,128)(2,1)S(1)} %get-tuple-element.38.column_ref, ...), custom_call_target="tpu_custom_call" | custom-call | tf_op jit(solution)/shard_map/second_half/pallas_call | solution.py:406
  (3 shorter events, 0.0 us)
Async XLA Ops:
  0.6 0.7 %copy-start = (s32[4]{0:T(128)S(1)}, s32[4]{0:T(128)}, u32[]{:S(2)}) copy-start(s32[4]{0:T(128)} %shear_ref.1) | copy-start | bytes 52
  0.6 2.2 %collective-permute-start = (bf16[480,512]{1,0:T(8,128)(2,1)}, bf16[480,512]{1,0:T(8,128)(2,1)S(1)}, u32[]{:S(2)}, u32[]{:S(2)}) collective-permute-start(bf16[480,512]{1,0:T(8,128)(2,1)} %bitcast.1), channel_id=1, source_target_pairs={{0,1},{1,0},{2,3},{3,2},{4,5},{5,4},{6,7},{7,6},{8,9},{9,8},{10,11... | collective-permute-start | bytes 1474568 | tf_op jit(solution)/shard_map/ppermute | solution.py:340
  1.3 1.4 %collective-permute-start.1 = (s32[4]{0:T(128)S(1)}, s32[4]{0:T(128)S(1)}, u32[]{:S(2)}, u32[]{:S(2)}) collective-permute-start(s32[4]{0:T(128)S(1)} %copy-done), channel_id=1, source_target_pairs={{0,1},{1,0},{2,3},{3,2},{4,5},{5,4},{6,7},{7,6},{8,9},{9,8},{10,11... | collective-permute-start | bytes 56 | tf_op jit(solution)/shard_map/ppermute | solution.py:341
  5.2 12.6 %collective-permute-start.4 = (bf16[208,384]{1,0:T(8,128)(2,1)S(1)}, bf16[208,384]{1,0:T(8,128)(2,1)S(1)}, u32[]{:S(2)}, u32[]{:S(2)}) collective-permute-start(bf16[208,384]{1,0:T(8,128)(2,1)S(1)} %get-tuple-element.49), channel_id=1, source_target_pairs={{0,4},{1,5},{2,6},{3,7},{4,0},{5,1},{6,2},{7,3},{8,12},{9,13},{10,... | collective-permute-start | bytes 479240 | tf_op jit(solution)/shard_map/ppermute | solution.py:322
  9.2 13.0 %collective-permute-start.8 = (bf16[208,384]{1,0:T(8,128)(2,1)S(1)}, bf16[208,384]{1,0:T(8,128)(2,1)S(1)}, u32[]{:S(2)}, u32[]{:S(2)}) collective-permute-start(bf16[208,384]{1,0:T(8,128)(2,1)S(1)} %get-tuple-element.57), channel_id=1, source_target_pairs={{0,2},{1,3},{2,0},{3,1},{4,6},{5,7},{6,4},{7,5},{8,10},{9,11},{10,... | collective-permute-start | bytes 479240 | tf_op jit(solution)/shard_map/ppermute | solution.py:322
  10.8 11.4 %collective-permute-start.9 = (bf16[208,384]{1,0:T(8,128)(2,1)S(1)}, bf16[208,384]{1,0:T(8,128)(2,1)S(1)}, u32[]{:S(2)}, u32[]{:S(2)}) collective-permute-start(bf16[208,384]{1,0:T(8,128)(2,1)S(1)} %get-tuple-element.59), channel_id=1, source_target_pairs={{0,6},{1,7},{2,4},{3,5},{4,2},{5,3},{6,0},{7,1},{8,14},{9,15},{10,... | collective-permute-start | bytes 479240 | tf_op jit(solution)/shard_map/ppermute | solution.py:322
  10.8 4.8 %collective-permute-start.2 = (bf16[16,480]{1,0:T(8,128)(2,1)S(1)}, bf16[16,480]{1,0:T(8,128)(2,1)S(1)}, u32[]{:S(2)}, u32[]{:S(2)}) collective-permute-start(bf16[16,480]{1,0:T(8,128)(2,1)S(1)} %get-tuple-element.44), channel_id=1, source_target_pairs={{0,8},{8,16},{16,24},{24,0},{1,9},{9,17},{17,25},{25,1},{2,10},{10... | collective-permute-start | bytes 46088 | tf_op jit(solution)/shard_map/ppermute | solution.py:328
  12.5 3.7 %collective-permute-start.3 = (bf16[16,480]{1,0:T(8,128)(2,1)S(1)}, bf16[16,480]{1,0:T(8,128)(2,1)S(1)}, u32[]{:S(2)}, u32[]{:S(2)}) collective-permute-start(bf16[16,480]{1,0:T(8,128)(2,1)S(1)} %get-tuple-element.35.order_ref), channel_id=1, source_target_pairs={{0,24},{8,0},{16,8},{24,16},{1,25},{9,1},{17,9},{25,17},{2,26},{10... | collective-permute-start | bytes 46088 | tf_op jit(solution)/shard_map/ppermute | solution.py:328
  17.8 7.4 %collective-permute-start.5 = (bf16[240,128]{1,0:T(8,128)(2,1)S(1)}, bf16[240,128]{1,0:T(8,128)(2,1)S(1)}, u32[]{:S(2)}, u32[]{:S(2)}) collective-permute-start(bf16[240,128]{1,0:T(8,128)(2,1)S(1)} %get-tuple-element.51), channel_id=1, source_target_pairs={{0,2},{1,3},{2,0},{3,1},{4,6},{5,7},{6,4},{7,5},{8,10},{9,11},{10,... | collective-permute-start | bytes 184328 | tf_op jit(solution)/shard_map/ppermute | solution.py:322
  18.4 10.0 %collective-permute-start.6 = (bf16[240,128]{1,0:T(8,128)(2,1)S(1)}, bf16[240,128]{1,0:T(8,128)(2,1)S(1)}, u32[]{:S(2)}, u32[]{:S(2)}) collective-permute-start(bf16[240,128]{1,0:T(8,128)(2,1)S(1)} %get-tuple-element.52), channel_id=1, source_target_pairs={{0,4},{1,5},{2,6},{3,7},{4,0},{5,1},{6,2},{7,3},{8,12},{9,13},{10,... | collective-permute-start | bytes 184328 | tf_op jit(solution)/shard_map/ppermute | solution.py:322
  22.0 6.3 %collective-permute-start.7 = (bf16[240,128]{1,0:T(8,128)(2,1)S(1)}, bf16[240,128]{1,0:T(8,128)(2,1)S(1)}, u32[]{:S(2)}, u32[]{:S(2)}) collective-permute-start(bf16[240,128]{1,0:T(8,128)(2,1)S(1)} %get-tuple-element.53), channel_id=1, source_target_pairs={{0,6},{1,7},{2,4},{3,5},{4,2},{5,3},{6,0},{7,1},{8,14},{9,15},{10,... | collective-permute-start | bytes 184328 | tf_op jit(solution)/shard_map/ppermute | solution.py:322

commit v6 on v5

--- a/solution.py
+++ b/solution.py
@@ -114,43 +114,64 @@
     return jnp.where(lane == wanted, 1.0, 0.0).astype(BF16)
 
 
-def pack_first(raw_ref, other_ref, shear_ref, other_shear_ref, width_ref, right_ref, left_ref, kept_ref, shift_ref, *refs):
-    out_refs, (shears, other_shears, widths, sems) = refs[:-4], refs[-4:]
+def spread_shifts(values, slots):
+    plane = lax.broadcasted_iota(jnp.int32, (slots, LANE), 0) & 3
+    return jnp.where(plane < 2, jnp.where(plane == 0, values[0], values[1]), jnp.where(plane == 2, values[2], values[3]))
+
+
+def strip_picks(widths, columns):
+    tile = lax.axis_index("tile")
+    tiles = lax.axis_size("tile")
+    lane = lax.broadcasted_iota(jnp.int32, (8, columns), 1)
+    line = lax.broadcasted_iota(jnp.int32, (8, columns), 0)
+    right_width = widths[jnp.minimum(tile, tiles - 2)]
+    left_width = widths[jnp.maximum(tile - 1, 0)]
+    toward_right = jnp.where((lane == columns - right_width - 8 + line) & (line >= 2), 1.0, 0.0)
+    toward_left = jnp.where((lane == left_width + line) & (line < 6), 1.0, 0.0)
+    return jnp.concatenate([toward_right, toward_left], 0).astype(BF16)
+
+
+def pack_own(raw_ref, shear_ref, width_ref, kept_ref, shift_ref, pick_ref, strip_ref, *refs):
+    out_refs, (shears, widths, sems) = refs[:-3], refs[-3:]
     loads = [
         pltpu.make_async_copy(source, target, sems.at[index])
-        for index, (source, target) in enumerate(
-            ((raw_ref, kept_ref), (shear_ref, shears), (other_shear_ref, other_shears), (width_ref, widths))
-        )
+        for index, (source, target) in enumerate(((raw_ref, kept_ref), (shear_ref, shears), (width_ref, widths)))
     ]
     for load in loads:
         load.start()
     camera = raw_ref.shape[0] // 4
     columns = raw_ref.shape[1]
-    tile = lax.axis_index("tile")
-    tiles = lax.axis_size("tile")
     slab = lax.axis_index("slab")
-    lane = lax.broadcasted_iota(jnp.int32, (8, columns), 1)
-    line = lax.broadcasted_iota(jnp.int32, (8, columns), 0)
     for load in loads[1:]:
         load.wait()
-    right_width = widths[jnp.minimum(tile, tiles - 2)]
-    left_width = widths[jnp.maximum(tile - 1, 0)]
-    toward_right = jnp.where((lane == columns - right_width - 8 + line) & (line >= 2), 1.0, 0.0).astype(BF16)
-    toward_left = jnp.where((lane == left_width + line) & (line < 6), 1.0, 0.0).astype(BF16)
-    plane = lax.broadcasted_iota(jnp.int32, shift_ref.shape[1:], 0) & 3
-    for owner, values in enumerate((shears, other_shears)):
-        shift_ref[owner] = jnp.where(
-            plane < 2, jnp.where(plane == 0, values[0], values[1]), jnp.where(plane == 2, values[2], values[3])
-        )
+    pick_ref[...] = strip_picks(widths, columns)
+    shift_ref[...] = spread_shifts(shears, LANE)
     loads[0].wait()
     for step, out_ref in enumerate(out_refs):
-        for owner, planes_ref in enumerate((kept_ref, other_ref)):
-            table = place_table(shift_ref[owner, :SLOTS, :1], slab ^ (2 * step), camera)
-            placed = dot(table, planes_ref[:, : columns - LANE])
-            out_ref[owner * SLOTS : (owner + 1) * SLOTS, :] = placed.astype(BF16)
-    for owner, planes_ref in enumerate((kept_ref, other_ref)):
-        right_ref[8 * owner : 8 * owner + 8, :] = dot_rows(toward_right, planes_ref[...]).astype(BF16)
-        left_ref[8 * owner : 8 * owner + 8, :] = dot_rows(toward_left, planes_ref[...]).astype(BF16)
+        table = place_table(shift_ref[:SLOTS, :1], slab ^ (2 * step), camera)
+        out_ref[...] = dot(table, kept_ref[:, : columns - LANE]).astype(BF16)
+    strip_ref[...] = dot_rows(pick_ref[...], kept_ref[...])
+
+
+def pack_other(other_ref, shear_ref, pick_ref, strip_ref, *refs):
+    (shears, sem), refs = refs[-2:], refs[:-2]
+    pairs = (len(refs) - 3) // 2
+    own_refs, (right_ref, left_ref, shift_ref), out_refs = refs[:pairs], refs[pairs : pairs + 3], refs[pairs + 3 :]
+    load = pltpu.make_async_copy(shear_ref, shears, sem)
+    load.start()
+    camera = other_ref.shape[0] // 4
+    columns = other_ref.shape[1]
+    slab = lax.axis_index("slab")
+    for own_ref, out_ref in zip(own_refs, out_refs):
+        out_ref[:SLOTS, :] = own_ref[...]
+    strips = jnp.concatenate([strip_ref[...], dot_rows(pick_ref[...], other_ref[...])], 0)
+    right_ref[...] = jnp.concatenate([strips[:8], strips[16:24]], 0).astype(BF16)
+    left_ref[...] = jnp.concatenate([strips[8:16], strips[24:]], 0).astype(BF16)
+    load.wait()
+    shift_ref[...] = spread_shifts(shears, LANE)
+    for step, out_ref in enumerate(out_refs):
+        table = place_table(shift_ref[:SLOTS, :1], slab ^ (2 * step), camera)
+        out_ref[SLOTS:, :] = dot(table, other_ref[:, : columns - LANE]).astype(BF16)
 
 
 def stage(order_ref, *refs):
@@ -163,7 +184,7 @@
         load.wait()
 
 
-def pack_second(raw_ref, other_ref, shift_ref, from_left_ref, from_right_ref, order_ref, *out_refs):
+def pack_second(raw_ref, other_ref, shift_ref, other_shift_ref, from_left_ref, from_right_ref, order_ref, *out_refs):
     camera = raw_ref.shape[0] // 4
     columns = raw_ref.shape[1]
     slab = lax.axis_index("slab")
@@ -171,8 +192,8 @@
     right = jnp.where(tile < lax.axis_size("tile") - 1, from_right_ref[...].astype(F32), 0.0)
     left = jnp.where(tile > 0, from_left_ref[...].astype(F32), 0.0)
     for step, out_ref in enumerate(out_refs):
-        for owner, planes_ref in enumerate((raw_ref, other_ref)):
-            table = place_table(shift_ref[owner, :, :1], slab ^ (2 * step), camera)
+        for owner, (planes_ref, shifts_ref) in enumerate(((raw_ref, shift_ref), (other_ref, other_shift_ref))):
+            table = place_table(shifts_ref[:, :1], slab ^ (2 * step), camera)
             placed = dot(table[:SLOTS], planes_ref[:, columns - LANE :])
             out_ref[owner * SLOTS : (owner + 1) * SLOTS, :] = placed.astype(BF16)
             own = slice(8 * owner, 8 * owner + 8)
@@ -341,27 +362,35 @@
     other_shear = lax.ppermute(shear_offsets, "slab", swap)
     outside = [pltpu.with_memory_space_constraint(each, pltpu.HBM) for each in (raw, shear_offsets, intersection_widths)]
     strip = jax.ShapeDtypeStruct((16, planes * camera), BF16)
-    first = jax.ShapeDtypeStruct((2 * SLOTS, cut), BF16)
-    toward_right, toward_left, raw, shift, *chunks = pl.pallas_call(
-        pack_first,
+    shift = jax.ShapeDtypeStruct((LANE, LANE), jnp.int32)
+    raw, own_shift, pick, own_strip, *own = pl.pallas_call(
+        pack_own,
         out_shape=[
-            strip,
-            strip,
             jax.ShapeDtypeStruct((planes * camera, columns), BF16),
-            jax.ShapeDtypeStruct((2, LANE, LANE), jnp.int32),
+            shift,
+            jax.ShapeDtypeStruct((16, columns), BF16),
+            jax.ShapeDtypeStruct((16, planes * camera), F32),
         ]
-        + [first] * pairs,
-        in_specs=[OUTSIDE, VECTOR, OUTSIDE, ANYWHERE, OUTSIDE],
+        + [jax.ShapeDtypeStruct((SLOTS, cut), BF16)] * pairs,
+        in_specs=[OUTSIDE] * 3,
         out_specs=[VECTOR] * (4 + pairs),
         scratch_shapes=[
             pltpu.SMEM(shear_offsets.shape, jnp.int32),
-            pltpu.SMEM(shear_offsets.shape, jnp.int32),
             pltpu.SMEM(intersection_widths.shape, jnp.int32),
-            pltpu.SemaphoreType.DMA((4,)),
+            pltpu.SemaphoreType.DMA((3,)),
         ],
         compiler_params=PARAMS,
-        name="pack_first",
-    )(outside[0], other, outside[1], other_shear, outside[2])
+        name="pack_own",
+    )(*outside)
+    toward_right, toward_left, other_shift, *chunks = pl.pallas_call(
+        pack_other,
+        out_shape=[strip, strip, shift] + [jax.ShapeDtypeStruct((2 * SLOTS, cut), BF16)] * pairs,
+        in_specs=[VECTOR, ANYWHERE] + [VECTOR] * (2 + pairs),
+        out_specs=[VECTOR] * (3 + pairs),
+        scratch_shapes=[pltpu.SMEM(shear_offsets.shape, jnp.int32), pltpu.SemaphoreType.DMA],
+        compiler_params=PARAMS,
+        name="pack_other",
+    )(other, other_shear, pick, own_strip, *own)
     got_first = along(chunks, slabs)
     from_left = shifted(toward_right, 1)
     from_right = shifted(toward_left, -1)
@@ -380,11 +409,11 @@
     chunks = pl.pallas_call(
         pack_second,
         out_shape=[second] * pairs,
-        in_specs=[VECTOR] * 5 + [ANYWHERE],
+        in_specs=[VECTOR] * 6 + [ANYWHERE],
         out_specs=[VECTOR] * pairs,
         compiler_params=PARAMS,
         name="pack_second",
-    )(raw, other, shift, from_left, from_right, table["two"])
+    )(raw, other, own_shift, other_shift, from_left, from_right, table["two"])
     chunks, got_first[2] = lax.optimization_barrier((chunks, got_first[2]))
     got_second = along(chunks, slabs)
     partial, coarse = pl.pallas_call(

time: 31.2 us -> 30.6 us (0.981); the launches traced: 31 us -> 30.1 us
  waiting for transfers between devices: 5.76 us -> 4.71 us
  Pallas kernels: 10.6 us -> 11 us
  starting transfers between devices: 13.9 us -> 13.5 us
    ppermute x1, waiting for transfers between devices: 0.91 us -> 0.01 us  [body(): other_shear = lax.ppermute(shear_offsets, 'slab', swap)]
    pallas_call x1 -> x2, Pallas kernels: 2.3 us -> 2.72 us  [the longest x1 1.64 us: body(): pl.pallas_call(pack_own, out_shape=[jax.ShapeDtypeStruct((planes * camera...]
    ppermute x6, starting transfers between devices: 9.98 us -> 9.62 us  [along(): lax.ppermute(chunks[step], 'slab', [(i, i ^ 2 * step) for i in range(slab...]
  transfers between devices with their start and end apart: 10 -> 10, of which waited for: 5 -> 4; matrix products, arithmetic and copies ran while one was open for 0% -> 0% of each run, Pallas kernels for 18% -> 24%
where the time goes in v6:
time: 30.6 us; the launch traced here: 30.1 us
  starting transfers between devices  13.5 us (44%)
  Pallas kernels  11 us (36%)
  waiting for transfers between devices  4.71 us (15%)
  between operations  0.71 us (2%)
    ppermute x6, starting transfers between devices, along(): lax.ppermute(chunks[step], 'slab', [(i, i ^ 2 * step) for i in range(slab...  9.62 us
    ppermute x6, waiting for transfers between devices, along(): lax.ppermute(chunks[step], 'slab', [(i, i ^ 2 * step) for i in range(slab...  4.06 us
    pallas_call x1, Pallas kernels, body(): pl.pallas_call(functools.partial(first_half, pairs, scans), out_shape=[ja...  3 us
    ppermute x2, starting transfers between devices, shifted(): lax.ppermute(block, 'tile', [(i, (i + distance) % count) for i in range(c...  2.92 us
    pallas_call x1, Pallas kernels, body(): pl.pallas_call(functools.partial(second_half, pairs, scans), out_shape=[j...  2.67 us
    pallas_call x1, Pallas kernels, body(): pl.pallas_call(stage, out_shape=[jax.ShapeDtypeStruct(table[name].shape,...  1.86 us
    pallas_call x1, Pallas kernels, body(): pl.pallas_call(pack_own, out_shape=[jax.ShapeDtypeStruct((planes * camera...  1.64 us
    pallas_call x1, Pallas kernels, body(): pl.pallas_call(pack_other, out_shape=[strip, strip, shift] + [jax.ShapeDt...  1.08 us
  transfers between devices with their start and end apart: 10, of which 4 were waited for; matrix products, arithmetic and copies ran while one was open for 0% of the time, Pallas kernels for 24%

profile of v6, /device:TPU:0, one launch (start us, length us, event | category | flops | bytes accessed | tf_op | source)
XLA Modules:
  0.0 30.1 jit_solution(11959777376332213736)
XLA Ops:
  0.6 0.5 %collective-permute-start = (bf16[480,512]{1,0:T(8,128)(2,1)}, bf16[480,512]{1,0:T(8,128)(2,1)S(1)}, u32[]{:S(2)}, u32[]{:S(2)}) collective-permute-start(bf16[480,512]{1,0:T(8,128)(2,1)} %bitcast.1), channel_id=1, source_target_pairs={{0,1},{1,0},{2,3},{3,2},{4,5},{5,4},{6,7},{7,6},{8,9},{9,8},{10,11... | collective-permute-start | bytes 1474568 | tf_op jit(solution)/shard_map/ppermute | solution.py:361
  1.2 0.1 copy-done
  1.3 0.5 %collective-permute-start.1 = (s32[4]{0:T(128)S(1)}, s32[4]{0:T(128)S(1)}, u32[]{:S(2)}, u32[]{:S(2)}) collective-permute-start(s32[4]{0:T(128)S(1)} %copy-done), channel_id=1, source_target_pairs={{0,1},{1,0},{2,3},{3,2},{4,5},{5,4},{6,7},{7,6},{8,9},{9,8},{10,11... | collective-permute-start | bytes 56 | tf_op jit(solution)/shard_map/ppermute | solution.py:362
  1.7 1.6 %pack_own.1 = (bf16[480,512]{1,0:T(8,128)(2,1)S(1)}, s32[128,128]{1,0:T(8,128)S(1)}, bf16[16,512]{1,0:T(8,128)(2,1)S(1)}, f32[16,480]{1,0:T(8,128)S(1)}, bf16[10...) custom-call(bf16[480,512]{1,0:T(8,128)(2,1)} %bitcast.2, ...), custom_call_target="tpu_custom_call" | custom-call | tf_op jit(solution)/shard_map/pack_own/pallas_call | solution.py:366
  3.4 0.0 collective-permute-done.1.shear_ref
  3.4 0.0 collective-permute-done.other_ref
  3.4 1.1 %pack_other.1 = (bf16[16,480]{1,0:T(8,128)(2,1)S(1)}, bf16[16,480]{1,0:T(8,128)(2,1)S(1)}, s32[128,128]{1,0:T(8,128)S(1)}, bf16[208,384]{1,0:T(8,128)(2,1)S(1)},...) custom-call(bf16[480,512]{1,0:T(8,128)(2,1)S(1)} %collective-permute-done.other_ref, ...), custom_call_target="tpu_custom_call" | custom-call | tf_op jit(solution)/shard_map/pack_other/pallas_call | solution.py:385
  4.5 3.7 %collective-permute-start.4 = (bf16[208,384]{1,0:T(8,128)(2,1)S(1)}, bf16[208,384]{1,0:T(8,128)(2,1)S(1)}, u32[]{:S(2)}, u32[]{:S(2)}) collective-permute-start(bf16[208,384]{1,0:T(8,128)(2,1)S(1)} %get-tuple-element.63), channel_id=1, source_target_pairs={{0,4},{1,5},{2,6},{3,7},{4,0},{5,1},{6,2},{7,3},{8,12},{9,13},{10,... | collective-permute-start | bytes 479240 | tf_op jit(solution)/shard_map/ppermute | solution.py:343
  8.2 1.6 %collective-permute-start.8 = (bf16[208,384]{1,0:T(8,128)(2,1)S(1)}, bf16[208,384]{1,0:T(8,128)(2,1)S(1)}, u32[]{:S(2)}, u32[]{:S(2)}) collective-permute-start(bf16[208,384]{1,0:T(8,128)(2,1)S(1)} %get-tuple-element.71), channel_id=1, source_target_pairs={{0,2},{1,3},{2,0},{3,1},{4,6},{5,7},{6,4},{7,5},{8,10},{9,11},{10,... | collective-permute-start | bytes 479240 | tf_op jit(solution)/shard_map/ppermute | solution.py:343
  9.7 0.0 collective-permute-start.9
  9.7 1.7 %collective-permute-start.2 = (bf16[16,480]{1,0:T(8,128)(2,1)S(1)}, bf16[16,480]{1,0:T(8,128)(2,1)S(1)}, u32[]{:S(2)}, u32[]{:S(2)}) collective-permute-start(bf16[16,480]{1,0:T(8,128)(2,1)S(1)} %get-tuple-element.58), channel_id=1, source_target_pairs={{0,8},{8,16},{16,24},{24,0},{1,9},{9,17},{17,25},{25,1},{2,10},{10... | collective-permute-start | bytes 46088 | tf_op jit(solution)/shard_map/ppermute | solution.py:349
  11.4 1.2 %collective-permute-start.3 = (bf16[16,480]{1,0:T(8,128)(2,1)S(1)}, bf16[16,480]{1,0:T(8,128)(2,1)S(1)}, u32[]{:S(2)}, u32[]{:S(2)}) collective-permute-start(bf16[16,480]{1,0:T(8,128)(2,1)S(1)} %get-tuple-element.48.order_ref), channel_id=1, source_target_pairs={{0,24},{8,0},{16,8},{24,16},{1,25},{9,1},{17,9},{25,17},{2,26},{10... | collective-permute-start | bytes 46088 | tf_op jit(solution)/shard_map/ppermute | solution.py:349
  12.7 1.9 %stage.1 = (bf16[512,512]{1,0:T(8,128)(2,1)S(1)}, bf16[176,1024]{1,0:T(8,128)(2,1)S(1)}, bf16[4,512,256]{2,1,0:T(8,128)(2,1)S(1)}, bf16[4,256,256]{2,1,0:T(8,128...) custom-call(bf16[16,480]{1,0:T(8,128)(2,1)S(1)} %get-tuple-element.4, ...), custom_call_target="tpu_custom_call" | custom-call | tf_op jit(solution)/shard_map/stage/pallas_call | solution.py:399
  14.5 0.6 %collective-permute-done.3.from_right_ref = bf16[16,480]{1,0:T(8,128)(2,1)S(1)} collective-permute-done((bf16[16,480]{1,0:T(8,128)(2,1)S(1)}, bf16[16,480]{1,0:T(8,128)(2,1)S(1)}, u32[]{:S(2)}, u32[]{:S(2)}) %collective-permute-start.3) | collective-permute-done | bytes 15392 | tf_op jit(solution)/shard_map/ppermute | solution.py:349
  15.2 0.7 %pack_second.1 = (bf16[240,128]{1,0:T(8,128)(2,1)S(1)}, bf16[240,128]{1,0:T(8,128)(2,1)S(1)}, bf16[240,128]{1,0:T(8,128)(2,1)S(1)}, bf16[240,128]{1,0:T(8,128)(2,1)S(1)}) custom-call(bf16[480,512]{1,0:T(8,128)(2,1)S(1)} %get-tuple-element.55.raw_ref, bf16[480,512]{1,0:T(8,128)(2,1)S(1)} %collective-permute-done.other_ref, ...), custom_call_target="tpu_custom_call" | custom-call | tf_op jit(solution)/shard_map/pack_second/pallas_call | solution.py:409
  15.9 0.7 %collective-permute-done.4.refs_2_ = bf16[208,384]{1,0:T(8,128)(2,1)S(1)} collective-permute-done((bf16[208,384]{1,0:T(8,128)(2,1)S(1)}, bf16[208,384]{1,0:T(8,128)(2,1)S(1)}, u32[]{:S(2)}, u32[]{:S(2)}) %collective-permute-start.4) | collective-permute-done | bytes 159776 | tf_op jit(solution)/shard_map/ppermute | solution.py:343
  16.6 0.7 %collective-permute-start.5 = (bf16[240,128]{1,0:T(8,128)(2,1)S(1)}, bf16[240,128]{1,0:T(8,128)(2,1)S(1)}, u32[]{:S(2)}, u32[]{:S(2)}) collective-permute-start(bf16[240,128]{1,0:T(8,128)(2,1)S(1)} %get-tuple-element.65), channel_id=1, source_target_pairs={{0,2},{1,3},{2,0},{3,1},{4,6},{5,7},{6,4},{7,5},{8,10},{9,11},{10,... | collective-permute-start | bytes 184328 | tf_op jit(solution)/shard_map/ppermute | solution.py:343
  17.3 3.6 %collective-permute-start.6 = (bf16[240,128]{1,0:T(8,128)(2,1)S(1)}, bf16[240,128]{1,0:T(8,128)(2,1)S(1)}, u32[]{:S(2)}, u32[]{:S(2)}) collective-permute-start(bf16[240,128]{1,0:T(8,128)(2,1)S(1)} %get-tuple-element.66), channel_id=1, source_target_pairs={{0,4},{1,5},{2,6},{3,7},{4,0},{5,1},{6,2},{7,3},{8,12},{9,13},{10,... | collective-permute-start | bytes 184328 | tf_op jit(solution)/shard_map/ppermute | solution.py:343
  20.9 0.1 collective-permute-start.7
  21.0 0.0 collective-permute-done.8.refs_1_
  21.0 0.1 collective-permute-done.9.refs_3_
  21.1 3.0 %first_half.1 = (f32[512,512]{1,0:T(8,128)S(1)}, f32[176,384]{1,0:T(8,128)S(1)}) custom-call(bf16[512,512]{1,0:T(8,128)(2,1)S(1)} %get-tuple-element.49.rowscan_ref, bf16[176,1024]{1,0:T(8,128)(2,1)S(1)} %get-tuple-element.50.level_ref, bf16[4,512,256]{2,1,0:T(8,128)(2,1)S(1)} %get-tuple-element.68.column_ref, ...), custom_call_target="tpu_custom_call" | custom-call | tf_op jit(solution)/shard_map/first_half/pallas_call | solution.py:419
  24.1 3.3 %collective-permute-done.6.refs_4_ = bf16[240,128]{1,0:T(8,128)(2,1)S(1)} collective-permute-done((bf16[240,128]{1,0:T(8,128)(2,1)S(1)}, bf16[240,128]{1,0:T(8,128)(2,1)S(1)}, u32[]{:S(2)}, u32[]{:S(2)}) %collective-permute-start.6) | collective-permute-done | bytes 61472 | tf_op jit(solution)/shard_map/ppermute | solution.py:343
  27.4 2.7 %second_half.1 = (bf16[16,32,512]{2,1,0:T(8,128)(2,1)}, bf16[8,16,256]{2,1,0:T(8,128)(2,1)}, bf16[4,8,128]{2,1,0:T(8,128)(2,1)}) custom-call(bf16[512,512]{1,0:T(8,128)(2,1)S(1)} %get-tuple-element.49.rowscan_ref, bf16[176,1024]{1,0:T(8,128)(2,1)S(1)} %get-tuple-element.50.level_ref, bf16[4,256,256]{2,1,0:T(8,128)(2,1)S(1)} %get-tuple-element.51.column_ref, ...), custom_call_target="tpu_custom_call" | custom-call | tf_op jit(solution)/shard_map/second_half/pallas_call | solution.py:435
  (4 shorter events, 0.0 us)
Async XLA Ops:
  0.6 0.7 %copy-start = (s32[4]{0:T(128)S(1)}, s32[4]{0:T(128)}, u32[]{:S(2)}) copy-start(s32[4]{0:T(128)} %shear_ref.1) | copy-start | bytes 52
  0.6 2.8 %collective-permute-start = (bf16[480,512]{1,0:T(8,128)(2,1)}, bf16[480,512]{1,0:T(8,128)(2,1)S(1)}, u32[]{:S(2)}, u32[]{:S(2)}) collective-permute-start(bf16[480,512]{1,0:T(8,128)(2,1)} %bitcast.1), channel_id=1, source_target_pairs={{0,1},{1,0},{2,3},{3,2},{4,5},{5,4},{6,7},{7,6},{8,9},{9,8},{10,11... | collective-permute-start | bytes 1474568 | tf_op jit(solution)/shard_map/ppermute | solution.py:361
  1.3 2.1 %collective-permute-start.1 = (s32[4]{0:T(128)S(1)}, s32[4]{0:T(128)S(1)}, u32[]{:S(2)}, u32[]{:S(2)}) collective-permute-start(s32[4]{0:T(128)S(1)} %copy-done), channel_id=1, source_target_pairs={{0,1},{1,0},{2,3},{3,2},{4,5},{5,4},{6,7},{7,6},{8,9},{9,8},{10,11... | collective-permute-start | bytes 56 | tf_op jit(solution)/shard_map/ppermute | solution.py:362
  4.5 12.1 %collective-permute-start.4 = (bf16[208,384]{1,0:T(8,128)(2,1)S(1)}, bf16[208,384]{1,0:T(8,128)(2,1)S(1)}, u32[]{:S(2)}, u32[]{:S(2)}) collective-permute-start(bf16[208,384]{1,0:T(8,128)(2,1)S(1)} %get-tuple-element.63), channel_id=1, source_target_pairs={{0,4},{1,5},{2,6},{3,7},{4,0},{5,1},{6,2},{7,3},{8,12},{9,13},{10,... | collective-permute-start | bytes 479240 | tf_op jit(solution)/shard_map/ppermute | solution.py:343
  8.2 12.8 %collective-permute-start.8 = (bf16[208,384]{1,0:T(8,128)(2,1)S(1)}, bf16[208,384]{1,0:T(8,128)(2,1)S(1)}, u32[]{:S(2)}, u32[]{:S(2)}) collective-permute-start(bf16[208,384]{1,0:T(8,128)(2,1)S(1)} %get-tuple-element.71), channel_id=1, source_target_pairs={{0,2},{1,3},{2,0},{3,1},{4,6},{5,7},{6,4},{7,5},{8,10},{9,11},{10,... | collective-permute-start | bytes 479240 | tf_op jit(solution)/shard_map/ppermute | solution.py:343
  9.7 11.4 %collective-permute-start.9 = (bf16[208,384]{1,0:T(8,128)(2,1)S(1)}, bf16[208,384]{1,0:T(8,128)(2,1)S(1)}, u32[]{:S(2)}, u32[]{:S(2)}) collective-permute-start(bf16[208,384]{1,0:T(8,128)(2,1)S(1)} %get-tuple-element.73), channel_id=1, source_target_pairs={{0,6},{1,7},{2,4},{3,5},{4,2},{5,3},{6,0},{7,1},{8,14},{9,15},{10,... | collective-permute-start | bytes 479240 | tf_op jit(solution)/shard_map/ppermute | solution.py:343
  9.7 4.8 %collective-permute-start.2 = (bf16[16,480]{1,0:T(8,128)(2,1)S(1)}, bf16[16,480]{1,0:T(8,128)(2,1)S(1)}, u32[]{:S(2)}, u32[]{:S(2)}) collective-permute-start(bf16[16,480]{1,0:T(8,128)(2,1)S(1)} %get-tuple-element.58), channel_id=1, source_target_pairs={{0,8},{8,16},{16,24},{24,0},{1,9},{9,17},{17,25},{25,1},{2,10},{10... | collective-permute-start | bytes 46088 | tf_op jit(solution)/shard_map/ppermute | solution.py:349
  11.4 3.7 %collective-permute-start.3 = (bf16[16,480]{1,0:T(8,128)(2,1)S(1)}, bf16[16,480]{1,0:T(8,128)(2,1)S(1)}, u32[]{:S(2)}, u32[]{:S(2)}) collective-permute-start(bf16[16,480]{1,0:T(8,128)(2,1)S(1)} %get-tuple-element.48.order_ref), channel_id=1, source_target_pairs={{0,24},{8,0},{16,8},{24,16},{1,25},{9,1},{17,9},{25,17},{2,26},{10... | collective-permute-start | bytes 46088 | tf_op jit(solution)/shard_map/ppermute | solution.py:349
  16.6 7.5 %collective-permute-start.5 = (bf16[240,128]{1,0:T(8,128)(2,1)S(1)}, bf16[240,128]{1,0:T(8,128)(2,1)S(1)}, u32[]{:S(2)}, u32[]{:S(2)}) collective-permute-start(bf16[240,128]{1,0:T(8,128)(2,1)S(1)} %get-tuple-element.65), channel_id=1, source_target_pairs={{0,2},{1,3},{2,0},{3,1},{4,6},{5,7},{6,4},{7,5},{8,10},{9,11},{10,... | collective-permute-start | bytes 184328 | tf_op jit(solution)/shard_map/ppermute | solution.py:343
  17.3 10.1 %collective-permute-start.6 = (bf16[240,128]{1,0:T(8,128)(2,1)S(1)}, bf16[240,128]{1,0:T(8,128)(2,1)S(1)}, u32[]{:S(2)}, u32[]{:S(2)}) collective-permute-start(bf16[240,128]{1,0:T(8,128)(2,1)S(1)} %get-tuple-element.66), channel_id=1, source_target_pairs={{0,4},{1,5},{2,6},{3,7},{4,0},{5,1},{6,2},{7,3},{8,12},{9,13},{10,... | collective-permute-start | bytes 184328 | tf_op jit(solution)/shard_map/ppermute | solution.py:343
  20.9 6.5 %collective-permute-start.7 = (bf16[240,128]{1,0:T(8,128)(2,1)S(1)}, bf16[240,128]{1,0:T(8,128)(2,1)S(1)}, u32[]{:S(2)}, u32[]{:S(2)}) collective-permute-start(bf16[240,128]{1,0:T(8,128)(2,1)S(1)} %get-tuple-element.67), channel_id=1, source_target_pairs={{0,6},{1,7},{2,4},{3,5},{4,2},{5,3},{6,0},{7,1},{8,14},{9,15},{10,... | collective-permute-start | bytes 184328 | tf_op jit(solution)/shard_map/ppermute | solution.py:343

commit v7 on v6

--- a/solution.py
+++ b/solution.py
@@ -13,10 +13,9 @@
 SLAB_ROWS = 16
 STRIP = 6
 RADIUS = 4
-LOW = 6
-HIGH = 4
-NEED = SLAB_ROWS + LOW + HIGH
-SLOTS = 4 * NEED
+NEED = SLAB_ROWS + 2 * RADIUS
+PLACED = 4 * NEED
+SLOTS = PLACED + 8
 LEVEL = 11
 LANE = 128
 F32 = jnp.float32
@@ -44,18 +43,21 @@
     return [high, (table - high.astype(np.float64)).astype(ml_dtypes.bfloat16)]
 
 
-def row_scan_table(row_band, scan_band, groups):
+def row_scan_table(row_band, scan_band, groups, early=None):
     rows_out, rows_in = row_band.shape
     scans_out = scan_band.shape[0]
     scans = scan_band.reshape(scans_out, groups, 4)
-    table = np.einsum("yr,sgp->ysgrp", row_band, scans)
-    table = table.reshape(rows_out * scans_out, groups, rows_in * 4)
-    table = np.pad(table, ((0, 0), (0, 0), (0, LANE - rows_in * 4)))
+    table = np.zeros((rows_out, scans_out, groups, LANE))
+    table[..., :PLACED] = np.einsum("yr,sgp->ysgrp", row_band, scans).reshape(rows_out, scans_out, groups, PLACED)
+    if early is not None:
+        for group in range(groups):
+            start = PLACED + 4 * (group & 1)
+            table[:, :, group, start : start + 4] = early[:, None, None] * scans[:, group]
     return table.reshape(rows_out * scans_out, groups * LANE)
 
 
 def tables(scans, columns):
-    row_in = np.arange(NEED) - LOW
+    row_in = np.arange(NEED) - RADIUS
     own = np.arange(SLAB_ROWS)
     near = np.arange(16) - 4
     block = np.arange(8)
@@ -71,8 +73,12 @@
         column_last += two_parts(sign * band(taps, last, touched).T)
     level_rows = 2 * np.arange(LEVEL) - 4
     level_scans = 2 * np.arange(scans // 2)
+    early = np.arange(LEVEL) == 0
     level = row_scan_table(
-        band(BINOMIAL, row_in, level_rows), band(BINOMIAL, np.arange(scans), level_scans), scans // 4
+        band(BINOMIAL, row_in, level_rows) * ~early[:, None],
+        band(BINOMIAL, np.arange(scans), level_scans),
+        scans // 4,
+        early * 1.0,
     )
     edges = np.array([-4, -2, columns, columns + 2])
     targets = np.concatenate([2 * np.arange(columns // 2), edges])
@@ -103,15 +109,28 @@
     return lax.dot_general(left, right, (((1,), (1,)), ((), ())), preferred_element_type=F32)
 
 
-def place_table(shift, slab, camera):
-    slots = shift.shape[0]
-    slot = lax.broadcasted_iota(jnp.int32, (slots, 1), 0)
-    plane, row = slot & 3, slot >> 2
-    source = slab * SLAB_ROWS - LOW + row - shift
-    inside = (source >= 0) & (source < camera) & (row < NEED)
-    wanted = jnp.where(inside, plane * camera + source, -1)
-    lane = lax.broadcasted_iota(jnp.int32, (slots, 4 * camera), 1)
-    return jnp.where(lane == wanted, 1.0, 0.0).astype(BF16)
+def place_table(shift, slab, camera, owner):
+    lanes = 4 * camera
+    slot = lax.broadcasted_iota(jnp.int32, (PLACED, 1), 0)
+    plane = slot & 3
+    source = slab * SLAB_ROWS - RADIUS + (slot >> 2) - shift[:PLACED]
+    wanted = jnp.where((source >= 0) & (source < camera), plane * camera + source, -1)
+    lane = lax.broadcasted_iota(jnp.int32, (PLACED, lanes), 1)
+    rows = jnp.where(lane == wanted, 1.0, 0.0).astype(BF16)
+    slot = lax.broadcasted_iota(jnp.int32, (8, 1), 0)
+    source = lax.broadcasted_iota(jnp.int32, (8, lanes), 1) - (slot & 3) * camera
+    tap = source + shift[:8] - (slab * SLAB_ROWS - 6)
+    inside = (source >= 0) & (source < camera) & ((slot >> 2) == owner) & (tap >= 0) & (tap < 5)
+    weight = jnp.where(tap == 2, 6.0 / 16.0, jnp.where((tap == 1) | (tap == 3), 4.0 / 16.0, 1.0 / 16.0))
+    return rows, jnp.where(inside, weight, 0.0).astype(BF16)
+
+
+def place_tables(stack, pairs, shift, slab, camera, owner):
+    for step in range(pairs):
+        rows, early = place_table(shift, slab ^ (2 * step), camera, owner)
+        stack[step * LANE : step * LANE + PLACED, :] = rows
+        stack[step * LANE + PLACED : step * LANE + SLOTS, :] = early
+        stack[step * LANE + SLOTS : (step + 1) * LANE, :] = jnp.zeros((LANE - SLOTS, 4 * camera), BF16)
 
 
 def spread_shifts(values, slots):
@@ -131,8 +150,8 @@
     return jnp.concatenate([toward_right, toward_left], 0).astype(BF16)
 
 
-def pack_own(raw_ref, shear_ref, width_ref, kept_ref, shift_ref, pick_ref, strip_ref, *refs):
-    out_refs, (shears, widths, sems) = refs[:-3], refs[-3:]
+def pack_own(raw_ref, shear_ref, width_ref, kept_ref, shift_ref, pick_ref, strip_ref, early_ref, *refs):
+    out_refs, (shears, widths, sems, stack) = refs[:-4], refs[-4:]
     loads = [
         pltpu.make_async_copy(source, target, sems.at[index])
         for index, (source, target) in enumerate(((raw_ref, kept_ref), (shear_ref, shears), (width_ref, widths)))
@@ -146,15 +165,17 @@
         load.wait()
     pick_ref[...] = strip_picks(widths, columns)
     shift_ref[...] = spread_shifts(shears, LANE)
+    place_tables(stack, len(out_refs), shift_ref[:, :1], slab, camera, slab & 1)
     loads[0].wait()
+    placed = dot(stack[...], kept_ref[:, : columns - LANE])
     for step, out_ref in enumerate(out_refs):
-        table = place_table(shift_ref[:SLOTS, :1], slab ^ (2 * step), camera)
-        out_ref[...] = dot(table, kept_ref[:, : columns - LANE]).astype(BF16)
+        out_ref[...] = placed[step * LANE : step * LANE + PLACED].astype(BF16)
+        early_ref[step] = placed[step * LANE + PLACED : step * LANE + SLOTS]
     strip_ref[...] = dot_rows(pick_ref[...], kept_ref[...])
 
 
-def pack_other(other_ref, shear_ref, pick_ref, strip_ref, *refs):
-    (shears, sem), refs = refs[-2:], refs[:-2]
+def pack_other(other_ref, shear_ref, pick_ref, strip_ref, early_ref, *refs):
+    (shears, sem, stack), refs = refs[-3:], refs[:-3]
     pairs = (len(refs) - 3) // 2
     own_refs, (right_ref, left_ref, shift_ref), out_refs = refs[:pairs], refs[pairs : pairs + 3], refs[pairs + 3 :]
     load = pltpu.make_async_copy(shear_ref, shears, sem)
@@ -163,15 +184,17 @@
     columns = other_ref.shape[1]
     slab = lax.axis_index("slab")
     for own_ref, out_ref in zip(own_refs, out_refs):
-        out_ref[:SLOTS, :] = own_ref[...]
+        out_ref[:PLACED, :] = own_ref[...]
     strips = jnp.concatenate([strip_ref[...], dot_rows(pick_ref[...], other_ref[...])], 0)
     right_ref[...] = jnp.concatenate([strips[:8], strips[16:24]], 0).astype(BF16)
     left_ref[...] = jnp.concatenate([strips[8:16], strips[24:]], 0).astype(BF16)
     load.wait()
     shift_ref[...] = spread_shifts(shears, LANE)
+    place_tables(stack, pairs, shift_ref[:, :1], slab, camera, ~slab & 1)
+    placed = dot(stack[...], other_ref[:, : columns - LANE])
     for step, out_ref in enumerate(out_refs):
-        table = place_table(shift_ref[:SLOTS, :1], slab ^ (2 * step), camera)
-        out_ref[SLOTS:, :] = dot(table, other_ref[:, : columns - LANE]).astype(BF16)
+        out_ref[PLACED : 2 * PLACED, :] = placed[step * LANE : step * LANE + PLACED].astype(BF16)
+        out_ref[2 * PLACED :, :] = (early_ref[step] + placed[step * LANE + PLACED : step * LANE + SLOTS]).astype(BF16)
 
 
 def stage(order_ref, *refs):
@@ -192,14 +215,20 @@
     right = jnp.where(tile < lax.axis_size("tile") - 1, from_right_ref[...].astype(F32), 0.0)
     left = jnp.where(tile > 0, from_left_ref[...].astype(F32), 0.0)
     for step, out_ref in enumerate(out_refs):
+        total = 0.0
         for owner, (planes_ref, shifts_ref) in enumerate(((raw_ref, shift_ref), (other_ref, other_shift_ref))):
-            table = place_table(shifts_ref[:, :1], slab ^ (2 * step), camera)
-            placed = dot(table[:SLOTS], planes_ref[:, columns - LANE :])
-            out_ref[owner * SLOTS : (owner + 1) * SLOTS, :] = placed.astype(BF16)
+            rows, early = place_table(shifts_ref[:, :1], slab ^ (2 * step), camera, (slab & 1) ^ owner)
+            planes = planes_ref[:, columns - LANE :]
+            out_ref[owner * PLACED : (owner + 1) * PLACED, :] = dot(rows, planes).astype(BF16)
+            total = total + dot(early, planes)
             own = slice(8 * owner, 8 * owner + 8)
             strips = jnp.concatenate([right[own], left[own]], 0).astype(BF16)
-            start = 2 * SLOTS + 16 * owner
-            out_ref[start : start + 16, :] = dot_rows(strips, table).astype(BF16)
+            start = 2 * PLACED + 8 + 16 * owner
+            table = jnp.concatenate(
+                [rows.astype(F32), early.astype(F32), jnp.zeros((LANE - SLOTS, rows.shape[1]), F32)], 0
+            )
+            out_ref[start : start + 16, :] = dot_rows(strips, table.astype(BF16)).astype(BF16)
+        out_ref[2 * PLACED : 2 * PLACED + 8, :] = total.astype(BF16)
 
 
 def collect(in_refs, volume, scans):
@@ -211,8 +240,9 @@
     volume[groups + 1] = outside
     for index in range(groups):
         group = (slab ^ index) + 1
-        start = (index & 1) * SLOTS
-        volume[group, :SLOTS, :lanes] = in_refs[index >> 1][start : start + SLOTS, :]
+        start = (index & 1) * PLACED
+        volume[group, :PLACED, :lanes] = in_refs[index >> 1][start : start + PLACED, :]
+        volume[group, PLACED:SLOTS, :lanes] = in_refs[index >> 1][2 * PLACED : 2 * PLACED + 8, :]
         volume[group, SLOTS:, :lanes] = jnp.zeros((LANE - SLOTS, lanes), BF16)
 
 
@@ -273,7 +303,7 @@
     collect(in_refs, volume, scans)
     for index in range(groups):
         place = pl.multiple_of((slab ^ index) * LANE, LANE)
-        start = 2 * SLOTS + 16 * (index & 1)
+        start = 2 * PLACED + 8 + 16 * (index & 1)
         strips[:, pl.ds(place, LANE)] = in_refs[index >> 1][start : start + 16, :]
     line = lax.broadcasted_iota(jnp.int32, (16, LANE), 0)
     lane = lax.broadcasted_iota(jnp.int32, (16, LANE), 1)
@@ -363,38 +393,44 @@
     outside = [pltpu.with_memory_space_constraint(each, pltpu.HBM) for each in (raw, shear_offsets, intersection_widths)]
     strip = jax.ShapeDtypeStruct((16, planes * camera), BF16)
     shift = jax.ShapeDtypeStruct((LANE, LANE), jnp.int32)
-    raw, own_shift, pick, own_strip, *own = pl.pallas_call(
+    raw, own_shift, pick, own_strip, early, *own = pl.pallas_call(
         pack_own,
         out_shape=[
             jax.ShapeDtypeStruct((planes * camera, columns), BF16),
             shift,
             jax.ShapeDtypeStruct((16, columns), BF16),
             jax.ShapeDtypeStruct((16, planes * camera), F32),
+            jax.ShapeDtypeStruct((pairs, 8, cut), F32),
         ]
-        + [jax.ShapeDtypeStruct((SLOTS, cut), BF16)] * pairs,
+        + [jax.ShapeDtypeStruct((PLACED, cut), BF16)] * pairs,
         in_specs=[OUTSIDE] * 3,
-        out_specs=[VECTOR] * (4 + pairs),
+        out_specs=[VECTOR] * (5 + pairs),
         scratch_shapes=[
             pltpu.SMEM(shear_offsets.shape, jnp.int32),
             pltpu.SMEM(intersection_widths.shape, jnp.int32),
             pltpu.SemaphoreType.DMA((3,)),
+            pltpu.VMEM((pairs * LANE, planes * camera), BF16),
         ],
         compiler_params=PARAMS,
         name="pack_own",
     )(*outside)
     toward_right, toward_left, other_shift, *chunks = pl.pallas_call(
         pack_other,
-        out_shape=[strip, strip, shift] + [jax.ShapeDtypeStruct((2 * SLOTS, cut), BF16)] * pairs,
-        in_specs=[VECTOR, ANYWHERE] + [VECTOR] * (2 + pairs),
+        out_shape=[strip, strip, shift] + [jax.ShapeDtypeStruct((2 * PLACED + 8, cut), BF16)] * pairs,
+        in_specs=[VECTOR, ANYWHERE] + [VECTOR] * (3 + pairs),
         out_specs=[VECTOR] * (3 + pairs),
-        scratch_shapes=[pltpu.SMEM(shear_offsets.shape, jnp.int32), pltpu.SemaphoreType.DMA],
+        scratch_shapes=[
+            pltpu.SMEM(shear_offsets.shape, jnp.int32),
+            pltpu.SemaphoreType.DMA,
+            pltpu.VMEM((pairs * LANE, planes * camera), BF16),
+        ],
         compiler_params=PARAMS,
         name="pack_other",
-    )(other, other_shear, pick, own_strip, *own)
+    )(other, other_shear, pick, own_strip, early, *own)
     got_first = along(chunks, slabs)
     from_left = shifted(toward_right, 1)
     from_right = shifted(toward_left, -1)
-    second = jax.ShapeDtypeStruct((2 * SLOTS + 32, LANE), BF16)
+    second = jax.ShapeDtypeStruct((2 * PLACED + 40, LANE), BF16)
     names = list(table)
     staged = pl.pallas_call(
         stage,

time: 30.6 us -> 30 us (0.980)
  waiting for transfers between devices: 4.71 us -> 3.96 us
    ppermute x6, waiting for transfers between devices: 4.06 us -> 3.31 us  [along(): lax.ppermute(chunks[step], 'slab', [(i, i ^ 2 * step) for i in range(slab...]
  transfers between devices with their start and end apart: 10 -> 10, of which waited for: 4 -> 3; matrix products, arithmetic and copies ran while one was open for 0% -> 0% of each run, Pallas kernels for 24% -> 25%
where the time goes in v7:
time: 30 us; the launch traced here: 29.4 us
  starting transfers between devices  13.5 us (45%)
  Pallas kernels  11.1 us (37%)
  waiting for transfers between devices  3.96 us (13%)
  between operations  0.71 us (2%)
    ppermute x6, starting transfers between devices, along(): lax.ppermute(chunks[step], 'slab', [(i, i ^ 2 * step) for i in range(slab...  9.61 us
    ppermute x6, waiting for transfers between devices, along(): lax.ppermute(chunks[step], 'slab', [(i, i ^ 2 * step) for i in range(slab...  3.31 us
    pallas_call x1, Pallas kernels, body(): pl.pallas_call(functools.partial(first_half, pairs, scans), out_shape=[ja...  3 us
    ppermute x2, starting transfers between devices, shifted(): lax.ppermute(block, 'tile', [(i, (i + distance) % count) for i in range(c...  2.92 us
    pallas_call x1, Pallas kernels, body(): pl.pallas_call(functools.partial(second_half, pairs, scans), out_shape=[j...  2.67 us
    pallas_call x1, Pallas kernels, body(): pl.pallas_call(stage, out_shape=[jax.ShapeDtypeStruct(table[name].shape,...  1.86 us
    pallas_call x1, Pallas kernels, body(): pl.pallas_call(pack_own, out_shape=[jax.ShapeDtypeStruct((planes * camera...  1.56 us
    pallas_call x1, Pallas kernels, body(): pl.pallas_call(pack_other, out_shape=[strip, strip, shift] + [jax.ShapeDt...  1.17 us
  transfers between devices with their start and end apart: 10, of which 3 were waited for; matrix products, arithmetic and copies ran while one was open for 0% of the time, Pallas kernels for 25%

profile of v7, /device:TPU:0, one launch (start us, length us, event | category | flops | bytes accessed | tf_op | source)
XLA Modules:
  0.0 29.4 jit_solution(9244463224971799482)
XLA Ops:
  0.6 0.5 %collective-permute-start = (bf16[480,512]{1,0:T(8,128)(2,1)}, bf16[480,512]{1,0:T(8,128)(2,1)S(1)}, u32[]{:S(2)}, u32[]{:S(2)}) collective-permute-start(bf16[480,512]{1,0:T(8,128)(2,1)} %bitcast.1), channel_id=1, source_target_pairs={{0,1},{1,0},{2,3},{3,2},{4,5},{5,4},{6,7},{7,6},{8,9},{9,8},{10,11... | collective-permute-start | bytes 1474568 | tf_op jit(solution)/shard_map/ppermute | solution.py:391
  1.2 0.1 copy-done
  1.3 0.5 %collective-permute-start.1 = (s32[4]{0:T(128)S(1)}, s32[4]{0:T(128)S(1)}, u32[]{:S(2)}, u32[]{:S(2)}) collective-permute-start(s32[4]{0:T(128)S(1)} %copy-done), channel_id=1, source_target_pairs={{0,1},{1,0},{2,3},{3,2},{4,5},{5,4},{6,7},{7,6},{8,9},{9,8},{10,11... | collective-permute-start | bytes 56 | tf_op jit(solution)/shard_map/ppermute | solution.py:392
  1.7 1.6 %pack_own.1 = (bf16[480,512]{1,0:T(8,128)(2,1)S(1)}, s32[128,128]{1,0:T(8,128)S(1)}, bf16[16,512]{1,0:T(8,128)(2,1)S(1)}, f32[16,480]{1,0:T(8,128)S(1)}, f32[4,8...) custom-call(bf16[480,512]{1,0:T(8,128)(2,1)} %bitcast.2, ...), custom_call_target="tpu_custom_call" | custom-call | tf_op jit(solution)/shard_map/pack_own/pallas_call | solution.py:396
  3.3 0.0 collective-permute-done.1.shear_ref
  3.3 0.0 collective-permute-done.other_ref
  3.3 1.2 %pack_other.1 = (bf16[16,480]{1,0:T(8,128)(2,1)S(1)}, bf16[16,480]{1,0:T(8,128)(2,1)S(1)}, s32[128,128]{1,0:T(8,128)S(1)}, bf16[200,384]{1,0:T(8,128)(2,1)S(1)},...) custom-call(bf16[480,512]{1,0:T(8,128)(2,1)S(1)} %collective-permute-done.other_ref, ...), custom_call_target="tpu_custom_call" | custom-call | tf_op jit(solution)/shard_map/pack_other/pallas_call | solution.py:417
  4.5 3.7 %collective-permute-start.4 = (bf16[200,384]{1,0:T(8,128)(2,1)S(1)}, bf16[200,384]{1,0:T(8,128)(2,1)S(1)}, u32[]{:S(2)}, u32[]{:S(2)}) collective-permute-start(bf16[200,384]{1,0:T(8,128)(2,1)S(1)} %get-tuple-element.65), channel_id=1, source_target_pairs={{0,4},{1,5},{2,6},{3,7},{4,0},{5,1},{6,2},{7,3},{8,12},{9,13},{10,... | collective-permute-start | bytes 460808 | tf_op jit(solution)/shard_map/ppermute | solution.py:373
  8.2 1.6 %collective-permute-start.8 = (bf16[200,384]{1,0:T(8,128)(2,1)S(1)}, bf16[200,384]{1,0:T(8,128)(2,1)S(1)}, u32[]{:S(2)}, u32[]{:S(2)}) collective-permute-start(bf16[200,384]{1,0:T(8,128)(2,1)S(1)} %get-tuple-element.73), channel_id=1, source_target_pairs={{0,2},{1,3},{2,0},{3,1},{4,6},{5,7},{6,4},{7,5},{8,10},{9,11},{10,... | collective-permute-start | bytes 460808 | tf_op jit(solution)/shard_map/ppermute | solution.py:373
  9.7 0.0 collective-permute-start.9
  9.7 1.7 %collective-permute-start.2 = (bf16[16,480]{1,0:T(8,128)(2,1)S(1)}, bf16[16,480]{1,0:T(8,128)(2,1)S(1)}, u32[]{:S(2)}, u32[]{:S(2)}) collective-permute-start(bf16[16,480]{1,0:T(8,128)(2,1)S(1)} %get-tuple-element.60), channel_id=1, source_target_pairs={{0,8},{8,16},{16,24},{24,0},{1,9},{9,17},{17,25},{25,1},{2,10},{10... | collective-permute-start | bytes 46088 | tf_op jit(solution)/shard_map/ppermute | solution.py:379
  11.4 1.2 %collective-permute-start.3 = (bf16[16,480]{1,0:T(8,128)(2,1)S(1)}, bf16[16,480]{1,0:T(8,128)(2,1)S(1)}, u32[]{:S(2)}, u32[]{:S(2)}) collective-permute-start(bf16[16,480]{1,0:T(8,128)(2,1)S(1)} %get-tuple-element.50.order_ref), channel_id=1, source_target_pairs={{0,24},{8,0},{16,8},{24,16},{1,25},{9,1},{17,9},{25,17},{2,26},{10... | collective-permute-start | bytes 46088 | tf_op jit(solution)/shard_map/ppermute | solution.py:379
  12.7 1.9 %stage.1 = (bf16[512,512]{1,0:T(8,128)(2,1)S(1)}, bf16[176,1024]{1,0:T(8,128)(2,1)S(1)}, bf16[4,512,256]{2,1,0:T(8,128)(2,1)S(1)}, bf16[4,256,256]{2,1,0:T(8,128...) custom-call(bf16[16,480]{1,0:T(8,128)(2,1)S(1)} %get-tuple-element.5, ...), custom_call_target="tpu_custom_call" | custom-call | tf_op jit(solution)/shard_map/stage/pallas_call | solution.py:435
  14.5 0.6 %collective-permute-done.3.from_right_ref = bf16[16,480]{1,0:T(8,128)(2,1)S(1)} collective-permute-done((bf16[16,480]{1,0:T(8,128)(2,1)S(1)}, bf16[16,480]{1,0:T(8,128)(2,1)S(1)}, u32[]{:S(2)}, u32[]{:S(2)}) %collective-permute-start.3) | collective-permute-done | bytes 15392 | tf_op jit(solution)/shard_map/ppermute | solution.py:379
  15.2 0.8 %pack_second.1 = (bf16[232,128]{1,0:T(8,128)(2,1)S(1)}, bf16[232,128]{1,0:T(8,128)(2,1)S(1)}, bf16[232,128]{1,0:T(8,128)(2,1)S(1)}, bf16[232,128]{1,0:T(8,128)(2,1)S(1)}) custom-call(bf16[480,512]{1,0:T(8,128)(2,1)S(1)} %get-tuple-element.57.raw_ref, bf16[480,512]{1,0:T(8,128)(2,1)S(1)} %collective-permute-done.other_ref, ...), custom_call_target="tpu_custom_call" | custom-call | tf_op jit(solution)/shard_map/pack_second/pallas_call | solution.py:445
  16.0 0.3 %collective-permute-done.4.refs_2_ = bf16[200,384]{1,0:T(8,128)(2,1)S(1)} collective-permute-done((bf16[200,384]{1,0:T(8,128)(2,1)S(1)}, bf16[200,384]{1,0:T(8,128)(2,1)S(1)}, u32[]{:S(2)}, u32[]{:S(2)}) %collective-permute-start.4) | collective-permute-done | bytes 153632 | tf_op jit(solution)/shard_map/ppermute | solution.py:373
  16.3 0.7 %collective-permute-start.5 = (bf16[232,128]{1,0:T(8,128)(2,1)S(1)}, bf16[232,128]{1,0:T(8,128)(2,1)S(1)}, u32[]{:S(2)}, u32[]{:S(2)}) collective-permute-start(bf16[232,128]{1,0:T(8,128)(2,1)S(1)} %get-tuple-element.67), channel_id=1, source_target_pairs={{0,2},{1,3},{2,0},{3,1},{4,6},{5,7},{6,4},{7,5},{8,10},{9,11},{10,... | collective-permute-start | bytes 178184 | tf_op jit(solution)/shard_map/ppermute | solution.py:373
  17.0 3.6 %collective-permute-start.6 = (bf16[232,128]{1,0:T(8,128)(2,1)S(1)}, bf16[232,128]{1,0:T(8,128)(2,1)S(1)}, u32[]{:S(2)}, u32[]{:S(2)}) collective-permute-start(bf16[232,128]{1,0:T(8,128)(2,1)S(1)} %get-tuple-element.68), channel_id=1, source_target_pairs={{0,4},{1,5},{2,6},{3,7},{4,0},{5,1},{6,2},{7,3},{8,12},{9,13},{10,... | collective-permute-start | bytes 178184 | tf_op jit(solution)/shard_map/ppermute | solution.py:373
  20.6 0.1 collective-permute-start.7
  20.7 0.0 collective-permute-done.8.refs_1_
  20.7 3.0 %first_half.1 = (f32[512,512]{1,0:T(8,128)S(1)}, f32[176,384]{1,0:T(8,128)S(1)}) custom-call(bf16[512,512]{1,0:T(8,128)(2,1)S(1)} %get-tuple-element.51.rowscan_ref, bf16[176,1024]{1,0:T(8,128)(2,1)S(1)} %get-tuple-element.52.level_ref, bf16[4,512,256]{2,1,0:T(8,128)(2,1)S(1)} %get-tuple-element.70.column_ref, ...), custom_call_target="tpu_custom_call" | custom-call | tf_op jit(solution)/shard_map/first_half/pallas_call | solution.py:455
  23.7 3.0 %collective-permute-done.6.refs_4_ = bf16[232,128]{1,0:T(8,128)(2,1)S(1)} collective-permute-done((bf16[232,128]{1,0:T(8,128)(2,1)S(1)}, bf16[232,128]{1,0:T(8,128)(2,1)S(1)}, u32[]{:S(2)}, u32[]{:S(2)}) %collective-permute-start.6) | collective-permute-done | bytes 59424 | tf_op jit(solution)/shard_map/ppermute | solution.py:373
  26.7 0.0 collective-permute-done.7.refs_5_
  26.7 2.7 %second_half.1 = (bf16[16,32,512]{2,1,0:T(8,128)(2,1)}, bf16[8,16,256]{2,1,0:T(8,128)(2,1)}, bf16[4,8,128]{2,1,0:T(8,128)(2,1)}) custom-call(bf16[512,512]{1,0:T(8,128)(2,1)S(1)} %get-tuple-element.51.rowscan_ref, bf16[176,1024]{1,0:T(8,128)(2,1)S(1)} %get-tuple-element.52.level_ref, bf16[4,256,256]{2,1,0:T(8,128)(2,1)S(1)} %get-tuple-element.53.column_ref, ...), custom_call_target="tpu_custom_call" | custom-call | tf_op jit(solution)/shard_map/second_half/pallas_call | solution.py:471
  (4 shorter events, 0.0 us)
Async XLA Ops:
  0.6 0.7 %copy-start = (s32[4]{0:T(128)S(1)}, s32[4]{0:T(128)}, u32[]{:S(2)}) copy-start(s32[4]{0:T(128)} %shear_ref.1) | copy-start | bytes 52
  0.6 2.7 %collective-permute-start = (bf16[480,512]{1,0:T(8,128)(2,1)}, bf16[480,512]{1,0:T(8,128)(2,1)S(1)}, u32[]{:S(2)}, u32[]{:S(2)}) collective-permute-start(bf16[480,512]{1,0:T(8,128)(2,1)} %bitcast.1), channel_id=1, source_target_pairs={{0,1},{1,0},{2,3},{3,2},{4,5},{5,4},{6,7},{7,6},{8,9},{9,8},{10,11... | collective-permute-start | bytes 1474568 | tf_op jit(solution)/shard_map/ppermute | solution.py:391
  1.3 2.0 %collective-permute-start.1 = (s32[4]{0:T(128)S(1)}, s32[4]{0:T(128)S(1)}, u32[]{:S(2)}, u32[]{:S(2)}) collective-permute-start(s32[4]{0:T(128)S(1)} %copy-done), channel_id=1, source_target_pairs={{0,1},{1,0},{2,3},{3,2},{4,5},{5,4},{6,7},{7,6},{8,9},{9,8},{10,11... | collective-permute-start | bytes 56 | tf_op jit(solution)/shard_map/ppermute | solution.py:392
  4.5 11.8 %collective-permute-start.4 = (bf16[200,384]{1,0:T(8,128)(2,1)S(1)}, bf16[200,384]{1,0:T(8,128)(2,1)S(1)}, u32[]{:S(2)}, u32[]{:S(2)}) collective-permute-start(bf16[200,384]{1,0:T(8,128)(2,1)S(1)} %get-tuple-element.65), channel_id=1, source_target_pairs={{0,4},{1,5},{2,6},{3,7},{4,0},{5,1},{6,2},{7,3},{8,12},{9,13},{10,... | collective-permute-start | bytes 460808 | tf_op jit(solution)/shard_map/ppermute | solution.py:373
  8.2 12.6 %collective-permute-start.8 = (bf16[200,384]{1,0:T(8,128)(2,1)S(1)}, bf16[200,384]{1,0:T(8,128)(2,1)S(1)}, u32[]{:S(2)}, u32[]{:S(2)}) collective-permute-start(bf16[200,384]{1,0:T(8,128)(2,1)S(1)} %get-tuple-element.73), channel_id=1, source_target_pairs={{0,2},{1,3},{2,0},{3,1},{4,6},{5,7},{6,4},{7,5},{8,10},{9,11},{10,... | collective-permute-start | bytes 460808 | tf_op jit(solution)/shard_map/ppermute | solution.py:373
  9.7 11.0 %collective-permute-start.9 = (bf16[200,384]{1,0:T(8,128)(2,1)S(1)}, bf16[200,384]{1,0:T(8,128)(2,1)S(1)}, u32[]{:S(2)}, u32[]{:S(2)}) collective-permute-start(bf16[200,384]{1,0:T(8,128)(2,1)S(1)} %get-tuple-element.75), channel_id=1, source_target_pairs={{0,6},{1,7},{2,4},{3,5},{4,2},{5,3},{6,0},{7,1},{8,14},{9,15},{10,... | collective-permute-start | bytes 460808 | tf_op jit(solution)/shard_map/ppermute | solution.py:373
  9.7 4.8 %collective-permute-start.2 = (bf16[16,480]{1,0:T(8,128)(2,1)S(1)}, bf16[16,480]{1,0:T(8,128)(2,1)S(1)}, u32[]{:S(2)}, u32[]{:S(2)}) collective-permute-start(bf16[16,480]{1,0:T(8,128)(2,1)S(1)} %get-tuple-element.60), channel_id=1, source_target_pairs={{0,8},{8,16},{16,24},{24,0},{1,9},{9,17},{17,25},{25,1},{2,10},{10... | collective-permute-start | bytes 46088 | tf_op jit(solution)/shard_map/ppermute | solution.py:379
  11.4 3.7 %collective-permute-start.3 = (bf16[16,480]{1,0:T(8,128)(2,1)S(1)}, bf16[16,480]{1,0:T(8,128)(2,1)S(1)}, u32[]{:S(2)}, u32[]{:S(2)}) collective-permute-start(bf16[16,480]{1,0:T(8,128)(2,1)S(1)} %get-tuple-element.50.order_ref), channel_id=1, source_target_pairs={{0,24},{8,0},{16,8},{24,16},{1,25},{9,1},{17,9},{25,17},{2,26},{10... | collective-permute-start | bytes 46088 | tf_op jit(solution)/shard_map/ppermute | solution.py:379
  16.3 7.4 %collective-permute-start.5 = (bf16[232,128]{1,0:T(8,128)(2,1)S(1)}, bf16[232,128]{1,0:T(8,128)(2,1)S(1)}, u32[]{:S(2)}, u32[]{:S(2)}) collective-permute-start(bf16[232,128]{1,0:T(8,128)(2,1)S(1)} %get-tuple-element.67), channel_id=1, source_target_pairs={{0,2},{1,3},{2,0},{3,1},{4,6},{5,7},{6,4},{7,5},{8,10},{9,11},{10,... | collective-permute-start | bytes 178184 | tf_op jit(solution)/shard_map/ppermute | solution.py:373
  17.0 9.7 %collective-permute-start.6 = (bf16[232,128]{1,0:T(8,128)(2,1)S(1)}, bf16[232,128]{1,0:T(8,128)(2,1)S(1)}, u32[]{:S(2)}, u32[]{:S(2)}) collective-permute-start(bf16[232,128]{1,0:T(8,128)(2,1)S(1)} %get-tuple-element.68), channel_id=1, source_target_pairs={{0,4},{1,5},{2,6},{3,7},{4,0},{5,1},{6,2},{7,3},{8,12},{9,13},{10,... | collective-permute-start | bytes 178184 | tf_op jit(solution)/shard_map/ppermute | solution.py:373
  20.6 6.1 %collective-permute-start.7 = (bf16[232,128]{1,0:T(8,128)(2,1)S(1)}, bf16[232,128]{1,0:T(8,128)(2,1)S(1)}, u32[]{:S(2)}, u32[]{:S(2)}) collective-permute-start(bf16[232,128]{1,0:T(8,128)(2,1)S(1)} %get-tuple-element.69), channel_id=1, source_target_pairs={{0,6},{1,7},{2,4},{3,5},{4,2},{5,3},{6,0},{7,1},{8,14},{9,15},{10,... | collective-permute-start | bytes 178184 | tf_op jit(solution)/shard_map/ppermute | solution.py:373

commit v8 on v7

--- a/solution.py
+++ b/solution.py
@@ -261,12 +261,21 @@
         wide[2 * sigma + 1, block * rows : (block + 1) * rows, :] = low
 
 
+def dot_parts(high, low, right):
+    both = dot(jnp.concatenate([high, low], 0), right)
+    return both[: high.shape[0]] + both[high.shape[0] :]
+
+
 def across(wide, rows, lanes, column_ref, taken):
     total = None
     for sigma in range(2):
         high, low = wide[2 * sigma, rows, lanes], wide[2 * sigma + 1, rows, lanes]
-        part = dot(high, column_ref[2 * sigma, taken]) + dot(low, column_ref[2 * sigma, taken])
-        part = part + dot(high, column_ref[2 * sigma + 1, taken])
+        table = column_ref[2 * sigma, taken]
+        if rows == slice(None):
+            right = jnp.concatenate([table, table, column_ref[2 * sigma + 1, taken]], 0)
+            part = dot(jnp.concatenate([high, low, high], 1), right)
+        else:
+            part = dot(high, table) + dot(low, table) + dot(high, column_ref[2 * sigma + 1, taken])
         total = part if total is None else total + part
     return total
 
@@ -274,7 +283,7 @@
 def level_part(level_ref, level_column_ref, volume, scans):
     groups = scans // 4
     high, low = split(dot(level_ref[...], volume[1 : groups + 1].reshape(groups * LANE, volume.shape[-1])))
-    return dot(high, level_column_ref[...]) + dot(low, level_column_ref[...])
+    return dot_parts(high, low, level_column_ref[...])
 
 
 def first_half(count, scans, rowscan_ref, level_ref, column_ref, level_column_ref, *refs):
@@ -351,7 +360,7 @@
     copies.append(copy)
 
     high, low = split(dot(two_ref[...], ready.reshape(LEVEL * scans // 2, level.shape[-1])))
-    second = dot(high, two_column_ref[...]) + dot(low, two_column_ref[...])
+    second = dot_parts(high, low, two_column_ref[...])
     held_second[...] = second.reshape(second_ref.shape).astype(BF16)
     copy = pltpu.make_async_copy(held_second, second_ref, sems.at[scans // 16 + 1])
     copy.start()

time: 30 us -> 29.7 us (0.990)
  transfers between devices with their start and end apart: 10 -> 10, of which waited for: 3 -> 3; matrix products, arithmetic and copies ran while one was open for 0% -> 0% of each run, Pallas kernels for 25% -> 24%
where the time goes in v8:
time: 29.7 us; the launch traced here: 29.4 us
  starting transfers between devices  13.5 us (45%)
  Pallas kernels  10.9 us (37%)
  waiting for transfers between devices  4.14 us (14%)
  between operations  0.71 us (2%)
    ppermute x6, starting transfers between devices, along(): lax.ppermute(chunks[step], 'slab', [(i, i ^ 2 * step) for i in range(slab...  9.61 us
    ppermute x6, waiting for transfers between devices, along(): lax.ppermute(chunks[step], 'slab', [(i, i ^ 2 * step) for i in range(slab...  3.49 us
    ppermute x2, starting transfers between devices, shifted(): lax.ppermute(block, 'tile', [(i, (i + distance) % count) for i in range(c...  2.92 us
    pallas_call x1, Pallas kernels, body(): pl.pallas_call(functools.partial(first_half, pairs, scans), out_shape=[ja...  2.81 us
    pallas_call x1, Pallas kernels, body(): pl.pallas_call(functools.partial(second_half, pairs, scans), out_shape=[j...  2.63 us
    pallas_call x1, Pallas kernels, body(): pl.pallas_call(stage, out_shape=[jax.ShapeDtypeStruct(table[name].shape,...  1.86 us
    pallas_call x1, Pallas kernels, body(): pl.pallas_call(pack_own, out_shape=[jax.ShapeDtypeStruct((planes * camera...  1.56 us
    pallas_call x1, Pallas kernels, body(): pl.pallas_call(pack_other, out_shape=[strip, strip, shift] + [jax.ShapeDt...  1.17 us
  transfers between devices with their start and end apart: 10, of which 3 were waited for; matrix products, arithmetic and copies ran while one was open for 0% of the time, Pallas kernels for 24%

profile of v8, /device:TPU:0, one launch (start us, length us, event | category | flops | bytes accessed | tf_op | source)
XLA Modules:
  0.0 29.4 jit_solution(14473710551945852081)
XLA Ops:
  0.6 0.5 %collective-permute-start = (bf16[480,512]{1,0:T(8,128)(2,1)}, bf16[480,512]{1,0:T(8,128)(2,1)S(1)}, u32[]{:S(2)}, u32[]{:S(2)}) collective-permute-start(bf16[480,512]{1,0:T(8,128)(2,1)} %bitcast.1), channel_id=1, source_target_pairs={{0,1},{1,0},{2,3},{3,2},{4,5},{5,4},{6,7},{7,6},{8,9},{9,8},{10,11... | collective-permute-start | bytes 1474568 | tf_op jit(solution)/shard_map/ppermute | solution.py:400
  1.2 0.1 copy-done
  1.3 0.5 %collective-permute-start.1 = (s32[4]{0:T(128)S(1)}, s32[4]{0:T(128)S(1)}, u32[]{:S(2)}, u32[]{:S(2)}) collective-permute-start(s32[4]{0:T(128)S(1)} %copy-done), channel_id=1, source_target_pairs={{0,1},{1,0},{2,3},{3,2},{4,5},{5,4},{6,7},{7,6},{8,9},{9,8},{10,11... | collective-permute-start | bytes 56 | tf_op jit(solution)/shard_map/ppermute | solution.py:401
  1.7 1.6 %pack_own.1 = (bf16[480,512]{1,0:T(8,128)(2,1)S(1)}, s32[128,128]{1,0:T(8,128)S(1)}, bf16[16,512]{1,0:T(8,128)(2,1)S(1)}, f32[16,480]{1,0:T(8,128)S(1)}, f32[4,8...) custom-call(bf16[480,512]{1,0:T(8,128)(2,1)} %bitcast.2, ...), custom_call_target="tpu_custom_call" | custom-call | tf_op jit(solution)/shard_map/pack_own/pallas_call | solution.py:405
  3.3 0.0 collective-permute-done.1.shear_ref
  3.3 0.0 collective-permute-done.other_ref
  3.3 1.2 %pack_other.1 = (bf16[16,480]{1,0:T(8,128)(2,1)S(1)}, bf16[16,480]{1,0:T(8,128)(2,1)S(1)}, s32[128,128]{1,0:T(8,128)S(1)}, bf16[200,384]{1,0:T(8,128)(2,1)S(1)},...) custom-call(bf16[480,512]{1,0:T(8,128)(2,1)S(1)} %collective-permute-done.other_ref, ...), custom_call_target="tpu_custom_call" | custom-call | tf_op jit(solution)/shard_map/pack_other/pallas_call | solution.py:426
  4.5 3.7 %collective-permute-start.4 = (bf16[200,384]{1,0:T(8,128)(2,1)S(1)}, bf16[200,384]{1,0:T(8,128)(2,1)S(1)}, u32[]{:S(2)}, u32[]{:S(2)}) collective-permute-start(bf16[200,384]{1,0:T(8,128)(2,1)S(1)} %get-tuple-element.65), channel_id=1, source_target_pairs={{0,4},{1,5},{2,6},{3,7},{4,0},{5,1},{6,2},{7,3},{8,12},{9,13},{10,... | collective-permute-start | bytes 460808 | tf_op jit(solution)/shard_map/ppermute | solution.py:382
  8.2 1.6 %collective-permute-start.8 = (bf16[200,384]{1,0:T(8,128)(2,1)S(1)}, bf16[200,384]{1,0:T(8,128)(2,1)S(1)}, u32[]{:S(2)}, u32[]{:S(2)}) collective-permute-start(bf16[200,384]{1,0:T(8,128)(2,1)S(1)} %get-tuple-element.73), channel_id=1, source_target_pairs={{0,2},{1,3},{2,0},{3,1},{4,6},{5,7},{6,4},{7,5},{8,10},{9,11},{10,... | collective-permute-start | bytes 460808 | tf_op jit(solution)/shard_map/ppermute | solution.py:382
  9.7 0.0 collective-permute-start.9
  9.7 1.7 %collective-permute-start.2 = (bf16[16,480]{1,0:T(8,128)(2,1)S(1)}, bf16[16,480]{1,0:T(8,128)(2,1)S(1)}, u32[]{:S(2)}, u32[]{:S(2)}) collective-permute-start(bf16[16,480]{1,0:T(8,128)(2,1)S(1)} %get-tuple-element.60), channel_id=1, source_target_pairs={{0,8},{8,16},{16,24},{24,0},{1,9},{9,17},{17,25},{25,1},{2,10},{10... | collective-permute-start | bytes 46088 | tf_op jit(solution)/shard_map/ppermute | solution.py:388
  11.4 1.2 %collective-permute-start.3 = (bf16[16,480]{1,0:T(8,128)(2,1)S(1)}, bf16[16,480]{1,0:T(8,128)(2,1)S(1)}, u32[]{:S(2)}, u32[]{:S(2)}) collective-permute-start(bf16[16,480]{1,0:T(8,128)(2,1)S(1)} %get-tuple-element.50.order_ref), channel_id=1, source_target_pairs={{0,24},{8,0},{16,8},{24,16},{1,25},{9,1},{17,9},{25,17},{2,26},{10... | collective-permute-start | bytes 46088 | tf_op jit(solution)/shard_map/ppermute | solution.py:388
  12.7 1.9 %stage.1 = (bf16[512,512]{1,0:T(8,128)(2,1)S(1)}, bf16[176,1024]{1,0:T(8,128)(2,1)S(1)}, bf16[4,512,256]{2,1,0:T(8,128)(2,1)S(1)}, bf16[4,256,256]{2,1,0:T(8,128...) custom-call(bf16[16,480]{1,0:T(8,128)(2,1)S(1)} %get-tuple-element.5, ...), custom_call_target="tpu_custom_call" | custom-call | tf_op jit(solution)/shard_map/stage/pallas_call | solution.py:444
  14.5 0.6 %collective-permute-done.3.from_right_ref = bf16[16,480]{1,0:T(8,128)(2,1)S(1)} collective-permute-done((bf16[16,480]{1,0:T(8,128)(2,1)S(1)}, bf16[16,480]{1,0:T(8,128)(2,1)S(1)}, u32[]{:S(2)}, u32[]{:S(2)}) %collective-permute-start.3) | collective-permute-done | bytes 15392 | tf_op jit(solution)/shard_map/ppermute | solution.py:388
  15.2 0.8 %pack_second.1 = (bf16[232,128]{1,0:T(8,128)(2,1)S(1)}, bf16[232,128]{1,0:T(8,128)(2,1)S(1)}, bf16[232,128]{1,0:T(8,128)(2,1)S(1)}, bf16[232,128]{1,0:T(8,128)(2,1)S(1)}) custom-call(bf16[480,512]{1,0:T(8,128)(2,1)S(1)} %get-tuple-element.57.raw_ref, bf16[480,512]{1,0:T(8,128)(2,1)S(1)} %collective-permute-done.other_ref, ...), custom_call_target="tpu_custom_call" | custom-call | tf_op jit(solution)/shard_map/pack_second/pallas_call | solution.py:454
  16.0 0.3 %collective-permute-done.4.refs_2_ = bf16[200,384]{1,0:T(8,128)(2,1)S(1)} collective-permute-done((bf16[200,384]{1,0:T(8,128)(2,1)S(1)}, bf16[200,384]{1,0:T(8,128)(2,1)S(1)}, u32[]{:S(2)}, u32[]{:S(2)}) %collective-permute-start.4) | collective-permute-done | bytes 153632 | tf_op jit(solution)/shard_map/ppermute | solution.py:382
  16.3 0.7 %collective-permute-start.5 = (bf16[232,128]{1,0:T(8,128)(2,1)S(1)}, bf16[232,128]{1,0:T(8,128)(2,1)S(1)}, u32[]{:S(2)}, u32[]{:S(2)}) collective-permute-start(bf16[232,128]{1,0:T(8,128)(2,1)S(1)} %get-tuple-element.67), channel_id=1, source_target_pairs={{0,2},{1,3},{2,0},{3,1},{4,6},{5,7},{6,4},{7,5},{8,10},{9,11},{10,... | collective-permute-start | bytes 178184 | tf_op jit(solution)/shard_map/ppermute | solution.py:382
  17.0 3.6 %collective-permute-start.6 = (bf16[232,128]{1,0:T(8,128)(2,1)S(1)}, bf16[232,128]{1,0:T(8,128)(2,1)S(1)}, u32[]{:S(2)}, u32[]{:S(2)}) collective-permute-start(bf16[232,128]{1,0:T(8,128)(2,1)S(1)} %get-tuple-element.68), channel_id=1, source_target_pairs={{0,4},{1,5},{2,6},{3,7},{4,0},{5,1},{6,2},{7,3},{8,12},{9,13},{10,... | collective-permute-start | bytes 178184 | tf_op jit(solution)/shard_map/ppermute | solution.py:382
  20.6 0.1 collective-permute-start.7
  20.7 0.0 collective-permute-done.8.refs_1_
  20.7 2.8 %first_half.1 = (f32[512,512]{1,0:T(8,128)S(1)}, f32[176,384]{1,0:T(8,128)S(1)}) custom-call(bf16[512,512]{1,0:T(8,128)(2,1)S(1)} %get-tuple-element.51.rowscan_ref, bf16[176,1024]{1,0:T(8,128)(2,1)S(1)} %get-tuple-element.52.level_ref, bf16[4,512,256]{2,1,0:T(8,128)(2,1)S(1)} %get-tuple-element.70.column_ref, ...), custom_call_target="tpu_custom_call" | custom-call | tf_op jit(solution)/shard_map/first_half/pallas_call | solution.py:464
  23.6 3.2 %collective-permute-done.6.refs_4_ = bf16[232,128]{1,0:T(8,128)(2,1)S(1)} collective-permute-done((bf16[232,128]{1,0:T(8,128)(2,1)S(1)}, bf16[232,128]{1,0:T(8,128)(2,1)S(1)}, u32[]{:S(2)}, u32[]{:S(2)}) %collective-permute-start.6) | collective-permute-done | bytes 59424 | tf_op jit(solution)/shard_map/ppermute | solution.py:382
  26.7 0.0 collective-permute-done.7.refs_5_
  26.7 2.6 %second_half.1 = (bf16[16,32,512]{2,1,0:T(8,128)(2,1)}, bf16[8,16,256]{2,1,0:T(8,128)(2,1)}, bf16[4,8,128]{2,1,0:T(8,128)(2,1)}) custom-call(bf16[512,512]{1,0:T(8,128)(2,1)S(1)} %get-tuple-element.51.rowscan_ref, bf16[176,1024]{1,0:T(8,128)(2,1)S(1)} %get-tuple-element.52.level_ref, bf16[4,256,256]{2,1,0:T(8,128)(2,1)S(1)} %get-tuple-element.53.column_ref, ...), custom_call_target="tpu_custom_call" | custom-call | tf_op jit(solution)/shard_map/second_half/pallas_call | solution.py:480
  (4 shorter events, 0.0 us)
Async XLA Ops:
  0.6 0.7 %copy-start = (s32[4]{0:T(128)S(1)}, s32[4]{0:T(128)}, u32[]{:S(2)}) copy-start(s32[4]{0:T(128)} %shear_ref.1) | copy-start | bytes 52
  0.6 2.7 %collective-permute-start = (bf16[480,512]{1,0:T(8,128)(2,1)}, bf16[480,512]{1,0:T(8,128)(2,1)S(1)}, u32[]{:S(2)}, u32[]{:S(2)}) collective-permute-start(bf16[480,512]{1,0:T(8,128)(2,1)} %bitcast.1), channel_id=1, source_target_pairs={{0,1},{1,0},{2,3},{3,2},{4,5},{5,4},{6,7},{7,6},{8,9},{9,8},{10,11... | collective-permute-start | bytes 1474568 | tf_op jit(solution)/shard_map/ppermute | solution.py:400
  1.3 2.0 %collective-permute-start.1 = (s32[4]{0:T(128)S(1)}, s32[4]{0:T(128)S(1)}, u32[]{:S(2)}, u32[]{:S(2)}) collective-permute-start(s32[4]{0:T(128)S(1)} %copy-done), channel_id=1, source_target_pairs={{0,1},{1,0},{2,3},{3,2},{4,5},{5,4},{6,7},{7,6},{8,9},{9,8},{10,11... | collective-permute-start | bytes 56 | tf_op jit(solution)/shard_map/ppermute | solution.py:401
  4.5 11.8 %collective-permute-start.4 = (bf16[200,384]{1,0:T(8,128)(2,1)S(1)}, bf16[200,384]{1,0:T(8,128)(2,1)S(1)}, u32[]{:S(2)}, u32[]{:S(2)}) collective-permute-start(bf16[200,384]{1,0:T(8,128)(2,1)S(1)} %get-tuple-element.65), channel_id=1, source_target_pairs={{0,4},{1,5},{2,6},{3,7},{4,0},{5,1},{6,2},{7,3},{8,12},{9,13},{10,... | collective-permute-start | bytes 460808 | tf_op jit(solution)/shard_map/ppermute | solution.py:382
  8.2 12.6 %collective-permute-start.8 = (bf16[200,384]{1,0:T(8,128)(2,1)S(1)}, bf16[200,384]{1,0:T(8,128)(2,1)S(1)}, u32[]{:S(2)}, u32[]{:S(2)}) collective-permute-start(bf16[200,384]{1,0:T(8,128)(2,1)S(1)} %get-tuple-element.73), channel_id=1, source_target_pairs={{0,2},{1,3},{2,0},{3,1},{4,6},{5,7},{6,4},{7,5},{8,10},{9,11},{10,... | collective-permute-start | bytes 460808 | tf_op jit(solution)/shard_map/ppermute | solution.py:382
  9.7 11.0 %collective-permute-start.9 = (bf16[200,384]{1,0:T(8,128)(2,1)S(1)}, bf16[200,384]{1,0:T(8,128)(2,1)S(1)}, u32[]{:S(2)}, u32[]{:S(2)}) collective-permute-start(bf16[200,384]{1,0:T(8,128)(2,1)S(1)} %get-tuple-element.75), channel_id=1, source_target_pairs={{0,6},{1,7},{2,4},{3,5},{4,2},{5,3},{6,0},{7,1},{8,14},{9,15},{10,... | collective-permute-start | bytes 460808 | tf_op jit(solution)/shard_map/ppermute | solution.py:382
  9.7 4.8 %collective-permute-start.2 = (bf16[16,480]{1,0:T(8,128)(2,1)S(1)}, bf16[16,480]{1,0:T(8,128)(2,1)S(1)}, u32[]{:S(2)}, u32[]{:S(2)}) collective-permute-start(bf16[16,480]{1,0:T(8,128)(2,1)S(1)} %get-tuple-element.60), channel_id=1, source_target_pairs={{0,8},{8,16},{16,24},{24,0},{1,9},{9,17},{17,25},{25,1},{2,10},{10... | collective-permute-start | bytes 46088 | tf_op jit(solution)/shard_map/ppermute | solution.py:388
  11.4 3.7 %collective-permute-start.3 = (bf16[16,480]{1,0:T(8,128)(2,1)S(1)}, bf16[16,480]{1,0:T(8,128)(2,1)S(1)}, u32[]{:S(2)}, u32[]{:S(2)}) collective-permute-start(bf16[16,480]{1,0:T(8,128)(2,1)S(1)} %get-tuple-element.50.order_ref), channel_id=1, source_target_pairs={{0,24},{8,0},{16,8},{24,16},{1,25},{9,1},{17,9},{25,17},{2,26},{10... | collective-permute-start | bytes 46088 | tf_op jit(solution)/shard_map/ppermute | solution.py:388
  16.3 7.2 %collective-permute-start.5 = (bf16[232,128]{1,0:T(8,128)(2,1)S(1)}, bf16[232,128]{1,0:T(8,128)(2,1)S(1)}, u32[]{:S(2)}, u32[]{:S(2)}) collective-permute-start(bf16[232,128]{1,0:T(8,128)(2,1)S(1)} %get-tuple-element.67), channel_id=1, source_target_pairs={{0,2},{1,3},{2,0},{3,1},{4,6},{5,7},{6,4},{7,5},{8,10},{9,11},{10,... | collective-permute-start | bytes 178184 | tf_op jit(solution)/shard_map/ppermute | solution.py:382
  17.0 9.7 %collective-permute-start.6 = (bf16[232,128]{1,0:T(8,128)(2,1)S(1)}, bf16[232,128]{1,0:T(8,128)(2,1)S(1)}, u32[]{:S(2)}, u32[]{:S(2)}) collective-permute-start(bf16[232,128]{1,0:T(8,128)(2,1)S(1)} %get-tuple-element.68), channel_id=1, source_target_pairs={{0,4},{1,5},{2,6},{3,7},{4,0},{5,1},{6,2},{7,3},{8,12},{9,13},{10,... | collective-permute-start | bytes 178184 | tf_op jit(solution)/shard_map/ppermute | solution.py:382
  20.6 6.1 %collective-permute-start.7 = (bf16[232,128]{1,0:T(8,128)(2,1)S(1)}, bf16[232,128]{1,0:T(8,128)(2,1)S(1)}, u32[]{:S(2)}, u32[]{:S(2)}) collective-permute-start(bf16[232,128]{1,0:T(8,128)(2,1)S(1)} %get-tuple-element.69), channel_id=1, source_target_pairs={{0,6},{1,7},{2,4},{3,5},{4,2},{5,3},{6,0},{7,1},{8,14},{9,15},{10,... | collective-permute-start | bytes 178184 | tf_op jit(solution)/shard_map/ppermute | solution.py:382

commit v9 on v8

--- a/solution.py
+++ b/solution.py
@@ -18,6 +18,7 @@
 SLOTS = PLACED + 8
 LEVEL = 11
 LANE = 128
+BLOCK = 48
 F32 = jnp.float32
 BF16 = jnp.bfloat16
 
@@ -43,15 +44,15 @@
     return [high, (table - high.astype(np.float64)).astype(ml_dtypes.bfloat16)]
 
 
-def row_scan_table(row_band, scan_band, groups, early=None):
+def row_scan_table(row_band, scan_band, early=None):
     rows_out, rows_in = row_band.shape
-    scans_out = scan_band.shape[0]
+    scans_out, groups = scan_band.shape[0], scan_band.shape[1] // 4
     scans = scan_band.reshape(scans_out, groups, 4)
     table = np.zeros((rows_out, scans_out, groups, LANE))
     table[..., :PLACED] = np.einsum("yr,sgp->ysgrp", row_band, scans).reshape(rows_out, scans_out, groups, PLACED)
     if early is not None:
         for group in range(groups):
-            start = PLACED + 4 * (group & 1)
+            start = PLACED + 4 * (~group & 1)
             table[:, :, group, start : start + 4] = early[:, None, None] * scans[:, group]
     return table.reshape(rows_out * scans_out, groups * LANE)
 
@@ -68,30 +69,30 @@
     rowscan, column_first, column_last = [], [], []
     for sigma, sign in ((1.0, 1.0), (1.6, -1.0)):
         taps = gauss_taps(sigma)
-        rowscan += two_parts(row_scan_table(band(taps, row_in, own), band(taps, near, block), 4))
+        rowscan += two_parts(row_scan_table(band(taps, row_in, own), band(taps, near, block)))
         column_first += two_parts(sign * band(taps, np.arange(4 * LANE) - LANE, np.arange(2 * LANE)).T)
         column_last += two_parts(sign * band(taps, last, touched).T)
     level_rows = 2 * np.arange(LEVEL) - 4
-    level_scans = 2 * np.arange(scans // 2)
     early = np.arange(LEVEL) == 0
     level = row_scan_table(
-        band(BINOMIAL, row_in, level_rows) * ~early[:, None],
-        band(BINOMIAL, np.arange(scans), level_scans),
-        scans // 4,
-        early * 1.0,
+        band(BINOMIAL, row_in, level_rows) * ~early[:, None], band(BINOMIAL, near, 2 * np.arange(4)), early * 1.0
     )
+    level = np.pad(level, ((0, BLOCK - 4 * LEVEL), (0, 0))).astype(ml_dtypes.bfloat16)
     edges = np.array([-4, -2, columns, columns + 2])
     targets = np.concatenate([2 * np.arange(columns // 2), edges])
     two = np.einsum(
-        "yr,sp->ysrp",
+        "yr,sbp->ysbrp",
         band(BINOMIAL, np.arange(LEVEL) - 2, 2 * np.arange(4)),
-        band(BINOMIAL, np.arange(scans // 2), 2 * np.arange(scans // 4)),
-    ).reshape(scans, LEVEL * scans // 2)
+        band(BINOMIAL, np.arange(scans // 2), 2 * np.arange(scans // 4)).reshape(scans // 4, scans // 8, 4),
+    ).reshape(scans, scans // 8, 4 * LEVEL)
+    two = np.pad(two, ((0, 0), (0, 0), (0, BLOCK - 4 * LEVEL))).reshape(scans, scans // 8 * BLOCK)
+    row, scan = np.divmod(np.arange(SLAB_ROWS // 2 * scans // 2), scans // 2)
+    order = np.arange(scans // 8 * BLOCK)[None, :] == (scan // 4 * BLOCK + 4 * (row + 2) + scan % 4)[:, None]
     fill = ((0, 0), (0, LANE - 4))
     small = ml_dtypes.bfloat16
     return dict(
-        rowscan=np.concatenate(rowscan, 0),
-        level=level.astype(small),
+        rowscan=np.concatenate(rowscan + [level], 0),
+        order=order.astype(small),
         column_first=np.stack(column_first),
         column_last=np.stack(column_last),
         level_first=np.pad(band(BINOMIAL, np.arange(cut), targets).T, fill).astype(small),
@@ -215,7 +216,7 @@
     right = jnp.where(tile < lax.axis_size("tile") - 1, from_right_ref[...].astype(F32), 0.0)
     left = jnp.where(tile > 0, from_left_ref[...].astype(F32), 0.0)
     for step, out_ref in enumerate(out_refs):
-        total = 0.0
+        total, placed = 0.0, []
         for owner, (planes_ref, shifts_ref) in enumerate(((raw_ref, shift_ref), (other_ref, other_shift_ref))):
             rows, early = place_table(shifts_ref[:, :1], slab ^ (2 * step), camera, (slab & 1) ^ owner)
             planes = planes_ref[:, columns - LANE :]
@@ -223,12 +224,13 @@
             total = total + dot(early, planes)
             own = slice(8 * owner, 8 * owner + 8)
             strips = jnp.concatenate([right[own], left[own]], 0).astype(BF16)
-            start = 2 * PLACED + 8 + 16 * owner
             table = jnp.concatenate(
                 [rows.astype(F32), early.astype(F32), jnp.zeros((LANE - SLOTS, rows.shape[1]), F32)], 0
             )
-            out_ref[start : start + 16, :] = dot_rows(strips, table.astype(BF16)).astype(BF16)
+            columns_of = dot_rows(strips, table.astype(BF16))
+            placed += [columns_of[:STRIP], columns_of[16 - STRIP :]]
         out_ref[2 * PLACED : 2 * PLACED + 8, :] = total.astype(BF16)
+        out_ref[2 * PLACED + 8 :, :] = jnp.concatenate(placed, 0).astype(BF16)
 
 
 def collect(in_refs, volume, scans):
@@ -251,7 +253,7 @@
     return high, (value - high.astype(F32)).astype(BF16)
 
 
-def row_scan(rowscan_ref, volume, block, wide):
+def row_scan(rowscan_ref, volume, block, wide, rough):
     rows = 8 * SLAB_ROWS
     both = dot(rowscan_ref[...], volume[2 * block : 2 * block + 4].reshape(4 * LANE, volume.shape[-1]))
     for sigma in range(2):
@@ -259,6 +261,7 @@
         high, low = split(total)
         wide[2 * sigma, block * rows : (block + 1) * rows, :] = high
         wide[2 * sigma + 1, block * rows : (block + 1) * rows, :] = low
+    rough[block * BLOCK : (block + 1) * BLOCK, :] = both[4 * rows :]
 
 
 def dot_parts(high, low, right):
@@ -280,28 +283,27 @@
     return total
 
 
-def level_part(level_ref, level_column_ref, volume, scans):
-    groups = scans // 4
-    high, low = split(dot(level_ref[...], volume[1 : groups + 1].reshape(groups * LANE, volume.shape[-1])))
+def level_part(rough, level_column_ref):
+    high, low = split(rough[...])
     return dot_parts(high, low, level_column_ref[...])
 
 
-def first_half(count, scans, rowscan_ref, level_ref, column_ref, level_column_ref, *refs):
-    in_refs, (partial_ref, coarse_ref, volume, wide) = refs[:count], refs[count:]
+def first_half(count, scans, rowscan_ref, column_ref, level_column_ref, *refs):
+    in_refs, (partial_ref, coarse_ref, volume, wide, rough) = refs[:count], refs[count:]
     collect(in_refs, volume, scans)
     for block in range(scans // 8):
-        row_scan(rowscan_ref, volume, block, wide)
+        row_scan(rowscan_ref, volume, block, wide, rough)
     cut = wide.shape[-1]
     for start in range(0, partial_ref.shape[1], 2 * LANE):
         low, high = max(start - LANE, 0), min(start + 3 * LANE, cut)
         taken = slice(low - start + LANE, high - start + LANE)
         partial_ref[:, start : start + 2 * LANE] = across(wide, slice(None), slice(low, high), column_ref, taken)
-    coarse_ref[...] = level_part(level_ref, level_column_ref, volume, scans)
-
-
-def second_half(count, scans, rowscan_ref, level_ref, column_ref, level_column_ref, two_ref, two_column_ref, *refs):
+    coarse_ref[...] = level_part(rough, level_column_ref)
+
+
+def second_half(count, scans, rowscan_ref, order_ref, column_ref, level_column_ref, two_ref, two_column_ref, *refs):
     partial_ref, coarse_ref, *in_refs = refs[: 2 + count]
-    difference_ref, one_ref, second_ref, volume, strips, wide, held, held_one, held_second, sems = refs[2 + count :]
+    difference_ref, one_ref, second_ref, volume, strips, wide, rough, held, held_one, held_second, sems = refs[2 + count :]
     slab = lax.axis_index("slab")
     slabs = lax.axis_size("slab")
     tile = lax.axis_index("tile")
@@ -312,11 +314,13 @@
     collect(in_refs, volume, scans)
     for index in range(groups):
         place = pl.multiple_of((slab ^ index) * LANE, LANE)
-        start = 2 * PLACED + 8 + 16 * (index & 1)
-        strips[:, pl.ds(place, LANE)] = in_refs[index >> 1][start : start + 16, :]
+        start = 2 * STRIP * (index & 1)
+        both = in_refs[index >> 1][2 * PLACED + 8 :, :].astype(F32)[start : start + 2 * STRIP]
+        both = jnp.concatenate([both, jnp.zeros((16 - 2 * STRIP, LANE), F32)], 0)
+        strips[:, pl.ds(place, LANE)] = both.astype(BF16)
     line = lax.broadcasted_iota(jnp.int32, (16, LANE), 0)
     lane = lax.broadcasted_iota(jnp.int32, (16, LANE), 1)
-    spread = jnp.where(lane == jnp.where(line < 8, line, line + LANE - 16), 1.0, 0.0).astype(BF16)
+    spread = jnp.where(lane == jnp.where(line < STRIP, line, line + LANE - 2 * STRIP), 1.0, 0.0).astype(BF16)
     rim = lax.dot_general(strips[...], spread, (((0,), (0,)), ((), ())), preferred_element_type=F32)
     volume[1 : groups + 1, :, LANE:] = rim.astype(BF16).reshape(groups, LANE, LANE)
 
@@ -325,7 +329,7 @@
     left = lax.broadcasted_iota(jnp.int32, (2 * rows, LANE), 1) < LANE // 2
     for pair in range(scans // 16):
         for block in (2 * pair, 2 * pair + 1):
-            row_scan(rowscan_ref, volume, block, wide)
+            row_scan(rowscan_ref, volume, block, wide, rough)
         here = slice(2 * pair * rows, 2 * (pair + 1) * rows)
         late = across(wide, here, slice(None), column_ref, slice(None))
         ends = late[:, LANE:]
@@ -345,21 +349,23 @@
         )
         copy.start()
         copies.append(copy)
-    level = coarse_ref[...] + level_part(level_ref, level_column_ref, volume, scans)
+    level = coarse_ref[...] + level_part(rough, level_column_ref)
     half = columns // 2
-    shape = (LEVEL, scans // 2, level.shape[-1])
-    level = level.reshape(shape)
-    row = slab * (SLAB_ROWS // 2) - 2 + lax.broadcasted_iota(jnp.int32, shape, 0)
-    place = lax.broadcasted_iota(jnp.int32, shape, 2) - half
+    row = lax.broadcasted_iota(jnp.int32, level.shape, 0)
+    within = row
+    for block in range(1, scans // 8):
+        within = within - jnp.where(row >= block * BLOCK, BLOCK, 0)
+    row = slab * (SLAB_ROWS // 2) - 2 + (within >> 2)
+    place = lax.broadcasted_iota(jnp.int32, level.shape, 1) - half
     keep = (row >= 0) & (row < slabs * (SLAB_ROWS // 2))
     keep = keep & ((place < 0) | (place >= 2) | (tile > 0)) & ((place < 2) | (tile < tiles - 1))
     ready = jnp.where(keep, level, 0.0).astype(BF16)
-    held_one[...] = ready[2:10, :, :half]
+    held_one[...] = dot(order_ref[...], ready[:, :half]).reshape(held_one.shape).astype(BF16)
     copy = pltpu.make_async_copy(held_one, one_ref, sems.at[scans // 16])
     copy.start()
     copies.append(copy)
 
-    high, low = split(dot(two_ref[...], ready.reshape(LEVEL * scans // 2, level.shape[-1])))
+    high, low = split(dot(two_ref[...], ready))
     second = dot_parts(high, low, two_column_ref[...])
     held_second[...] = second.reshape(second_ref.shape).astype(BF16)
     copy = pltpu.make_async_copy(held_second, second_ref, sems.at[scans // 16 + 1])
@@ -439,7 +445,7 @@
     got_first = along(chunks, slabs)
     from_left = shifted(toward_right, 1)
     from_right = shifted(toward_left, -1)
-    second = jax.ShapeDtypeStruct((2 * PLACED + 40, LANE), BF16)
+    second = jax.ShapeDtypeStruct((2 * PLACED + 8 + 4 * STRIP, LANE), BF16)
     names = list(table)
     staged = pl.pallas_call(
         stage,
@@ -465,17 +471,18 @@
         functools.partial(first_half, pairs, scans),
         out_shape=[
             jax.ShapeDtypeStruct((scans * SLAB_ROWS, columns), F32),
-            jax.ShapeDtypeStruct((LEVEL * scans // 2, columns // 2 + LANE), F32),
+            jax.ShapeDtypeStruct((scans // 8 * BLOCK, columns // 2 + LANE), F32),
         ],
-        in_specs=[VECTOR] * (4 + pairs),
+        in_specs=[VECTOR] * (3 + pairs),
         out_specs=[VECTOR] * 2,
         scratch_shapes=[
             pltpu.VMEM((slabs + 2, LANE, cut), BF16),
             pltpu.VMEM((4, scans * SLAB_ROWS, cut), BF16),
+            pltpu.VMEM((scans // 8 * BLOCK, cut), F32),
         ],
         compiler_params=PARAMS,
         name="first_half",
-    )(table["rowscan"], table["level"], table["column_first"], table["level_first"], *got_first)
+    )(table["rowscan"], table["column_first"], table["level_first"], *got_first)
     got_second, partial = lax.optimization_barrier((got_second, partial))
     return pl.pallas_call(
         functools.partial(second_half, pairs, scans),
@@ -490,6 +497,7 @@
             pltpu.VMEM((slabs + 2, LANE, 2 * LANE), BF16),
             pltpu.VMEM((16, slabs * LANE), BF16),
             pltpu.VMEM((4, scans * SLAB_ROWS, 2 * LANE), BF16),
+            pltpu.VMEM((scans // 8 * BLOCK, 2 * LANE), F32),
             pltpu.VMEM((SLAB_ROWS, scans, columns), BF16),
             pltpu.VMEM((SLAB_ROWS // 2, scans // 2, columns // 2), BF16),
             pltpu.VMEM((SLAB_ROWS // 4, scans // 4, columns // 4), BF16),
@@ -499,7 +507,7 @@
         name="second_half",
     )(
         table["rowscan"],
-        table["level"],
+        table["order"],
         table["column_last"],
         table["level_last"],
         table["two"],

time: 29.7 us -> 29.5 us (level)
  Pallas kernels: 10.9 us -> 10.6 us
  transfers between devices with their start and end apart: 10 -> 10, of which waited for: 3 -> 4; matrix products, arithmetic and copies ran while one was open for 0% -> 0% of each run, Pallas kernels for 24% -> 24%
where the time goes in v9:
time: 29.5 us; the launch traced here: 29.2 us
  starting transfers between devices  13.5 us (46%)
  Pallas kernels  10.6 us (36%)
  waiting for transfers between devices  4.25 us (14%)
  between operations  0.71 us (2%)
    ppermute x6, starting transfers between devices, along(): lax.ppermute(chunks[step], 'slab', [(i, i ^ 2 * step) for i in range(slab...  9.61 us
    ppermute x6, waiting for transfers between devices, along(): lax.ppermute(chunks[step], 'slab', [(i, i ^ 2 * step) for i in range(slab...  3.53 us
    ppermute x2, starting transfers between devices, shifted(): lax.ppermute(block, 'tile', [(i, (i + distance) % count) for i in range(c...  2.92 us
    pallas_call x1, Pallas kernels, body(): pl.pallas_call(functools.partial(first_half, pairs, scans), out_shape=[ja...  2.75 us
    pallas_call x1, Pallas kernels, body(): pl.pallas_call(functools.partial(second_half, pairs, scans), out_shape=[j...  2.53 us
    pallas_call x1, Pallas kernels, body(): pl.pallas_call(stage, out_shape=[jax.ShapeDtypeStruct(table[name].shape,...  1.79 us
    pallas_call x1, Pallas kernels, body(): pl.pallas_call(pack_own, out_shape=[jax.ShapeDtypeStruct((planes * camera...  1.56 us
    pallas_call x1, Pallas kernels, body(): pl.pallas_call(pack_other, out_shape=[strip, strip, shift] + [jax.ShapeDt...  1.17 us
  transfers between devices with their start and end apart: 10, of which 4 were waited for; matrix products, arithmetic and copies ran while one was open for 0% of the time, Pallas kernels for 24%

profile of v9, /device:TPU:0, one launch (start us, length us, event | category | flops | bytes accessed | tf_op | source)
XLA Modules:
  0.0 29.2 jit_solution(18226722828497712799)
XLA Ops:
  0.6 0.5 %collective-permute-start = (bf16[480,512]{1,0:T(8,128)(2,1)}, bf16[480,512]{1,0:T(8,128)(2,1)S(1)}, u32[]{:S(2)}, u32[]{:S(2)}) collective-permute-start(bf16[480,512]{1,0:T(8,128)(2,1)} %bitcast.1), channel_id=1, source_target_pairs={{0,1},{1,0},{2,3},{3,2},{4,5},{5,4},{6,7},{7,6},{8,9},{9,8},{10,11... | collective-permute-start | bytes 1474568 | tf_op jit(solution)/shard_map/ppermute | solution.py:406
  1.2 0.1 copy-done
  1.3 0.5 %collective-permute-start.1 = (s32[4]{0:T(128)S(1)}, s32[4]{0:T(128)S(1)}, u32[]{:S(2)}, u32[]{:S(2)}) collective-permute-start(s32[4]{0:T(128)S(1)} %copy-done), channel_id=1, source_target_pairs={{0,1},{1,0},{2,3},{3,2},{4,5},{5,4},{6,7},{7,6},{8,9},{9,8},{10,11... | collective-permute-start | bytes 56 | tf_op jit(solution)/shard_map/ppermute | solution.py:407
  1.7 1.6 %pack_own.1 = (bf16[480,512]{1,0:T(8,128)(2,1)S(1)}, s32[128,128]{1,0:T(8,128)S(1)}, bf16[16,512]{1,0:T(8,128)(2,1)S(1)}, f32[16,480]{1,0:T(8,128)S(1)}, f32[4,8...) custom-call(bf16[480,512]{1,0:T(8,128)(2,1)} %bitcast.2, ...), custom_call_target="tpu_custom_call" | custom-call | tf_op jit(solution)/shard_map/pack_own/pallas_call | solution.py:411
  3.3 0.0 collective-permute-done.1.shear_ref
  3.3 0.0 collective-permute-done.other_ref
  3.3 1.2 %pack_other.1 = (bf16[16,480]{1,0:T(8,128)(2,1)S(1)}, bf16[16,480]{1,0:T(8,128)(2,1)S(1)}, s32[128,128]{1,0:T(8,128)S(1)}, bf16[200,384]{1,0:T(8,128)(2,1)S(1)},...) custom-call(bf16[480,512]{1,0:T(8,128)(2,1)S(1)} %collective-permute-done.other_ref, ...), custom_call_target="tpu_custom_call" | custom-call | tf_op jit(solution)/shard_map/pack_other/pallas_call | solution.py:432
  4.5 3.7 %collective-permute-start.4 = (bf16[200,384]{1,0:T(8,128)(2,1)S(1)}, bf16[200,384]{1,0:T(8,128)(2,1)S(1)}, u32[]{:S(2)}, u32[]{:S(2)}) collective-permute-start(bf16[200,384]{1,0:T(8,128)(2,1)S(1)} %get-tuple-element.65), channel_id=1, source_target_pairs={{0,4},{1,5},{2,6},{3,7},{4,0},{5,1},{6,2},{7,3},{8,12},{9,13},{10,... | collective-permute-start | bytes 460808 | tf_op jit(solution)/shard_map/ppermute | solution.py:388
  8.2 1.6 %collective-permute-start.8 = (bf16[200,384]{1,0:T(8,128)(2,1)S(1)}, bf16[200,384]{1,0:T(8,128)(2,1)S(1)}, u32[]{:S(2)}, u32[]{:S(2)}) collective-permute-start(bf16[200,384]{1,0:T(8,128)(2,1)S(1)} %get-tuple-element.73), channel_id=1, source_target_pairs={{0,2},{1,3},{2,0},{3,1},{4,6},{5,7},{6,4},{7,5},{8,10},{9,11},{10,... | collective-permute-start | bytes 460808 | tf_op jit(solution)/shard_map/ppermute | solution.py:388
  9.7 0.0 collective-permute-start.9
  9.7 1.7 %collective-permute-start.2 = (bf16[16,480]{1,0:T(8,128)(2,1)S(1)}, bf16[16,480]{1,0:T(8,128)(2,1)S(1)}, u32[]{:S(2)}, u32[]{:S(2)}) collective-permute-start(bf16[16,480]{1,0:T(8,128)(2,1)S(1)} %get-tuple-element.60), channel_id=1, source_target_pairs={{0,8},{8,16},{16,24},{24,0},{1,9},{9,17},{17,25},{25,1},{2,10},{10... | collective-permute-start | bytes 46088 | tf_op jit(solution)/shard_map/ppermute | solution.py:394
  11.4 1.2 %collective-permute-start.3 = (bf16[16,480]{1,0:T(8,128)(2,1)S(1)}, bf16[16,480]{1,0:T(8,128)(2,1)S(1)}, u32[]{:S(2)}, u32[]{:S(2)}) collective-permute-start(bf16[16,480]{1,0:T(8,128)(2,1)S(1)} %get-tuple-element.50.order_ref), channel_id=1, source_target_pairs={{0,24},{8,0},{16,8},{24,16},{1,25},{9,1},{17,9},{25,17},{2,26},{10... | collective-permute-start | bytes 46088 | tf_op jit(solution)/shard_map/ppermute | solution.py:394
  12.7 1.8 %stage.1 = (bf16[560,512]{1,0:T(8,128)(2,1)S(1)}, bf16[128,192]{1,0:T(8,128)(2,1)S(1)}, bf16[4,512,256]{2,1,0:T(8,128)(2,1)S(1)}, bf16[4,256,256]{2,1,0:T(8,128)...) custom-call(bf16[16,480]{1,0:T(8,128)(2,1)S(1)} %get-tuple-element.5, ...), custom_call_target="tpu_custom_call" | custom-call | tf_op jit(solution)/shard_map/stage/pallas_call | solution.py:450
  14.5 0.0 collective-permute-done.2.from_left_ref
  14.5 0.7 %collective-permute-done.3.from_right_ref = bf16[16,480]{1,0:T(8,128)(2,1)S(1)} collective-permute-done((bf16[16,480]{1,0:T(8,128)(2,1)S(1)}, bf16[16,480]{1,0:T(8,128)(2,1)S(1)}, u32[]{:S(2)}, u32[]{:S(2)}) %collective-permute-start.3) | collective-permute-done | bytes 15392 | tf_op jit(solution)/shard_map/ppermute | solution.py:394
  15.2 0.8 %pack_second.1 = (bf16[224,128]{1,0:T(8,128)(2,1)S(1)}, bf16[224,128]{1,0:T(8,128)(2,1)S(1)}, bf16[224,128]{1,0:T(8,128)(2,1)S(1)}, bf16[224,128]{1,0:T(8,128)(2,1)S(1)}) custom-call(bf16[480,512]{1,0:T(8,128)(2,1)S(1)} %get-tuple-element.57.raw_ref, bf16[480,512]{1,0:T(8,128)(2,1)S(1)} %collective-permute-done.other_ref, ...), custom_call_target="tpu_custom_call" | custom-call | tf_op jit(solution)/shard_map/pack_second/pallas_call | solution.py:460
  16.0 0.3 %collective-permute-done.4.refs_2_ = bf16[200,384]{1,0:T(8,128)(2,1)S(1)} collective-permute-done((bf16[200,384]{1,0:T(8,128)(2,1)S(1)}, bf16[200,384]{1,0:T(8,128)(2,1)S(1)}, u32[]{:S(2)}, u32[]{:S(2)}) %collective-permute-start.4) | collective-permute-done | bytes 153632 | tf_op jit(solution)/shard_map/ppermute | solution.py:388
  16.3 0.7 %collective-permute-start.5 = (bf16[224,128]{1,0:T(8,128)(2,1)S(1)}, bf16[224,128]{1,0:T(8,128)(2,1)S(1)}, u32[]{:S(2)}, u32[]{:S(2)}) collective-permute-start(bf16[224,128]{1,0:T(8,128)(2,1)S(1)} %get-tuple-element.67), channel_id=1, source_target_pairs={{0,2},{1,3},{2,0},{3,1},{4,6},{5,7},{6,4},{7,5},{8,10},{9,11},{10,... | collective-permute-start | bytes 172040 | tf_op jit(solution)/shard_map/ppermute | solution.py:388
  17.0 3.6 %collective-permute-start.6 = (bf16[224,128]{1,0:T(8,128)(2,1)S(1)}, bf16[224,128]{1,0:T(8,128)(2,1)S(1)}, u32[]{:S(2)}, u32[]{:S(2)}) collective-permute-start(bf16[224,128]{1,0:T(8,128)(2,1)S(1)} %get-tuple-element.68), channel_id=1, source_target_pairs={{0,4},{1,5},{2,6},{3,7},{4,0},{5,1},{6,2},{7,3},{8,12},{9,13},{10,... | collective-permute-start | bytes 172040 | tf_op jit(solution)/shard_map/ppermute | solution.py:388
  20.6 0.1 collective-permute-start.7
  20.7 2.7 %first_half.1 = (f32[512,512]{1,0:T(8,128)S(1)}, f32[192,384]{1,0:T(8,128)S(1)}) custom-call(bf16[560,512]{1,0:T(8,128)(2,1)S(1)} %get-tuple-element.51.rowscan_ref, bf16[4,512,256]{2,1,0:T(8,128)(2,1)S(1)} %get-tuple-element.70.column_ref, bf16[384,384]{1,0:T(8,128)(2,1)S(1)} %get-tuple-element.71.level_column_ref, ...), custom_call_target="tpu_custom_call" | custom-call | tf_op jit(solution)/shard_map/first_half/pallas_call | solution.py:470
  23.5 2.5 %collective-permute-done.6.refs_4_ = bf16[224,128]{1,0:T(8,128)(2,1)S(1)} collective-permute-done((bf16[224,128]{1,0:T(8,128)(2,1)S(1)}, bf16[224,128]{1,0:T(8,128)(2,1)S(1)}, u32[]{:S(2)}, u32[]{:S(2)}) %collective-permute-start.6) | collective-permute-done | bytes 57376 | tf_op jit(solution)/shard_map/ppermute | solution.py:388
  26.0 0.7 %collective-permute-done.7.refs_5_ = bf16[224,128]{1,0:T(8,128)(2,1)S(1)} collective-permute-done((bf16[224,128]{1,0:T(8,128)(2,1)S(1)}, bf16[224,128]{1,0:T(8,128)(2,1)S(1)}, u32[]{:S(2)}, u32[]{:S(2)}) %collective-permute-start.7) | collective-permute-done | bytes 57376 | tf_op jit(solution)/shard_map/ppermute | solution.py:388
  26.7 2.5 %second_half.1 = (bf16[16,32,512]{2,1,0:T(8,128)(2,1)}, bf16[8,16,256]{2,1,0:T(8,128)(2,1)}, bf16[4,8,128]{2,1,0:T(8,128)(2,1)}) custom-call(bf16[560,512]{1,0:T(8,128)(2,1)S(1)} %get-tuple-element.51.rowscan_ref, bf16[128,192]{1,0:T(8,128)(2,1)S(1)} %get-tuple-element.52.order_ref, bf16[4,256,256]{2,1,0:T(8,128)(2,1)S(1)} %get-tuple-element.53.column_ref, ...), custom_call_target="tpu_custom_call" | custom-call | tf_op jit(solution)/shard_map/second_half/pallas_call | solution.py:487
  (4 shorter events, 0.0 us)
Async XLA Ops:
  0.6 0.7 %copy-start = (s32[4]{0:T(128)S(1)}, s32[4]{0:T(128)}, u32[]{:S(2)}) copy-start(s32[4]{0:T(128)} %shear_ref.1) | copy-start | bytes 52
  0.6 2.7 %collective-permute-start = (bf16[480,512]{1,0:T(8,128)(2,1)}, bf16[480,512]{1,0:T(8,128)(2,1)S(1)}, u32[]{:S(2)}, u32[]{:S(2)}) collective-permute-start(bf16[480,512]{1,0:T(8,128)(2,1)} %bitcast.1), channel_id=1, source_target_pairs={{0,1},{1,0},{2,3},{3,2},{4,5},{5,4},{6,7},{7,6},{8,9},{9,8},{10,11... | collective-permute-start | bytes 1474568 | tf_op jit(solution)/shard_map/ppermute | solution.py:406
  1.3 2.0 %collective-permute-start.1 = (s32[4]{0:T(128)S(1)}, s32[4]{0:T(128)S(1)}, u32[]{:S(2)}, u32[]{:S(2)}) collective-permute-start(s32[4]{0:T(128)S(1)} %copy-done), channel_id=1, source_target_pairs={{0,1},{1,0},{2,3},{3,2},{4,5},{5,4},{6,7},{7,6},{8,9},{9,8},{10,11... | collective-permute-start | bytes 56 | tf_op jit(solution)/shard_map/ppermute | solution.py:407
  4.5 11.8 %collective-permute-start.4 = (bf16[200,384]{1,0:T(8,128)(2,1)S(1)}, bf16[200,384]{1,0:T(8,128)(2,1)S(1)}, u32[]{:S(2)}, u32[]{:S(2)}) collective-permute-start(bf16[200,384]{1,0:T(8,128)(2,1)S(1)} %get-tuple-element.65), channel_id=1, source_target_pairs={{0,4},{1,5},{2,6},{3,7},{4,0},{5,1},{6,2},{7,3},{8,12},{9,13},{10,... | collective-permute-start | bytes 460808 | tf_op jit(solution)/shard_map/ppermute | solution.py:388
  8.2 12.6 %collective-permute-start.8 = (bf16[200,384]{1,0:T(8,128)(2,1)S(1)}, bf16[200,384]{1,0:T(8,128)(2,1)S(1)}, u32[]{:S(2)}, u32[]{:S(2)}) collective-permute-start(bf16[200,384]{1,0:T(8,128)(2,1)S(1)} %get-tuple-element.73), channel_id=1, source_target_pairs={{0,2},{1,3},{2,0},{3,1},{4,6},{5,7},{6,4},{7,5},{8,10},{9,11},{10,... | collective-permute-start | bytes 460808 | tf_op jit(solution)/shard_map/ppermute | solution.py:388
  9.7 11.0 %collective-permute-start.9 = (bf16[200,384]{1,0:T(8,128)(2,1)S(1)}, bf16[200,384]{1,0:T(8,128)(2,1)S(1)}, u32[]{:S(2)}, u32[]{:S(2)}) collective-permute-start(bf16[200,384]{1,0:T(8,128)(2,1)S(1)} %get-tuple-element.75), channel_id=1, source_target_pairs={{0,6},{1,7},{2,4},{3,5},{4,2},{5,3},{6,0},{7,1},{8,14},{9,15},{10,... | collective-permute-start | bytes 460808 | tf_op jit(solution)/shard_map/ppermute | solution.py:388
  9.7 4.7 %collective-permute-start.2 = (bf16[16,480]{1,0:T(8,128)(2,1)S(1)}, bf16[16,480]{1,0:T(8,128)(2,1)S(1)}, u32[]{:S(2)}, u32[]{:S(2)}) collective-permute-start(bf16[16,480]{1,0:T(8,128)(2,1)S(1)} %get-tuple-element.60), channel_id=1, source_target_pairs={{0,8},{8,16},{16,24},{24,0},{1,9},{9,17},{17,25},{25,1},{2,10},{10... | collective-permute-start | bytes 46088 | tf_op jit(solution)/shard_map/ppermute | solution.py:394
  11.4 3.7 %collective-permute-start.3 = (bf16[16,480]{1,0:T(8,128)(2,1)S(1)}, bf16[16,480]{1,0:T(8,128)(2,1)S(1)}, u32[]{:S(2)}, u32[]{:S(2)}) collective-permute-start(bf16[16,480]{1,0:T(8,128)(2,1)S(1)} %get-tuple-element.50.order_ref), channel_id=1, source_target_pairs={{0,24},{8,0},{16,8},{24,16},{1,25},{9,1},{17,9},{25,17},{2,26},{10... | collective-permute-start | bytes 46088 | tf_op jit(solution)/shard_map/ppermute | solution.py:394
  16.3 7.1 %collective-permute-start.5 = (bf16[224,128]{1,0:T(8,128)(2,1)S(1)}, bf16[224,128]{1,0:T(8,128)(2,1)S(1)}, u32[]{:S(2)}, u32[]{:S(2)}) collective-permute-start(bf16[224,128]{1,0:T(8,128)(2,1)S(1)} %get-tuple-element.67), channel_id=1, source_target_pairs={{0,2},{1,3},{2,0},{3,1},{4,6},{5,7},{6,4},{7,5},{8,10},{9,11},{10,... | collective-permute-start | bytes 172040 | tf_op jit(solution)/shard_map/ppermute | solution.py:388
  17.0 9.0 %collective-permute-start.6 = (bf16[224,128]{1,0:T(8,128)(2,1)S(1)}, bf16[224,128]{1,0:T(8,128)(2,1)S(1)}, u32[]{:S(2)}, u32[]{:S(2)}) collective-permute-start(bf16[224,128]{1,0:T(8,128)(2,1)S(1)} %get-tuple-element.68), channel_id=1, source_target_pairs={{0,4},{1,5},{2,6},{3,7},{4,0},{5,1},{6,2},{7,3},{8,12},{9,13},{10,... | collective-permute-start | bytes 172040 | tf_op jit(solution)/shard_map/ppermute | solution.py:388
  20.6 6.1 %collective-permute-start.7 = (bf16[224,128]{1,0:T(8,128)(2,1)S(1)}, bf16[224,128]{1,0:T(8,128)(2,1)S(1)}, u32[]{:S(2)}, u32[]{:S(2)}) collective-permute-start(bf16[224,128]{1,0:T(8,128)(2,1)S(1)} %get-tuple-element.69), channel_id=1, source_target_pairs={{0,6},{1,7},{2,4},{3,5},{4,2},{5,3},{6,0},{7,1},{8,14},{9,15},{10,... | collective-permute-start | bytes 172040 | tf_op jit(solution)/shard_map/ppermute | solution.py:388

commit v10 on v9

--- a/solution.py
+++ b/solution.py
@@ -170,7 +170,8 @@
     loads[0].wait()
     placed = dot(stack[...], kept_ref[:, : columns - LANE])
     for step, out_ref in enumerate(out_refs):
-        out_ref[...] = placed[step * LANE : step * LANE + PLACED].astype(BF16)
+        out_ref[:PLACED, :] = placed[step * LANE : step * LANE + PLACED].astype(BF16)
+        out_ref[PLACED:, :] = jnp.zeros((out_ref.shape[0] - PLACED, out_ref.shape[1]), BF16)
         early_ref[step] = placed[step * LANE + PLACED : step * LANE + SLOTS]
     strip_ref[...] = dot_rows(pick_ref[...], kept_ref[...])
 
@@ -178,14 +179,12 @@
 def pack_other(other_ref, shear_ref, pick_ref, strip_ref, early_ref, *refs):
     (shears, sem, stack), refs = refs[-3:], refs[:-3]
     pairs = (len(refs) - 3) // 2
-    own_refs, (right_ref, left_ref, shift_ref), out_refs = refs[:pairs], refs[pairs : pairs + 3], refs[pairs + 3 :]
+    (right_ref, left_ref, shift_ref), out_refs = refs[pairs : pairs + 3], refs[pairs + 3 :]
     load = pltpu.make_async_copy(shear_ref, shears, sem)
     load.start()
     camera = other_ref.shape[0] // 4
     columns = other_ref.shape[1]
     slab = lax.axis_index("slab")
-    for own_ref, out_ref in zip(own_refs, out_refs):
-        out_ref[:PLACED, :] = own_ref[...]
     strips = jnp.concatenate([strip_ref[...], dot_rows(pick_ref[...], other_ref[...])], 0)
     right_ref[...] = jnp.concatenate([strips[:8], strips[16:24]], 0).astype(BF16)
     left_ref[...] = jnp.concatenate([strips[8:16], strips[24:]], 0).astype(BF16)
@@ -327,23 +326,26 @@
     copies = []
     rows = 8 * SLAB_ROWS
     left = lax.broadcasted_iota(jnp.int32, (2 * rows, LANE), 1) < LANE // 2
+
+    def keep(pair, start, total):
+        total = total.reshape(2, SLAB_ROWS, 8, LANE)
+        joined = jnp.concatenate([total[0], total[1]], 1)
+        held[:, 16 * pair : 16 * pair + 16, start : start + LANE] = joined.astype(BF16)
+
+    for pair in range(scans // 16):
+        here = slice(2 * pair * rows, 2 * (pair + 1) * rows)
+        for start in range(LANE, cut - LANE, LANE):
+            keep(pair, start, partial_ref[here, start : start + LANE])
     for pair in range(scans // 16):
         for block in (2 * pair, 2 * pair + 1):
             row_scan(rowscan_ref, volume, block, wide, rough)
+    for pair in range(scans // 16):
         here = slice(2 * pair * rows, 2 * (pair + 1) * rows)
         late = across(wide, here, slice(None), column_ref, slice(None))
         ends = late[:, LANE:]
-        for start in range(0, columns, LANE):
-            total = partial_ref[here, start : start + LANE]
-            if start == cut:
-                total = total + late[:, :LANE]
-            if start == 0:
-                total = total + jnp.where(left, ends, 0.0)
-            if start == cut - LANE:
-                total = total + jnp.where(left, 0.0, ends)
-            total = total.reshape(2, SLAB_ROWS, 8, LANE)
-            joined = jnp.concatenate([total[0], total[1]], 1)
-            held[:, 16 * pair : 16 * pair + 16, start : start + LANE] = joined.astype(BF16)
+        keep(pair, 0, partial_ref[here, :LANE] + jnp.where(left, ends, 0.0))
+        keep(pair, cut - LANE, partial_ref[here, cut - LANE : cut] + jnp.where(left, 0.0, ends))
+        keep(pair, cut, partial_ref[here, cut:] + late[:, :LANE])
         copy = pltpu.make_async_copy(
             held.at[:, 16 * pair : 16 * pair + 16, :], difference_ref.at[:, 16 * pair : 16 * pair + 16, :], sems.at[pair]
         )
@@ -417,7 +419,7 @@
             jax.ShapeDtypeStruct((16, planes * camera), F32),
             jax.ShapeDtypeStruct((pairs, 8, cut), F32),
         ]
-        + [jax.ShapeDtypeStruct((PLACED, cut), BF16)] * pairs,
+        + [jax.ShapeDtypeStruct((2 * PLACED + 8, cut), BF16)] * pairs,
         in_specs=[OUTSIDE] * 3,
         out_specs=[VECTOR] * (5 + pairs),
         scratch_shapes=[
@@ -439,6 +441,7 @@
             pltpu.SemaphoreType.DMA,
             pltpu.VMEM((pairs * LANE, planes * camera), BF16),
         ],
+        input_output_aliases={5 + step: 3 + step for step in range(pairs)},
         compiler_params=PARAMS,
         name="pack_other",
     )(other, other_shear, pick, own_strip, early, *own)

time: 29.5 us -> 29.4 us (level)
  no operation moved by 1% of the time
where the time goes in v10:
time: 29.4 us; the launch traced here: 29.2 us
  starting transfers between devices  13.5 us (46%)
  Pallas kernels  10.6 us (36%)
  waiting for transfers between devices  4.25 us (14%)
  between operations  0.71 us (2%)
    ppermute x6, starting transfers between devices, along(): lax.ppermute(chunks[step], 'slab', [(i, i ^ 2 * step) for i in range(slab...  9.62 us
    ppermute x6, waiting for transfers between devices, along(): lax.ppermute(chunks[step], 'slab', [(i, i ^ 2 * step) for i in range(slab...  3.53 us
    ppermute x2, starting transfers between devices, shifted(): lax.ppermute(block, 'tile', [(i, (i + distance) % count) for i in range(c...  2.92 us
    pallas_call x1, Pallas kernels, body(): pl.pallas_call(functools.partial(first_half, pairs, scans), out_shape=[ja...  2.74 us
    pallas_call x1, Pallas kernels, body(): pl.pallas_call(functools.partial(second_half, pairs, scans), out_shape=[j...  2.49 us
    pallas_call x1, Pallas kernels, body(): pl.pallas_call(stage, out_shape=[jax.ShapeDtypeStruct(table[name].shape,...  1.79 us
    pallas_call x1, Pallas kernels, body(): pl.pallas_call(pack_own, out_shape=[jax.ShapeDtypeStruct((planes * camera...  1.56 us
    pallas_call x1, Pallas kernels, body(): pl.pallas_call(pack_other, out_shape=[strip, strip, shift] + [jax.ShapeDt...  1.12 us
  transfers between devices with their start and end apart: 10, of which 4 were waited for; matrix products, arithmetic and copies ran while one was open for 0% of the time, Pallas kernels for 24%

profile of v10, /device:TPU:0, one launch (start us, length us, event | category | flops | bytes accessed | tf_op | source)
XLA Modules:
  0.0 29.2 jit_solution(13425025168677612668)
XLA Ops:
  0.6 0.5 %collective-permute-start = (bf16[480,512]{1,0:T(8,128)(2,1)}, bf16[480,512]{1,0:T(8,128)(2,1)S(1)}, u32[]{:S(2)}, u32[]{:S(2)}) collective-permute-start(bf16[480,512]{1,0:T(8,128)(2,1)} %bitcast.1), channel_id=1, source_target_pairs={{0,1},{1,0},{2,3},{3,2},{4,5},{5,4},{6,7},{7,6},{8,9},{9,8},{10,11... | collective-permute-start | bytes 1474568 | tf_op jit(solution)/shard_map/ppermute | solution.py:408
  1.2 0.1 copy-done
  1.3 0.5 %collective-permute-start.1 = (s32[4]{0:T(128)S(1)}, s32[4]{0:T(128)S(1)}, u32[]{:S(2)}, u32[]{:S(2)}) collective-permute-start(s32[4]{0:T(128)S(1)} %copy-done), channel_id=1, source_target_pairs={{0,1},{1,0},{2,3},{3,2},{4,5},{5,4},{6,7},{7,6},{8,9},{9,8},{10,11... | collective-permute-start | bytes 56 | tf_op jit(solution)/shard_map/ppermute | solution.py:409
  1.7 1.6 %pack_own.1 = (bf16[480,512]{1,0:T(8,128)(2,1)S(1)}, s32[128,128]{1,0:T(8,128)S(1)}, bf16[16,512]{1,0:T(8,128)(2,1)S(1)}, f32[16,480]{1,0:T(8,128)S(1)}, f32[4,8...) custom-call(bf16[480,512]{1,0:T(8,128)(2,1)} %bitcast.2, ...), custom_call_target="tpu_custom_call" | custom-call | tf_op jit(solution)/shard_map/pack_own/pallas_call | solution.py:413
  3.3 0.0 collective-permute-done.1.shear_ref
  3.3 0.0 collective-permute-done.other_ref
  3.3 1.1 %pack_other.1 = (bf16[16,480]{1,0:T(8,128)(2,1)S(1)}, bf16[16,480]{1,0:T(8,128)(2,1)S(1)}, s32[128,128]{1,0:T(8,128)S(1)}, bf16[200,384]{1,0:T(8,128)(2,1)S(1)},...) custom-call(bf16[480,512]{1,0:T(8,128)(2,1)S(1)} %collective-permute, ...), custom_call_target="tpu_custom_call", output_to_operand_aliasing={{3}: (5, {}), {4}: (6, {}), {5}: (7, {}), {6}: (8, {})} | custom-call | tf_op jit(solution)/shard_map/pack_other/pallas_call | solution.py:434
  4.5 3.7 %collective-permute-start.4 = (bf16[200,384]{1,0:T(8,128)(2,1)S(1)}, bf16[200,384]{1,0:T(8,128)(2,1)S(1)}, u32[]{:S(2)}, u32[]{:S(2)}) collective-permute-start(bf16[200,384]{1,0:T(8,128)(2,1)S(1)} %get-tuple-element.65), channel_id=1, source_target_pairs={{0,4},{1,5},{2,6},{3,7},{4,0},{5,1},{6,2},{7,3},{8,12},{9,13},{10,... | collective-permute-start | bytes 460808 | tf_op jit(solution)/shard_map/ppermute | solution.py:390
  8.1 1.6 %collective-permute-start.8 = (bf16[200,384]{1,0:T(8,128)(2,1)S(1)}, bf16[200,384]{1,0:T(8,128)(2,1)S(1)}, u32[]{:S(2)}, u32[]{:S(2)}) collective-permute-start(bf16[200,384]{1,0:T(8,128)(2,1)S(1)} %get-tuple-element.73), channel_id=1, source_target_pairs={{0,2},{1,3},{2,0},{3,1},{4,6},{5,7},{6,4},{7,5},{8,10},{9,11},{10,... | collective-permute-start | bytes 460808 | tf_op jit(solution)/shard_map/ppermute | solution.py:390
  9.7 0.0 collective-permute-start.9
  9.7 1.7 %collective-permute-start.2 = (bf16[16,480]{1,0:T(8,128)(2,1)S(1)}, bf16[16,480]{1,0:T(8,128)(2,1)S(1)}, u32[]{:S(2)}, u32[]{:S(2)}) collective-permute-start(bf16[16,480]{1,0:T(8,128)(2,1)S(1)} %get-tuple-element.60), channel_id=1, source_target_pairs={{0,8},{8,16},{16,24},{24,0},{1,9},{9,17},{17,25},{25,1},{2,10},{10... | collective-permute-start | bytes 46088 | tf_op jit(solution)/shard_map/ppermute | solution.py:396
  11.4 1.2 %collective-permute-start.3 = (bf16[16,480]{1,0:T(8,128)(2,1)S(1)}, bf16[16,480]{1,0:T(8,128)(2,1)S(1)}, u32[]{:S(2)}, u32[]{:S(2)}) collective-permute-start(bf16[16,480]{1,0:T(8,128)(2,1)S(1)} %get-tuple-element.50.order_ref), channel_id=1, source_target_pairs={{0,24},{8,0},{16,8},{24,16},{1,25},{9,1},{17,9},{25,17},{2,26},{10... | collective-permute-start | bytes 46088 | tf_op jit(solution)/shard_map/ppermute | solution.py:396
  12.6 1.8 %stage.1 = (bf16[560,512]{1,0:T(8,128)(2,1)S(1)}, bf16[128,192]{1,0:T(8,128)(2,1)S(1)}, bf16[4,512,256]{2,1,0:T(8,128)(2,1)S(1)}, bf16[4,256,256]{2,1,0:T(8,128)...) custom-call(bf16[16,480]{1,0:T(8,128)(2,1)S(1)} %get-tuple-element.5, ...), custom_call_target="tpu_custom_call" | custom-call | tf_op jit(solution)/shard_map/stage/pallas_call | solution.py:453
  14.4 0.0 collective-permute-done.2.from_left_ref
  14.4 0.7 %collective-permute-done.3.from_right_ref = bf16[16,480]{1,0:T(8,128)(2,1)S(1)} collective-permute-done((bf16[16,480]{1,0:T(8,128)(2,1)S(1)}, bf16[16,480]{1,0:T(8,128)(2,1)S(1)}, u32[]{:S(2)}, u32[]{:S(2)}) %collective-permute-start.3) | collective-permute-done | bytes 15392 | tf_op jit(solution)/shard_map/ppermute | solution.py:396
  15.1 0.8 %pack_second.1 = (bf16[224,128]{1,0:T(8,128)(2,1)S(1)}, bf16[224,128]{1,0:T(8,128)(2,1)S(1)}, bf16[224,128]{1,0:T(8,128)(2,1)S(1)}, bf16[224,128]{1,0:T(8,128)(2,1)S(1)}) custom-call(bf16[480,512]{1,0:T(8,128)(2,1)S(1)} %get-tuple-element.57.raw_ref, bf16[480,512]{1,0:T(8,128)(2,1)S(1)} %collective-permute-done.other_ref, ...), custom_call_target="tpu_custom_call" | custom-call | tf_op jit(solution)/shard_map/pack_second/pallas_call | solution.py:463
  16.0 0.3 %collective-permute-done.4.refs_2_ = bf16[200,384]{1,0:T(8,128)(2,1)S(1)} collective-permute-done((bf16[200,384]{1,0:T(8,128)(2,1)S(1)}, bf16[200,384]{1,0:T(8,128)(2,1)S(1)}, u32[]{:S(2)}, u32[]{:S(2)}) %collective-permute-start.4) | collective-permute-done | bytes 153632 | tf_op jit(solution)/shard_map/ppermute | solution.py:390
  16.3 0.7 %collective-permute-start.5 = (bf16[224,128]{1,0:T(8,128)(2,1)S(1)}, bf16[224,128]{1,0:T(8,128)(2,1)S(1)}, u32[]{:S(2)}, u32[]{:S(2)}) collective-permute-start(bf16[224,128]{1,0:T(8,128)(2,1)S(1)} %get-tuple-element.67), channel_id=1, source_target_pairs={{0,2},{1,3},{2,0},{3,1},{4,6},{5,7},{6,4},{7,5},{8,10},{9,11},{10,... | collective-permute-start | bytes 172040 | tf_op jit(solution)/shard_map/ppermute | solution.py:390
  17.0 3.6 %collective-permute-start.6 = (bf16[224,128]{1,0:T(8,128)(2,1)S(1)}, bf16[224,128]{1,0:T(8,128)(2,1)S(1)}, u32[]{:S(2)}, u32[]{:S(2)}) collective-permute-start(bf16[224,128]{1,0:T(8,128)(2,1)S(1)} %get-tuple-element.68), channel_id=1, source_target_pairs={{0,4},{1,5},{2,6},{3,7},{4,0},{5,1},{6,2},{7,3},{8,12},{9,13},{10,... | collective-permute-start | bytes 172040 | tf_op jit(solution)/shard_map/ppermute | solution.py:390
  20.6 0.1 collective-permute-start.7
  20.7 2.7 %first_half.1 = (f32[512,512]{1,0:T(8,128)S(1)}, f32[192,384]{1,0:T(8,128)S(1)}) custom-call(bf16[560,512]{1,0:T(8,128)(2,1)S(1)} %get-tuple-element.51.rowscan_ref, bf16[4,512,256]{2,1,0:T(8,128)(2,1)S(1)} %get-tuple-element.70.column_ref, bf16[384,384]{1,0:T(8,128)(2,1)S(1)} %get-tuple-element.71.level_column_ref, ...), custom_call_target="tpu_custom_call" | custom-call | tf_op jit(solution)/shard_map/first_half/pallas_call | solution.py:473
  23.4 2.5 %collective-permute-done.6.refs_4_ = bf16[224,128]{1,0:T(8,128)(2,1)S(1)} collective-permute-done((bf16[224,128]{1,0:T(8,128)(2,1)S(1)}, bf16[224,128]{1,0:T(8,128)(2,1)S(1)}, u32[]{:S(2)}, u32[]{:S(2)}) %collective-permute-start.6) | collective-permute-done | bytes 57376 | tf_op jit(solution)/shard_map/ppermute | solution.py:390
  25.9 0.7 %collective-permute-done.7.refs_5_ = bf16[224,128]{1,0:T(8,128)(2,1)S(1)} collective-permute-done((bf16[224,128]{1,0:T(8,128)(2,1)S(1)}, bf16[224,128]{1,0:T(8,128)(2,1)S(1)}, u32[]{:S(2)}, u32[]{:S(2)}) %collective-permute-start.7) | collective-permute-done | bytes 57376 | tf_op jit(solution)/shard_map/ppermute | solution.py:390
  26.7 2.5 %second_half.1 = (bf16[16,32,512]{2,1,0:T(8,128)(2,1)}, bf16[8,16,256]{2,1,0:T(8,128)(2,1)}, bf16[4,8,128]{2,1,0:T(8,128)(2,1)}) custom-call(bf16[560,512]{1,0:T(8,128)(2,1)S(1)} %get-tuple-element.51.rowscan_ref, bf16[128,192]{1,0:T(8,128)(2,1)S(1)} %get-tuple-element.52.order_ref, bf16[4,256,256]{2,1,0:T(8,128)(2,1)S(1)} %get-tuple-element.53.column_ref, ...), custom_call_target="tpu_custom_call" | custom-call | tf_op jit(solution)/shard_map/second_half/pallas_call | solution.py:490
  (4 shorter events, 0.0 us)
Async XLA Ops:
  0.6 0.7 %copy-start = (s32[4]{0:T(128)S(1)}, s32[4]{0:T(128)}, u32[]{:S(2)}) copy-start(s32[4]{0:T(128)} %shear_ref.1) | copy-start | bytes 52
  0.6 2.7 %collective-permute-start = (bf16[480,512]{1,0:T(8,128)(2,1)}, bf16[480,512]{1,0:T(8,128)(2,1)S(1)}, u32[]{:S(2)}, u32[]{:S(2)}) collective-permute-start(bf16[480,512]{1,0:T(8,128)(2,1)} %bitcast.1), channel_id=1, source_target_pairs={{0,1},{1,0},{2,3},{3,2},{4,5},{5,4},{6,7},{7,6},{8,9},{9,8},{10,11... | collective-permute-start | bytes 1474568 | tf_op jit(solution)/shard_map/ppermute | solution.py:408
  1.3 2.0 %collective-permute-start.1 = (s32[4]{0:T(128)S(1)}, s32[4]{0:T(128)S(1)}, u32[]{:S(2)}, u32[]{:S(2)}) collective-permute-start(s32[4]{0:T(128)S(1)} %copy-done), channel_id=1, source_target_pairs={{0,1},{1,0},{2,3},{3,2},{4,5},{5,4},{6,7},{7,6},{8,9},{9,8},{10,11... | collective-permute-start | bytes 56 | tf_op jit(solution)/shard_map/ppermute | solution.py:409
  4.5 11.8 %collective-permute-start.4 = (bf16[200,384]{1,0:T(8,128)(2,1)S(1)}, bf16[200,384]{1,0:T(8,128)(2,1)S(1)}, u32[]{:S(2)}, u32[]{:S(2)}) collective-permute-start(bf16[200,384]{1,0:T(8,128)(2,1)S(1)} %get-tuple-element.65), channel_id=1, source_target_pairs={{0,4},{1,5},{2,6},{3,7},{4,0},{5,1},{6,2},{7,3},{8,12},{9,13},{10,... | collective-permute-start | bytes 460808 | tf_op jit(solution)/shard_map/ppermute | solution.py:390
  8.1 12.6 %collective-permute-start.8 = (bf16[200,384]{1,0:T(8,128)(2,1)S(1)}, bf16[200,384]{1,0:T(8,128)(2,1)S(1)}, u32[]{:S(2)}, u32[]{:S(2)}) collective-permute-start(bf16[200,384]{1,0:T(8,128)(2,1)S(1)} %get-tuple-element.73), channel_id=1, source_target_pairs={{0,2},{1,3},{2,0},{3,1},{4,6},{5,7},{6,4},{7,5},{8,10},{9,11},{10,... | collective-permute-start | bytes 460808 | tf_op jit(solution)/shard_map/ppermute | solution.py:390
  9.7 11.0 %collective-permute-start.9 = (bf16[200,384]{1,0:T(8,128)(2,1)S(1)}, bf16[200,384]{1,0:T(8,128)(2,1)S(1)}, u32[]{:S(2)}, u32[]{:S(2)}) collective-permute-start(bf16[200,384]{1,0:T(8,128)(2,1)S(1)} %get-tuple-element.75), channel_id=1, source_target_pairs={{0,6},{1,7},{2,4},{3,5},{4,2},{5,3},{6,0},{7,1},{8,14},{9,15},{10,... | collective-permute-start | bytes 460808 | tf_op jit(solution)/shard_map/ppermute | solution.py:390
  9.7 4.7 %collective-permute-start.2 = (bf16[16,480]{1,0:T(8,128)(2,1)S(1)}, bf16[16,480]{1,0:T(8,128)(2,1)S(1)}, u32[]{:S(2)}, u32[]{:S(2)}) collective-permute-start(bf16[16,480]{1,0:T(8,128)(2,1)S(1)} %get-tuple-element.60), channel_id=1, source_target_pairs={{0,8},{8,16},{16,24},{24,0},{1,9},{9,17},{17,25},{25,1},{2,10},{10... | collective-permute-start | bytes 46088 | tf_op jit(solution)/shard_map/ppermute | solution.py:396
  11.4 3.7 %collective-permute-start.3 = (bf16[16,480]{1,0:T(8,128)(2,1)S(1)}, bf16[16,480]{1,0:T(8,128)(2,1)S(1)}, u32[]{:S(2)}, u32[]{:S(2)}) collective-permute-start(bf16[16,480]{1,0:T(8,128)(2,1)S(1)} %get-tuple-element.50.order_ref), channel_id=1, source_target_pairs={{0,24},{8,0},{16,8},{24,16},{1,25},{9,1},{17,9},{25,17},{2,26},{10... | collective-permute-start | bytes 46088 | tf_op jit(solution)/shard_map/ppermute | solution.py:396
  16.3 7.1 %collective-permute-start.5 = (bf16[224,128]{1,0:T(8,128)(2,1)S(1)}, bf16[224,128]{1,0:T(8,128)(2,1)S(1)}, u32[]{:S(2)}, u32[]{:S(2)}) collective-permute-start(bf16[224,128]{1,0:T(8,128)(2,1)S(1)} %get-tuple-element.67), channel_id=1, source_target_pairs={{0,2},{1,3},{2,0},{3,1},{4,6},{5,7},{6,4},{7,5},{8,10},{9,11},{10,... | collective-permute-start | bytes 172040 | tf_op jit(solution)/shard_map/ppermute | solution.py:390
  17.0 9.0 %collective-permute-start.6 = (bf16[224,128]{1,0:T(8,128)(2,1)S(1)}, bf16[224,128]{1,0:T(8,128)(2,1)S(1)}, u32[]{:S(2)}, u32[]{:S(2)}) collective-permute-start(bf16[224,128]{1,0:T(8,128)(2,1)S(1)} %get-tuple-element.68), channel_id=1, source_target_pairs={{0,4},{1,5},{2,6},{3,7},{4,0},{5,1},{6,2},{7,3},{8,12},{9,13},{10,... | collective-permute-start | bytes 172040 | tf_op jit(solution)/shard_map/ppermute | solution.py:390
  20.6 6.1 %collective-permute-start.7 = (bf16[224,128]{1,0:T(8,128)(2,1)S(1)}, bf16[224,128]{1,0:T(8,128)(2,1)S(1)}, u32[]{:S(2)}, u32[]{:S(2)}) collective-permute-start(bf16[224,128]{1,0:T(8,128)(2,1)S(1)} %get-tuple-element.69), channel_id=1, source_target_pairs={{0,6},{1,7},{2,4},{3,5},{4,2},{5,3},{6,0},{7,1},{8,14},{9,15},{10,... | collective-permute-start | bytes 172040 | tf_op jit(solution)/shard_map/ppermute | solution.py:390
